TPU v7x, 256 devices: a whole 4x4x8 slice. The times are simulated.
256 devices in a mesh: shift: 8 (over y_lo, x), sub: 32 (over y_hi, z, core).
Axes of the slice: x: 4, y: 4 (y_hi: 2, y_lo: 2; y = y_hi * 2 + y_lo), z: 8, core: 2. Of those that a mesh axis runs over, the one named last changes fastest.
Arguments:
- interior_rhs: bfloat16 [32, 1024, 384], P('sub'), may hold values from -6 to 6
- interface_rhs: bfloat16 [2048, 384], replicated, may hold values from -6 to 6
- interior_inverse: bfloat16 [16, 32, 1024, 1024], P('shift', 'sub'), may hold values from -0.1875 to 0.1875
- coupling: bfloat16 [32, 1024, 256], P('sub'), may hold values from -0.1875 to 0.1875
- schur_inverse: bfloat16 [16, 2048, 2048], P('shift', 'sub'), may hold values from -0.125 to 0.125
- weights: float32 [16], P('shift'), may hold values from -1 to 1
- owner_sub: int32 [32], replicated, may hold values from 0 to 31, each once
- index_blocks: int32 [32, 256], replicated, may hold values from 0 to 2047, as said below
Outputs:
- filtered: float32 [1024, 32, 384], P('shift', 'sub')
Inputs may be any that keep to these rules, and one draw needn't show every extreme that they name: `index_blocks`: each row holds 256 distinct interface unknowns; of each aligned block of 2048 // 32 interface unknowns a row holds at most 16, and exactly 16 of some block. `owner_sub`: each position names a different substructure.
All inputs are finite; a program needn't handle non-finite values.
Results may differ from a plain program's by a relative error of at most 0.0053.
Values may be sent and summed in bfloat16 or wider, within the bound.
No kernel may reach another device: no remote copies, remote signals or barrier semaphores. Data moves between devices by JAX's collectives and lax.ppermute only.
A program may use at most 64 MiB of HBM per device.

v0:
```python
import jax
import jax.numpy as jnp
from jax import lax
from jax.sharding import PartitionSpec as P


def on_device(
    interior_rhs,
    interface_rhs,
    interior_inverse,
    coupling,
    schur_inverse,
    weights,
    owner_sub,
    index_blocks,
):
    position = lax.axis_index("sub")
    substructure = lax.dynamic_index_in_dim(owner_sub, position, 0, keepdims=False)
    idx = lax.dynamic_index_in_dim(index_blocks, substructure, 0, keepdims=False)
    rhs_local = interior_rhs[0]
    couple_local = coupling[0]
    accumulated = jnp.zeros(rhs_local.shape, jnp.float32)
    for which in range(interior_inverse.shape[0]):
        inverse = interior_inverse[which, 0]
        schur_local = schur_inverse[which]
        eliminated = jnp.dot(inverse, rhs_local, preferred_element_type=jnp.float32).astype(
            jnp.bfloat16
        )
        coupled = lax.dot_general(
            couple_local, eliminated, (((0,), (0,)), ((), ())), preferred_element_type=jnp.float32
        ).astype(jnp.bfloat16)
        targets = lax.iota(jnp.int32, interface_rhs.shape[0])
        selector = (idx[None, :] == targets[:, None]).astype(jnp.bfloat16)
        summed_all = lax.psum(jnp.dot(selector, coupled, preferred_element_type=jnp.float32), "sub")
        reduced_all = (interface_rhs.astype(jnp.float32) - summed_all).astype(jnp.bfloat16)
        solved = jnp.dot(schur_local, reduced_all, preferred_element_type=jnp.float32)
        interface_sol = solved.astype(jnp.bfloat16)
        piece = lax.all_gather(interface_sol, "sub", axis=0, tiled=True)
        sources = lax.iota(jnp.int32, piece.shape[0])
        pick_selector = (idx[:, None] == sources[None, :]).astype(jnp.bfloat16)
        picked = jnp.dot(pick_selector, piece, preferred_element_type=jnp.float32)
        correction = jnp.dot(
            couple_local, picked.astype(jnp.bfloat16), preferred_element_type=jnp.float32
        ).astype(jnp.bfloat16)
        interior_sol = eliminated.astype(jnp.float32) - jnp.dot(
            inverse, correction, preferred_element_type=jnp.float32
        )
        accumulated = accumulated + weights[which] * interior_sol
    share_rows = accumulated.shape[0] // lax.axis_size("shift")
    whole_sum = lax.psum(accumulated, "shift")
    own_rows = lax.dynamic_slice_in_dim(
        whole_sum, lax.axis_index("shift") * share_rows, share_rows, 0
    )
    return own_rows[:, None, :]


def solution(mesh):
    in_specs = (
        P("sub", None, None),
        P(),
        P("shift", "sub", None, None),
        P("sub", None, None),
        P("shift", "sub", None),
        P("shift"),
        P(),
        P(),
    )
    out_specs = P("shift", "sub", None)
    return jax.shard_map(
        on_device, mesh=mesh, in_specs=in_specs, out_specs=out_specs, check_vma=False
    )
```

profile of v0, /device:TPU:32, one launch (start us, length us, event | category | flops | bytes accessed | tf_op | source)
XLA Modules:
  0.0 565.3 jit_solution(16608008642296047814)
XLA Ops:
  6.5 0.0 copy-start
  6.5 0.0 all-reduce.6.cloned.1.call-start
  6.5 1.3 dynamic_slice.11
  9.1 0.0 copy-done
  9.2 0.0 copy-start.9
  9.2 3.0 fusion.27
  12.2 0.0 copy-done.9
  12.2 0.0 copy-start.3
  12.2 0.0 copy-start.2
  12.2 1.3 fusion.30
  13.5 0.0 copy-start.5
  14.1 0.7 constant_dynamic-slice_fusion.1
  14.8 0.0 copy-done.3
  14.8 0.0 copy-done.2
  14.8 3.1 fusion.11
  17.9 0.0 copy-done.5
  17.9 3.1 fusion.10
  21.0 0.0 copy-start.1
  21.0 0.0 copy-start.7
  21.0 0.0 all-reduce.6.cloned.1.call-update
  21.0 0.0 all-gather.5.cloned.1.call-start
  21.1 283.2 %all-reduce.6.cloned.1.call-done = (f32[2048,384]{1,0:T(8,128)}, f32[2048,384]{1,0:T(8,128)}) async-done(((f32[2048,384]{1,0:T(8,128)}, f32[2048,384]{1,0:T(8,128)}), (f32[2048,384]{1,0:T(8,128)}, f32[2048,384]{1,0:T(8,128)})) %all-reduce.6.cloned.1.call-update) | async-done | bytes 6291472 | tf_op jit(solution)/shard_map/psum | solution.py:34
  304.3 0.0 copy-done.1
  304.3 0.0 copy-done.7
  304.3 3.0 fusion.41
  307.3 0.0 all-gather.5.cloned.1.call-update
  307.4 0.0 all-gather.3.cloned.1.call-start
  307.4 0.0 copy-start.8
  307.4 3.0 fusion.44
  310.4 0.0 all-gather.3.cloned.1.call-update
  310.5 0.0 all-reduce.4.cloned.1.call-start
  310.5 0.0 copy-done.8
  310.5 0.6 fusion.65
  311.1 78.0 %all-gather.5.cloned.1.call-done = bf16[2048,384]{1,0:T(8,128)(2,1)} async-done(((bf16[64,384]{1,0:T(8,128)(2,1)}), bf16[2048,384]{1,0:T(8,128)(2,1)}) %all-gather.5.cloned.1.call-update) | async-done | bytes 1572880 | tf_op jit(solution)/shard_map/all_gather | solution.py:38
  389.1 2.2 fusion.34
  391.3 4.2 fusion.2
  395.5 0.0 copy-start.4
  395.5 0.0 copy-start.6
  395.5 71.4 %all-gather.3.cloned.1.call-done = bf16[2048,384]{1,0:T(8,128)(2,1)} async-done(((bf16[64,384]{1,0:T(8,128)(2,1)}), bf16[2048,384]{1,0:T(8,128)(2,1)}) %all-gather.3.cloned.1.call-update) | async-done | bytes 1572880 | tf_op jit(solution)/shard_map/all_gather | solution.py:38
  466.9 2.2 fusion.33
  469.1 0.0 copy-done.4
  469.1 0.0 copy-done.6
  469.1 6.1 %fusion.23 = f32[1024,384]{1,0:T(8,128)} fusion(f32[384,1024]{0,1:T(8,128)} %fusion.2, bf16[1024,384]{1,0:T(8,128)(2,1)S(1)} %copy-done.6, bf16[1024,384]{1,0:T(8,128)(2,1)S(1)} %copy-done.4, bf16[2,1,1024,1024]{3,2,1,0:T(8,128)(2,1)} %param.10, bf16[256,384]{1,0:T(8,128)(2,1)S(1)} %fusion.33, f32[]{:T(128)} %bitcast.9, f32[]{:T(128)} %bitcast, ...), kind=kOutput, calls=%fused_computation.26 | convolution fusion | flops 1009778688 | bytes 7537664 | tf_op jit(solution)/shard_map/dot_general | solution.py:45
  475.2 0.0 all-reduce.4.cloned.1.call-update
  475.2 81.8 %all-reduce.4.cloned.1.call-done = f32[1024,384]{1,0:T(8,128)} async-done(((f32[1024,384]{1,0:T(8,128)}), f32[1024,384]{1,0:T(8,128)}) %all-reduce.4.cloned.1.call-update) | async-done | bytes 1572880 | tf_op jit(solution)/shard_map/psum | solution.py:50
  557.0 0.9 constant_dynamic-slice_fusion
  557.9 0.8 broadcast_in_dim.2
Async XLA Ops:
  6.5 2.6 copy-start
  6.5 297.8 %all-reduce.6.cloned.1.call-start = ((), (), s32[]{:S(2)}) async-start(), calls=%async_computation.3 | async-start | bytes 12582912 | tf_op jit(solution)/shard_map/psum | solution.py:34
  9.2 3.0 copy-start.9
  12.2 2.6 copy-start.3
  12.2 2.6 copy-start.2
  13.5 4.4 copy-start.5
  21.0 283.3 %copy-start.1 = (bf16[2048,384]{1,0:T(8,128)(2,1)S(1)}, bf16[2048,384]{1,0:T(8,128)(2,1)}, u32[]{:S(2)}) copy-start(bf16[2048,384]{1,0:T(8,128)(2,1)} %param.9) | copy-start | bytes 4718596
  21.0 283.3 %copy-start.7 = (bf16[2,64,2048]{2,1,0:T(8,128)(2,1)S(1)}, bf16[2,64,2048]{2,1,0:T(8,128)(2,1)}, u32[]{:S(2)}) copy-start(bf16[2,64,2048]{2,1,0:T(8,128)(2,1)} %param.12) | copy-start | bytes 1572868
  21.0 368.1 %all-gather.5.cloned.1.call-start = ((), (), s32[]{:S(2)}) async-start(), calls=%async_computation.1 | async-start | bytes 1622016 | tf_op jit(solution)/shard_map/all_gather | solution.py:38
  307.4 159.6 %all-gather.3.cloned.1.call-start = ((), (), s32[]{:S(2)}) async-start(), calls=%async_computation | async-start | bytes 1622016 | tf_op jit(solution)/shard_map/all_gather | solution.py:38
  307.4 3.1 copy-start.8
  310.5 246.6 %all-reduce.4.cloned.1.call-start = ((), (), s32[]{:S(2)}) async-start(), calls=%async_computation.2 | async-start | bytes 3145728 | tf_op jit(solution)/shard_map/psum | solution.py:50
  395.5 73.6 %copy-start.4 = (bf16[1024,384]{1,0:T(8,128)(2,1)S(1)}, bf16[1024,384]{1,0:T(8,128)(2,1)}, u32[]{:S(2)}) copy-start(bf16[1024,384]{1,0:T(8,128)(2,1)} %copy-done.3) | copy-start | bytes 2359300
  395.5 73.6 %copy-start.6 = (bf16[1024,384]{1,0:T(8,128)(2,1)S(1)}, bf16[1024,384]{1,0:T(8,128)(2,1)}, u32[]{:S(2)}) copy-start(bf16[1024,384]{1,0:T(8,128)(2,1)} %copy-done.5) | copy-start | bytes 2359300
Sparse Core Ops, SparseCore 0:
  21.1 283.1 all-reduce.5
  307.5 81.5 all-gather.4
  391.9 75.0 all-gather.2
  475.3 81.6 all-reduce.3
where the time goes:
time: 566 us; the launch traced here: 565 us
  waiting for transfers between devices  515 us (91%)
  matrix products  31 us (5%)
  between operations  15.2 us (3%)
    psum x1, waiting for transfers between devices, on_device(): lax.psum(jnp.dot(selector, coupled, preferred_element_type=jnp.float32),...  283 us
    all_gather x2, waiting for transfers between devices, on_device(): piece = lax.all_gather(interface_sol, 'sub', axis=0, tiled=True)  149 us
    psum x1, waiting for transfers between devices, on_device(): whole_sum = lax.psum(accumulated, 'shift')  81.8 us
  transfers between devices with their start and end apart: 4, of which 4 were waited for; matrix products, arithmetic and copies ran while one was open for 2% of the time, Pallas kernels for 0%

commit v1 on v0

v1 whole, which is shorter than its diff:
```python
import jax
import jax.numpy as jnp
from jax import lax
from jax.sharding import Mesh, PartitionSpec as P

BF = jnp.bfloat16
F32 = jnp.float32
SUB = ("yh", "z", "c")
CHIPS = ("yh", "z")
SHIFT = ("yl", "x")


def dot(a, b):
    return jnp.dot(a, b, preferred_element_type=F32)


def on_device(
    interior_rhs,
    interface_rhs,
    interior_inverse,
    coupling,
    schur_inverse,
    weights,
    owner_sub,
    index_blocks,
):
    core = lax.axis_index("c")
    chip = lax.axis_index(CHIPS)
    first = core == 0
    swap = [(0, 1), (1, 0)]
    rhs = interior_rhs[0]
    couple = coupling[0]

    schur_keep = jnp.where(first, schur_inverse[0], schur_inverse[1])
    schur_give = jnp.where(first, schur_inverse[1], schur_inverse[0])
    schur_got = lax.ppermute(schur_give, "c", swap)
    schur = jnp.concatenate(
        [jnp.where(first, schur_keep, schur_got), jnp.where(first, schur_got, schur_keep)], axis=0
    )

    names = lax.broadcasted_iota(jnp.int32, (32, 32, 1), 1)
    idx_all = jnp.sum(
        jnp.where(owner_sub[:, None, None] == names, index_blocks[None], 0), axis=1
    )

    def packer(position):
        idx = lax.dynamic_index_in_dim(idx_all, position, 0, keepdims=False)
        mine, other = idx[:, None], idx[None, :]
        rank = jnp.sum(((mine // 64 == other // 64) & (other < mine)).astype(jnp.int32), axis=1)
        slot = (idx // 64) * 16 + rank
        return (lax.broadcasted_iota(jnp.int32, (512, 256), 0) == slot[None, :]).astype(BF)

    pack = [packer(2 * chip), packer(2 * chip + 1)]

    rows = lax.broadcasted_iota(jnp.int32, (1, 1, 128), 2) + 128 * chip
    held = jnp.any(idx_all[:, :, None] == rows, axis=1)
    low = lax.broadcasted_iota(jnp.int32, (128, 128), 0)
    high = lax.broadcasted_iota(jnp.int32, (128, 128), 1)
    before = ((low < high) & (low // 64 == high // 64)).astype(BF)
    place = dot(held.astype(BF), before).astype(jnp.int32)
    place = place + 16 * (lax.broadcasted_iota(jnp.int32, (32, 128), 1) // 64)
    place = jnp.where(held, place, -1)
    select = (
        (place[:, None, :] == lax.broadcasted_iota(jnp.int32, (32, 32, 128), 1))
        .astype(BF)
        .reshape(1024, 128)
    )

    eliminated = [dot(interior_inverse[j, 0], rhs).astype(BF) for j in range(2)]
    coupled = [
        lax.dot_general(couple, e, (((0,), (0,)), ((), ())), preferred_element_type=F32).astype(BF)
        for e in eliminated
    ]
    keep = jnp.where(first, coupled[0], coupled[1])
    give = jnp.where(first, coupled[1], coupled[0])
    got = lax.ppermute(give, "c", swap)
    of_chip = [jnp.where(first, keep, got), jnp.where(first, got, keep)]
    packed = jnp.concatenate(
        [dot(pack[i], of_chip[i]).astype(BF).reshape(16, 32, 384) for i in range(2)], axis=1
    )
    arrived = lax.all_to_all(packed, CHIPS, 0, 0, tiled=True).reshape(1024, 384)
    summed = lax.dot_general(
        select, arrived, (((0,), (0,)), ((), ())), preferred_element_type=F32
    )
    own_rows = lax.dynamic_slice_in_dim(interface_rhs, 128 * chip, 128, 0)
    reduced = (own_rows.astype(F32) - summed).astype(BF)
    everywhere = lax.all_to_all(
        jnp.broadcast_to(reduced[None], (16, 128, 384)), CHIPS, 0, 0, tiled=True
    ).reshape(2048, 384)
    solved = dot(schur, everywhere).astype(BF)
    answers = dot(select, solved).astype(BF).reshape(16, 64, 384)
    back = lax.all_to_all(answers, CHIPS, 0, 0, tiled=True).reshape(16, 2, 32, 384)
    picked = [
        lax.dot_general(
            pack[i],
            back[:, i].reshape(512, 384),
            (((0,), (0,)), ((), ())),
            preferred_element_type=F32,
        ).astype(BF)
        for i in range(2)
    ]
    keep = jnp.where(first, picked[0], picked[1])
    give = jnp.where(first, picked[1], picked[0])
    got = lax.ppermute(give, "c", swap)
    by_shift = [jnp.where(first, keep, got), jnp.where(first, got, keep)]

    spread = [dot(interior_inverse[j, 0], couple).astype(BF) for j in range(2)]
    total = jnp.zeros((1024, 384), F32)
    for j in range(2):
        interior_sol = eliminated[j].astype(F32) - dot(spread[j], by_shift[j])
        total = total + weights[j] * interior_sol
    pieces = lax.all_to_all(total.astype(BF).reshape(8, 128, 384), SHIFT, 0, 0, tiled=True)
    return jnp.sum(pieces.astype(F32), axis=0)[:, None, :]


def solution(mesh):
    fine = Mesh(mesh.devices.reshape(2, 4, 2, 8, 2), ("yl", "x", "yh", "z", "c"))
    in_specs = (
        P(SUB, None, None),
        P(),
        P(SHIFT, SUB, None, None),
        P(SUB, None, None),
        P(SHIFT, SUB, None),
        P(SHIFT),
        P(),
        P(),
    )
    out_specs = P(SHIFT, SUB, None)
    return jax.shard_map(
        on_device, mesh=fine, in_specs=in_specs, out_specs=out_specs, check_vma=False
    )
```

time: 566 us -> 151 us (0.27)
  waiting for transfers between devices: 515 us -> 58.2 us
  blocking collectives: 0 us -> 46 us
  starting transfers between devices: 0.13 us -> 17.3 us
  between operations: 15.2 us -> 0.35 us
  matrix products: 31 us -> 18.7 us
    psum x2 -> x0, waiting for transfers between devices: 365 us -> none  [the longest x1 283 us: on_device(): lax.psum(jnp.dot(selector, coupled, preferred_element_type=jnp.float32),...]
    all_gather x2 -> x0, waiting for transfers between devices: 149 us -> none  [on_device(): piece = lax.all_gather(interface_sol, 'sub', axis=0, tiled=True)]
    all_to_all x0 -> x2, waiting for transfers between devices: none -> 56.9 us  [the longest x1 36.7 us: on_device(): lax.all_to_all(jnp.broadcast_to(reduced[None], (16, 128, 384)), CHIPS, 0,...]
    all_to_all x0 -> x2, blocking collectives: none -> 46 us  [the longest x1 28.6 us: on_device(): lax.all_to_all(answers, CHIPS, 0, 0, tiled=True).reshape(16, 2, 32, 384)]
    all_to_all x0 -> x2, starting transfers between devices: none -> 17 us  [the longest x1 11.2 us: on_device(): arrived = lax.all_to_all(packed, CHIPS, 0, 0, tiled=True).reshape(1024, 384)]
    dot_general x10 -> x13, matrix products: 31 us -> 18.7 us  [the longest x8 16 us: dot(): return jnp.dot(a, b, preferred_element_type=F32)]
  transfers between devices with their start and end apart: 4 -> 5, of which waited for: 4 -> 4; matrix products, arithmetic and copies ran while one was open for 2% -> 4% of each run, Pallas kernels for 0% -> 0%
where the time goes in v1:
time: 151 us
  waiting for transfers between devices  58.2 us (39%)
  blocking collectives  46 us (30%)
  matrix products  18.7 us (12%)
  starting transfers between devices  17.3 us (11%)
  other arithmetic  5.13 us (3%)
  local copies, waits for them, and re-layouts  4.9 us (3%)
    all_to_all x1, waiting for transfers between devices, on_device(): lax.all_to_all(jnp.broadcast_to(reduced[None], (16, 128, 384)), CHIPS, 0,...  36.7 us
    all_to_all x1, blocking collectives, on_device(): lax.all_to_all(answers, CHIPS, 0, 0, tiled=True).reshape(16, 2, 32, 384)  28.6 us
    all_to_all x1, waiting for transfers between devices, on_device(): arrived = lax.all_to_all(packed, CHIPS, 0, 0, tiled=True).reshape(1024, 384)  20.3 us
    all_to_all x1, blocking collectives, on_device(): lax.all_to_all(total.astype(BF).reshape(8, 128, 384), SHIFT, 0, 0, tiled=...  17.4 us
    dot_general x8, matrix products, dot(): return jnp.dot(a, b, preferred_element_type=F32)  16 us
    all_to_all x1, starting transfers between devices, on_device(): arrived = lax.all_to_all(packed, CHIPS, 0, 0, tiled=True).reshape(1024, 384)  11.2 us
    all_to_all x1, starting transfers between devices, on_device(): lax.all_to_all(jnp.broadcast_to(reduced[None], (16, 128, 384)), CHIPS, 0,...  5.79 us
  transfers between devices with their start and end apart: 5, of which 4 were waited for; matrix products, arithmetic and copies ran while one was open for 4% of the time, Pallas kernels for 0%

profile of v1, /device:TPU:32, one launch (start us, length us, event | category | flops | bytes accessed | tf_op | source)
XLA Modules:
  0.0 150.6 jit_solution(1984747340637474498)
XLA Ops:
  0.0 1.1 copy-done
  1.1 3.0 %fusion.15 = bf16[1024,384]{1,0:T(8,128)(2,1)S(1)} fusion(bf16[2,1,1024,1024]{3,2,1,0:T(8,128)(2,1)} %param.10, bf16[1,1024,384]{2,1,0:T(8,128)(2,1)S(1)} %copy-done), kind=kOutput, calls=%fused_computation.17 | convolution fusion | flops 805699584 | bytes 3670016 | tf_op jit(solution)/shard_map/dot_general | solution.py:14
  4.1 0.0 copy-start.10
  4.2 1.3 fusion.12
  5.4 0.0 copy-done.10
  5.5 0.4 convolution_convert_fusion.5
  5.9 0.0 copy-start.8
  5.9 0.0 copy-start.2
  5.9 0.4 convolution_convert_fusion.6
  6.3 0.0 copy-done.14
  6.4 0.1 collective-permute-start.1
  6.5 0.1 copy-done.8
  6.6 0.1 iota_compare_fusion.9
  6.6 0.0 copy-done.2
  6.7 0.3 select_reduce_fusion
  7.0 0.2 convert_reduce_fusion.2
  7.2 0.2 convert_reduce_fusion.1
  7.4 0.5 collective-permute-done.1
  7.9 0.3 convolution_convert_fusion.2
  8.3 0.4 convolution_convert_fusion.1
  8.6 1.0 pad_maximum_fusion
  9.7 11.2 %all-to-all-start = ((bf16[16,64,384]{2,1,0:T(8,128)(2,1)}), bf16[16,64,384]{2,1,0:T(8,128)(2,1)S(1)}, u32[]{:S(2)}, u32[]{:S(2)}) async-start(bf16[16,64,384]{2,1,0:T(8,128)(2,1)} %pad_maximum_fusion), calls=%async_computation | async-start | bytes 1572864 | tf_op jit(solution)/shard_map/all_to_all | solution.py:81
  20.9 1.4 compare_reduce_fusion
  22.3 0.2 fusion.29
  22.6 0.1 iota_compare_fusion.3
  22.6 20.3 %all-to-all-done = bf16[16,64,384]{2,1,0:T(8,128)(2,1)S(1)} async-done(((bf16[16,64,384]{2,1,0:T(8,128)(2,1)}), bf16[16,64,384]{2,1,0:T(8,128)(2,1)S(1)}, u32[]{:S(2)}, u32[]{:S(2)}) %all-to-all-start) | async-done | bytes 786464 | tf_op jit(solution)/shard_map/all_to_all | solution.py:81
  42.9 1.2 fusion.27
  44.1 1.4 broadcast_in_dim.53
  45.5 5.8 %all-to-all-start.1 = ((bf16[16,128,384]{2,1,0:T(8,128)(2,1)}), bf16[16,128,384]{2,1,0:T(8,128)(2,1)S(1)}, u32[]{:S(2)}, u32[]{:S(2)}) async-start(bf16[16,128,384]{2,1,0:T(8,128)(2,1)} %broadcast_in_dim.53), calls=%async_computation.1 | async-start | bytes 3145728 | tf_op jit(solution)/shard_map/all_to_all | solution.py:87
  51.4 0.1 collective-permute-start
  51.5 0.7 iota.94
  52.1 0.9 bitcast_compare_fusion
  53.0 0.0 collective-permute-done
  53.0 0.7 bitcast_select_fusion.1
  53.8 36.7 %all-to-all-done.1 = bf16[16,128,384]{2,1,0:T(8,128)(2,1)S(1)} async-done(((bf16[16,128,384]{2,1,0:T(8,128)(2,1)}), bf16[16,128,384]{2,1,0:T(8,128)(2,1)S(1)}, u32[]{:S(2)}, u32[]{:S(2)}) %all-to-all-start.1) | async-done | bytes 1572896 | tf_op jit(solution)/shard_map/all_to_all | solution.py:87
  90.5 1.7 %convolution_convert_fusion = bf16[1024,384]{1,0:T(8,128)(2,1)S(1)} fusion(pred[1024,128]{1,0:T(32,128)(4,1)S(1)} %bitcast_compare_fusion, bf16[2048,384]{1,0:T(8,128)(2,1)S(1)} %bitcast.81, bf16[64,2048]{1,0:T(8,128)(2,1)} %get-tuple-element.12, bf16[64,2048]{1,0:T(8,128)(2,1)S(1)} %get-tuple-element.11), kind=kOutput, calls=%fused_computation.15 | convolution fusion | flops 303480832 | bytes 3014656 | tf_op jit(solution)/shard_map/dot_general | solution.py:14
  92.2 28.6 %all_to_all.20 = bf16[16,64,384]{2,1,0:T(8,128)(2,1)S(1)} all-to-all(bf16[16,64,384]{2,1,0:T(8,128)(2,1)S(1)} %bitcast.84), channel_id=1, replica_groups=mesh['yl'=2,'x'=4,'yh'=2,'z'=8,'c'=2] {'yh','z'}, dimensions={0} | all-to-all | bytes 1572864 | tf_op jit(solution)/shard_map/all_to_all | solution.py:92
  120.8 0.1 fusion.66
  120.9 0.3 convolution_convert_fusion.4
  121.3 0.3 broadcast_select_fusion.2
  121.6 0.1 collective-permute-start.2
  121.7 0.6 fusion.67
  122.4 0.8 collective-permute-done.2
  123.2 4.2 %fusion.25 = f32[1024,384]{1,0:T(8,128)} fusion(bf16[2,1,1024,1024]{3,2,1,0:T(8,128)(2,1)} %param.10, bf16[1,1024,256]{2,1,0:T(8,128)(2,1)S(1)} %copy-done.11, bf16[256,384]{0,1:T(8,128)(2,1)S(1)} %collective-permute-done.2, pred[]{:T(512)S(6)} %eq.104, bf16[256,384]{0,1:T(8,128)(2,1)S(1)} %convolution_convert_fusion.4, ...), kind=kOutput, calls=%fused_computation.22 | convolution fusion | flops 738656256 | bytes 4784129 | tf_op jit(solution)/shard_map/dot_general | solution.py:14
  127.4 4.9 %add_convert_fusion = bf16[1024,384]{1,0:T(8,128)(2,1)S(1)} fusion(bf16[1024,384]{1,0:T(8,128)(2,1)S(1)} %copy-done.13, f32[1024,384]{1,0:T(8,128)} %fusion.25, bf16[1024,384]{1,0:T(8,128)(2,1)} %copy-done.14, bf16[2,1,1024,1024]{3,2,1,0:T(8,128)(2,1)} %param.10, f32[]{:T(128)} %bitcast.27, f32[]{:T(128)} %bitcast, ...), kind=kOutput, calls=%fused_computation.14 | convolution fusion | flops 741801984 | bytes 7144449 | tf_op jit(solution)/shard_map/dot_general | solution.py:14
  132.2 17.4 %all_to_all.21 = bf16[8,128,384]{2,1,0:T(8,128)(2,1)S(1)} all-to-all(bf16[8,128,384]{2,1,0:T(8,128)(2,1)S(1)} %bitcast.85), channel_id=1, replica_groups=mesh['yl'=2,'x'=4,'yh'=2,'z'=8,'c'=2] {'yl','x'}, dimensions={0} | all-to-all | bytes 1572864 | tf_op jit(solution)/shard_map/all_to_all | solution.py:112
  149.6 0.1 convert_reduce_fusion
  149.8 0.8 broadcast_in_dim.54
  (32 shorter events, 0.2 us)
Async XLA Ops:
  0.0 1.1 copy-start
  1.1 3.0 %copy-start.9 = (bf16[2,1,1024,1024]{3,2,1,0:T(8,128)(2,1)S(1)}, bf16[2,1,1024,1024]{3,2,1,0:T(8,128)(2,1)}, u32[]{:S(2)}) copy-start(bf16[2,1,1024,1024]{3,2,1,0:T(8,128)(2,1)} %param.10) | copy-start | bytes 12582916
  4.1 1.3 copy-start.12
  4.1 1.3 copy-start.10
  5.4 0.9 copy-start.14
  5.9 0.7 copy-start.8
  5.9 0.8 copy-start.2
  6.4 1.5 %collective-permute-start.1 = (bf16[256,384]{0,1:T(8,128)(2,1)S(1)}, bf16[256,384]{0,1:T(8,128)(2,1)S(1)}, u32[]{:S(2)}, u32[]{:S(2)}) collective-permute-start(bf16[256,384]{0,1:T(8,128)(2,1)S(1)} %select_bitcast_fusion.1), channel_id=1, source_target_pairs={{0,1},{1,0},{2,3},{3,2},{4,5},{5,4},{6,7},{7,6},{8,9},{9,8},{10,11... | collective-permute-start | bytes 589832 | tf_op jit(solution)/shard_map/ppermute | solution.py:76
  7.2 2.5 %copy-start.4 = (s32[1,256]{1,0:T(1,128)}, s32[1,256]{1,0:T(1,128)S(1)}, u32[]{:S(2)}) copy-start(s32[1,256]{1,0:T(1,128)S(1)} %multiply_add_fusion.1) | copy-start | bytes 3076
  7.4 2.2 %copy-start.6 = (s32[1,256]{1,0:T(1,128)}, s32[1,256]{1,0:T(1,128)S(1)}, u32[]{:S(2)}) copy-start(s32[1,256]{1,0:T(1,128)S(1)} %multiply_add_fusion) | copy-start | bytes 3076
  9.7 33.2 %all-to-all-start = ((bf16[16,64,384]{2,1,0:T(8,128)(2,1)}), bf16[16,64,384]{2,1,0:T(8,128)(2,1)S(1)}, u32[]{:S(2)}, u32[]{:S(2)}) async-start(bf16[16,64,384]{2,1,0:T(8,128)(2,1)} %pad_maximum_fusion), calls=%async_computation | async-start | bytes 1572864 | tf_op jit(solution)/shard_map/all_to_all | solution.py:81
  45.5 5.8 %copy-start.1 = (bf16[2,64,2048]{2,1,0:T(8,128)(2,1)S(1)}, bf16[2,64,2048]{2,1,0:T(8,128)(2,1)}, u32[]{:S(2)}) copy-start(bf16[2,64,2048]{2,1,0:T(8,128)(2,1)} %param.12) | copy-start | bytes 1572868
  45.5 44.9 %all-to-all-start.1 = ((bf16[16,128,384]{2,1,0:T(8,128)(2,1)}), bf16[16,128,384]{2,1,0:T(8,128)(2,1)S(1)}, u32[]{:S(2)}, u32[]{:S(2)}) async-start(bf16[16,128,384]{2,1,0:T(8,128)(2,1)} %broadcast_in_dim.53), calls=%async_computation.1 | async-start | bytes 3145728 | tf_op jit(solution)/shard_map/all_to_all | solution.py:87
  51.4 1.7 %collective-permute-start = (bf16[64,2048]{1,0:T(8,128)(2,1)S(1)}, bf16[64,2048]{1,0:T(8,128)(2,1)S(1)}, u32[]{:S(2)}, u32[]{:S(2)}) collective-permute-start(bf16[64,2048]{1,0:T(8,128)(2,1)S(1)} %select_bitcast_fusion), channel_id=1, source_target_pairs={{0,1},{1,0},{2,3},{3,2},{4,5},{5,4},{6,7},{7,6},{8,9},{9,8},{10,11... | collective-permute-start | bytes 786440 | tf_op jit(solution)/shard_map/ppermute | solution.py:36
  92.2 28.7 %copy-start.5 = (s32[1,256]{1,0:T(1,128)S(1)}, s32[1,256]{1,0:T(1,128)}, u32[]{:S(2)}) copy-start(s32[1,256]{1,0:T(1,128)} %copy-done.4) | copy-start | bytes 3076
  92.2 29.0 %copy-start.7 = (s32[1,256]{1,0:T(1,128)S(1)}, s32[1,256]{1,0:T(1,128)}, u32[]{:S(2)}) copy-start(s32[1,256]{1,0:T(1,128)} %copy-done.6) | copy-start | bytes 3076
  120.8 0.9 copy-start.3
  120.8 2.4 %copy-start.11 = (bf16[1,1024,256]{2,1,0:T(8,128)(2,1)S(1)}, bf16[1,1024,256]{2,1,0:T(8,128)(2,1)}, u32[]{:S(2)}) copy-start(bf16[1,1024,256]{2,1,0:T(8,128)(2,1)} %param.11) | copy-start | bytes 1572868
  121.6 1.5 %collective-permute-start.2 = (bf16[256,384]{0,1:T(8,128)(2,1)S(1)}, bf16[256,384]{0,1:T(8,128)(2,1)S(1)}, u32[]{:S(2)}, u32[]{:S(2)}) collective-permute-start(bf16[256,384]{0,1:T(8,128)(2,1)S(1)} %get-tuple-element.17), channel_id=1, source_target_pairs={{0,1},{1,0},{2,3},{3,2},{4,5},{5,4},{6,7},{7,6},{8,9},{9,8},{10,11... | collective-permute-start | bytes 589832 | tf_op jit(solution)/shard_map/ppermute | solution.py:104
  123.2 4.2 %copy-start.13 = (bf16[1024,384]{1,0:T(8,128)(2,1)S(1)}, bf16[1024,384]{1,0:T(8,128)(2,1)}, u32[]{:S(2)}) copy-start(bf16[1024,384]{1,0:T(8,128)(2,1)} %copy-done.12) | copy-start | bytes 2359300

commit v2 on v0

v2 whole, which is shorter than its diff:
```python
import jax
import jax.numpy as jnp
from jax import lax
from jax.sharding import Mesh, PartitionSpec as P

BF = jnp.bfloat16
F32 = jnp.float32
SUB = ("yh", "z", "c")
EXCHANGE = ("yh", "c", "z")
SHIFT = ("yl", "x")
HALF = 192


def dot(a, b):
    return jnp.dot(a, b, preferred_element_type=F32)


def dot_t(a, b):
    return lax.dot_general(a, b, (((0,), (0,)), ((), ())), preferred_element_type=F32)


def roll(a):
    return jnp.concatenate([a[:, HALF:], a[:, :HALF]], axis=1)


def on_device(
    interior_rhs,
    interface_rhs,
    interior_inverse,
    coupling,
    schur_inverse,
    weights,
    owner_sub,
    index_blocks,
):
    y, z, c = lax.axis_index("yh"), lax.axis_index("z"), lax.axis_index("c")
    swap = [(0, 1), (1, 0)]
    rhs = interior_rhs[0]
    couple = coupling[0]

    def low(shape):
        return lax.broadcasted_iota(jnp.int32, shape, len(shape) - 1) < HALF

    mine = c == 0
    schur_keep = jnp.where(mine, schur_inverse[0], schur_inverse[1])
    schur_give = jnp.where(mine, schur_inverse[1], schur_inverse[0])
    schur_got = lax.ppermute(schur_give, "c", swap)
    schur_own = jnp.concatenate(
        [jnp.where(mine, schur_keep, schur_got), jnp.where(mine, schur_got, schur_keep)], axis=0
    )
    schur_other = lax.ppermute(schur_own, "yh", swap)

    eliminated = [dot(interior_inverse[j, 0], rhs).astype(BF) for j in range(2)]
    coupled = [dot_t(couple, e).astype(BF) for e in eliminated]

    owner = lax.dynamic_index_in_dim(owner_sub, (y * 8 + z) * 2 + c, 0, keepdims=False)
    idx = lax.dynamic_index_in_dim(index_blocks, owner, 0, keepdims=False)
    here, other = idx[:, None], idx[None, :]
    rank = jnp.sum(((here // 64 == other // 64) & (other < here)).astype(jnp.int32), axis=1)
    slot = ((idx // 128) % 8) * 32 + ((idx // 64) % 2) * 16 + rank
    line = lax.broadcasted_iota(jnp.int32, (256, 256), 0)
    hit = line == slot[None, :]
    upper = (idx >= 1024)[None, :]
    pack = jnp.concatenate([(hit & ~upper).astype(BF), (hit & upper).astype(BF)], axis=1)

    low_k = low((256, 384))
    zero = jnp.zeros((), BF)
    packed = []
    rolled = [roll(x) for x in coupled]
    for h in range(2):
        for j in range(2):
            a, b = (coupled[j], rolled[j]) if h == 0 else (rolled[j], coupled[j])
            both = jnp.concatenate([jnp.where(low_k, a, zero), jnp.where(low_k, zero, b)], axis=0)
            packed.append(dot(pack, both).astype(BF).reshape(8, 32, 384))
    packed = jnp.concatenate(packed, axis=0)
    arrived = lax.all_to_all(packed, EXCHANGE, 0, 0, tiled=True).reshape(1024, 384)

    owners = owner_sub.reshape(2, 8, 2).transpose(0, 2, 1).reshape(32)
    names = lax.broadcasted_iota(jnp.int32, (32, 32, 1), 1)
    idx_all = jnp.sum(jnp.where(owners[:, None, None] == names, index_blocks[None], 0), axis=1)
    rows = lax.broadcasted_iota(jnp.int32, (1, 1, 256), 2)
    rows = (rows // 128) * 1024 + z * 128 + rows % 128
    held = jnp.any(idx_all[:, :, None] == rows, axis=1)
    first = lax.broadcasted_iota(jnp.int32, (256, 256), 0)
    second = lax.broadcasted_iota(jnp.int32, (256, 256), 1)
    before = ((first < second) & (first // 64 == second // 64)).astype(BF)
    place = dot(held.astype(BF), before).astype(jnp.int32)
    place = place + 16 * ((lax.broadcasted_iota(jnp.int32, (32, 256), 1) // 64) % 2)
    place = jnp.where(held, place, -1)
    select = (
        (place[:, None, :] == lax.broadcasted_iota(jnp.int32, (32, 32, 256), 1))
        .astype(BF)
        .reshape(1024, 256)
    )

    base = [lax.dynamic_slice_in_dim(interface_rhs, q * 1024 + z * 128, 128, 0) for q in range(2)]
    low_i = low((128, 384))
    plane_rhs = jnp.where(
        y == 0,
        jnp.where(low_i, base[0], roll(base[1])),
        jnp.where(low_i, roll(base[0]), base[1]),
    )

    spread = jnp.concatenate(
        [(weights[j] * dot(interior_inverse[j, 0], couple)).astype(BF) for j in range(2)], axis=1
    )
    direct = weights[0] * eliminated[0].astype(F32) + weights[1] * eliminated[1].astype(F32)

    rows0 = jnp.where(y == 0, schur_own, schur_other)
    rows1 = jnp.where(y == 0, schur_other, schur_own)
    order = (0, -1, 1, -2, 2, -3, 3, 4)
    blocks = []
    for s in order:
        at = (z + s + 8) % 8 * 128
        blocks.append(
            jnp.concatenate(
                [
                    lax.dynamic_slice_in_dim(r, q * 1024 + at, 128, 1)
                    for r in (rows0, rows1)
                    for q in range(2)
                ],
                axis=0,
            )
        )
    schur = jnp.concatenate(blocks, axis=1)
    arrived, select, spread, direct, plane_rhs, schur = lax.optimization_barrier(
        (arrived, select, spread, direct, plane_rhs, schur)
    )

    summed = dot_t(select, arrived)
    summed = jnp.where(low_i, summed[:128], summed[128:])
    reduced = (plane_rhs.astype(F32) - summed).astype(BF)

    up = [(i, (i + 1) % 8) for i in range(8)]
    down = [(i, (i + 7) % 8) for i in range(8)]
    ring = [reduced]
    a = b = reduced
    for s in range(3):
        a = lax.ppermute(a, "z", up)
        b = lax.ppermute(b, "z", down)
        ring += [a, b]
    ring.append(lax.ppermute(a, "z", up))
    solved = dot(schur, jnp.concatenate(ring, axis=0))
    s00, s01, s10, s11 = [solved[128 * i : 128 * (i + 1)] for i in range(4)]
    solved = (jnp.where(low_i, s00, s11) + roll(jnp.where(low_i, s10, s01))).astype(BF)
    both = jnp.concatenate(
        [jnp.where(low_i, solved, zero), jnp.where(low_i, zero, solved)], axis=0
    )
    answers = dot(select, both).astype(BF).reshape(32, 32, 384)
    back = lax.all_to_all(answers, EXCHANGE, 0, 0, tiled=True).reshape(4, 256, 384)
    picked = []
    for j in range(2):
        from0, from1 = dot_t(pack, back[j]), dot_t(pack, back[2 + j])
        straight = jnp.where(low_k, from0[:256], from1[256:])
        crossed = jnp.where(low_k, from1[:256], from0[256:])
        picked.append((straight + roll(crossed)).astype(BF))
    total = direct - dot(spread, jnp.concatenate(picked, axis=0))
    pieces = lax.all_to_all(total.astype(BF).reshape(8, 128, 384), SHIFT, 0, 0, tiled=True)
    return jnp.sum(pieces.reshape(8, 128, 1, 384).astype(F32), axis=0)


def solution(mesh):
    fine = Mesh(mesh.devices.reshape(2, 4, 2, 8, 2), ("yl", "x", "yh", "z", "c"))
    in_specs = (
        P(SUB, None, None),
        P(),
        P(SHIFT, SUB, None, None),
        P(SUB, None, None),
        P(SHIFT, SUB, None),
        P(SHIFT),
        P(),
        P(),
    )
    out_specs = P(SHIFT, SUB, None)
    return jax.shard_map(
        on_device, mesh=fine, in_specs=in_specs, out_specs=out_specs, check_vma=False
    )
```

time: 566 us -> 147 us (0.26)
  waiting for transfers between devices: 515 us -> 27.7 us
  blocking collectives: 0 us -> 50.5 us
  starting transfers between devices: 0.13 us -> 20.6 us
  other arithmetic: 0 us -> 16.8 us
  between operations: 15.2 us -> 2.49 us
  matrix products: 31 us -> 21.5 us
    psum x2 -> x0, waiting for transfers between devices: 365 us -> none  [the longest x1 283 us: on_device(): lax.psum(jnp.dot(selector, coupled, preferred_element_type=jnp.float32),...]
    all_gather x2 -> x0, waiting for transfers between devices: 149 us -> none  [on_device(): piece = lax.all_gather(interface_sol, 'sub', axis=0, tiled=True)]
    all_to_all x0 -> x2, blocking collectives: none -> 50.5 us  [the longest x1 32.9 us: on_device(): lax.all_to_all(answers, EXCHANGE, 0, 0, tiled=True).reshape(4, 256, 384)]
    ppermute x0 -> x9, waiting for transfers between devices: none -> 27.7 us  [the longest x1 10.6 us: on_device(): schur_other = lax.ppermute(schur_own, 'yh', swap)]
    all_to_all x0 -> x1, starting transfers between devices: none -> 11.5 us  [on_device(): lax.all_to_all(packed, EXCHANGE, 0, 0, tiled=True).reshape(1024, 384)]
    dot_general x10 -> x19, matrix products: 31 us -> 21.5 us  [the longest x12 19 us: dot(): return jnp.dot(a, b, preferred_element_type=F32)]
    ppermute x0 -> x9, starting transfers between devices: none -> 9.18 us  [the longest x3 5.1 us: on_device(): b = lax.ppermute(b, 'z', down)]
  transfers between devices with their start and end apart: 4 -> 10, of which waited for: 4 -> 6; matrix products, arithmetic and copies ran while one was open for 2% -> 25% of each run, Pallas kernels for 0% -> 0%
where the time goes in v2:
time: 147 us
  blocking collectives  50.5 us (34%)
  waiting for transfers between devices  27.7 us (19%)
  matrix products  21.5 us (15%)
  starting transfers between devices  20.6 us (14%)
  other arithmetic  16.8 us (11%)
  local copies, waits for them, and re-layouts  6.88 us (5%)
  between operations  2.49 us (2%)
    all_to_all x1, blocking collectives, on_device(): lax.all_to_all(answers, EXCHANGE, 0, 0, tiled=True).reshape(4, 256, 384)  32.9 us
    dot_general x12, matrix products, dot(): return jnp.dot(a, b, preferred_element_type=F32)  19 us
    all_to_all x1, blocking collectives, on_device(): lax.all_to_all(total.astype(BF).reshape(8, 128, 384), SHIFT, 0, 0, tiled=...  17.6 us
    all_to_all x1, starting transfers between devices, on_device(): lax.all_to_all(packed, EXCHANGE, 0, 0, tiled=True).reshape(1024, 384)  11.5 us
    ppermute x1, waiting for transfers between devices, on_device(): schur_other = lax.ppermute(schur_own, 'yh', swap)  10.6 us
    ppermute x3, waiting for transfers between devices, on_device(): a = lax.ppermute(a, 'z', up)  6.04 us
    ppermute x1, waiting for transfers between devices, on_device(): ring.append(lax.ppermute(a, 'z', up))  5.93 us
    ppermute x3, waiting for transfers between devices, on_device(): b = lax.ppermute(b, 'z', down)  5.13 us
  transfers between devices with their start and end apart: 10, of which 6 were waited for; matrix products, arithmetic and copies ran while one was open for 25% of the time, Pallas kernels for 0%

profile of v2, /device:TPU:32, one launch (start us, length us, event | category | flops | bytes accessed | tf_op | source)
XLA Modules:
  0.0 146.6 jit_solution(227384202884006373)
XLA Ops:
  0.0 1.1 select_bitcast_fusion
  1.2 1.3 dynamic_slice.110
  3.8 1.4 fusion.111
  5.8 0.7 not_reduce_fusion
  6.8 3.0 %fusion.12 = bf16[1024,384]{1,0:T(8,128)(2,1)S(1)} fusion(bf16[2,1,1024,1024]{3,2,1,0:T(8,128)(2,1)} %param.10, bf16[1,1024,384]{2,1,0:T(8,128)(2,1)S(1)} %copy-done), kind=kOutput, calls=%fused_computation.17 | convolution fusion | flops 805699584 | bytes 3670016 | tf_op jit(solution)/shard_map/dot_general | solution.py:15
  9.8 0.4 fusion.30
  10.3 3.7 %multiply_add_fusion = (f32[1024,384]{1,0:T(8,128)}, bf16[1024,384]{1,0:T(8,128)(2,1)S(1)}) fusion(bf16[1024,384]{1,0:T(8,128)(2,1)S(1)} %fusion.12, f32[]{:T(128)} %bitcast.19, f32[]{:T(128)} %bitcast.18, bf16[1,1024,384]{2,1,0:T(8,128)(2,1)S(1)} %copy-done, bf16[2,1,1024,1024]{3,2,1,0:T(8,128)(2,1)S(1)} %copy-done.8), kind=kOutput, calls=%fused_computation.15 | convolution fusion | flops 807665664 | bytes 6029320 | tf_op jit(solution)/shard_map/dot_general | solution.py:15
  14.0 0.4 fusion.31
  15.2 0.3 convolution_convert_fusion.2
  16.2 1.0 pad_maximum_fusion.1
  17.2 11.5 %all-to-all-start = ((bf16[32,32,384]{2,1,0:T(8,128)(2,1)}), bf16[32,32,384]{2,1,0:T(8,128)(2,1)S(1)}, u32[]{:S(2)}, u32[]{:S(2)}) async-start(bf16[32,32,384]{2,1,0:T(8,128)(2,1)} %pad_maximum_fusion.1), calls=%async_computation | async-start | bytes 1572864 | tf_op jit(solution)/shard_map/all_to_all | solution.py:76
  28.7 3.8 %fusion.27 = bf16[1024,256]{0,1:T(8,128)(2,1)} fusion(bf16[2,1,1024,1024]{3,2,1,0:T(8,128)(2,1)} %param.10, bf16[1,1024,256]{2,1,0:T(8,128)(2,1)S(1)} %copy-done.9, f32[]{:T(128)} %bitcast.18), kind=kOutput, calls=%fused_computation.22 | convolution fusion | flops 537395200 | bytes 3146240 | tf_op jit(solution)/shard_map/dot_general | solution.py:15
  33.1 1.4 compare_reduce_fusion
  34.5 3.8 %fusion.24 = bf16[1024,256]{0,1:T(8,128)(2,1)} fusion(bf16[2,1,1024,1024]{3,2,1,0:T(8,128)(2,1)} %param.10, bf16[1,1024,256]{2,1,0:T(8,128)(2,1)S(1)} %copy-done.9, f32[]{:T(128)} %bitcast.19), kind=kOutput, calls=%fused_computation.21 | convolution fusion | flops 537395200 | bytes 3146240 | tf_op jit(solution)/shard_map/dot_general | solution.py:15
  38.4 0.9 pad_maximum_fusion.2
  39.3 3.0 %collective-permute-start.1 = (bf16[128,2048]{1,0:T(8,128)(2,1)}, bf16[128,2048]{1,0:T(8,128)(2,1)}, u32[]{:S(2)}, u32[]{:S(2)}) collective-permute-start(bf16[128,2048]{1,0:T(8,128)(2,1)} %pad_maximum_fusion.2), channel_id=1, source_target_pairs={{0,16},{16,0},{1,17},{17,1},{2,18},{18,2},{3,19},{19,3},{4,20},{20... | collective-permute-start | bytes 1572872 | tf_op jit(solution)/shard_map/ppermute | solution.py:51
  43.0 1.1 fusion.104
  44.1 1.3 pad_maximum_fusion
  45.3 1.7 %fusion.77 = bf16[128,384]{1,0:T(8,128)(2,1)} fusion(bf16[128,192]{1,0:T(8,128)(2,1)S(1)} %get-tuple-element.25, bf16[128,192]{1,0:T(8,128)(2,1)S(1)} %get-tuple-element.26, bf16[128,192]{1,0:T(8,128)(2,1)S(1)} %get-tuple-element.27, bf16[128,192]{1,0:T(8,128)(2,1)S(1)} %get-tuple-element.24, bf16[2048,384]{1,0:T(8,128)(2,1)} %param.9, s32[]{:T(128)S(6)} %select_n.333, ...), kind=kLoop, calls=%fused_computation.118 | loop fusion | flops 540672 | bytes 491913 | tf_op jit(solution)/shard_map/jit(_where)/select_n | solution.py:98
  47.0 10.6 %collective-permute-done.1 = bf16[128,2048]{1,0:T(8,128)(2,1)} collective-permute-done((bf16[128,2048]{1,0:T(8,128)(2,1)}, bf16[128,2048]{1,0:T(8,128)(2,1)}, u32[]{:S(2)}, u32[]{:S(2)}) %collective-permute-start.1) | collective-permute-done | bytes 524320 | tf_op jit(solution)/shard_map/ppermute | solution.py:51
  57.7 1.3 broadcast_select_fusion.1
  58.9 0.4 constant_dynamic-slice_fusion.1
  59.4 0.7 maximum_dynamic-update-slice_fusion.7
  60.1 0.7 maximum_dynamic-update-slice_fusion.6
  60.8 0.7 maximum_dynamic-update-slice_fusion.5
  61.5 0.7 maximum_dynamic-update-slice_fusion.4
  62.1 0.7 maximum_dynamic-update-slice_fusion.3
  62.8 0.7 maximum_dynamic-update-slice_fusion.2
  63.5 0.7 maximum_dynamic-update-slice_fusion.1
  64.2 0.7 maximum_dynamic-update-slice_fusion
  64.9 0.5 fusion.112
  65.4 1.7 %collective-permute-start.3 = (bf16[128,384]{1,0:T(8,128)(2,1)S(1)}, bf16[128,384]{1,0:T(8,128)(2,1)S(1)}, u32[]{:S(2)}, u32[]{:S(2)}) collective-permute-start(bf16[128,384]{1,0:T(8,128)(2,1)S(1)} %get-tuple-element.22), channel_id=1, source_target_pairs={{0,14},{2,0},{4,2},{6,4},{8,6},{10,8},{12,10},{14,12},{1,15},{3,1}... | collective-permute-start | bytes 294920 | tf_op jit(solution)/shard_map/ppermute | solution.py:140
  67.1 0.4 collective-permute-start.2
  67.5 2.6 %collective-permute-done.3 = bf16[128,384]{1,0:T(8,128)(2,1)S(1)} collective-permute-done((bf16[128,384]{1,0:T(8,128)(2,1)S(1)}, bf16[128,384]{1,0:T(8,128)(2,1)S(1)}, u32[]{:S(2)}, u32[]{:S(2)}) %collective-permute-start.3) | collective-permute-done | bytes 98336 | tf_op jit(solution)/shard_map/ppermute | solution.py:140
  70.1 1.6 %collective-permute-start.5 = (bf16[128,384]{1,0:T(8,128)(2,1)S(1)}, bf16[128,384]{1,0:T(8,128)(2,1)S(1)}, u32[]{:S(2)}, u32[]{:S(2)}) collective-permute-start(bf16[128,384]{1,0:T(8,128)(2,1)S(1)} %collective-permute-done.3), channel_id=1, source_target_pairs={{0,14},{2,0},{4,2},{6,4},{8,6},{10,8},{12,10},{14,12},{1,15},{3,1}... | collective-permute-start | bytes 294920 | tf_op jit(solution)/shard_map/ppermute | solution.py:140
  71.7 0.4 collective-permute-start.4
  72.2 2.5 %collective-permute-done.5 = bf16[128,384]{1,0:T(8,128)(2,1)S(1)} collective-permute-done((bf16[128,384]{1,0:T(8,128)(2,1)S(1)}, bf16[128,384]{1,0:T(8,128)(2,1)S(1)}, u32[]{:S(2)}, u32[]{:S(2)}) %collective-permute-start.5) | collective-permute-done | bytes 98336 | tf_op jit(solution)/shard_map/ppermute | solution.py:140
  74.7 1.9 %collective-permute-start.7 = (bf16[128,384]{1,0:T(8,128)(2,1)S(1)}, bf16[128,384]{1,0:T(8,128)(2,1)S(1)}, u32[]{:S(2)}, u32[]{:S(2)}) collective-permute-start(bf16[128,384]{1,0:T(8,128)(2,1)S(1)} %collective-permute-done.5), channel_id=1, source_target_pairs={{0,14},{2,0},{4,2},{6,4},{8,6},{10,8},{12,10},{14,12},{1,15},{3,1}... | collective-permute-start | bytes 294920 | tf_op jit(solution)/shard_map/ppermute | solution.py:140
  76.6 0.4 collective-permute-done.4
  77.2 5.7 %collective-permute-done.6 = bf16[128,384]{1,0:T(8,128)(2,1)S(1)} collective-permute-done((bf16[128,384]{1,0:T(8,128)(2,1)S(1)}, bf16[128,384]{1,0:T(8,128)(2,1)S(1)}, u32[]{:S(2)}, u32[]{:S(2)}) %collective-permute-start.6) | collective-permute-done | bytes 98336 | tf_op jit(solution)/shard_map/ppermute | solution.py:139
  82.9 5.9 %collective-permute-done.8 = bf16[128,384]{1,0:T(8,128)(2,1)S(1)} collective-permute-done((bf16[128,384]{1,0:T(8,128)(2,1)S(1)}, bf16[128,384]{1,0:T(8,128)(2,1)S(1)}, u32[]{:S(2)}, u32[]{:S(2)}) %collective-permute-start.8) | collective-permute-done | bytes 98336 | tf_op jit(solution)/shard_map/ppermute | solution.py:142
  88.8 1.9 %fusion.113 = f32[512,384]{1,0:T(8,128)S(1)} fusion(bf16[512,1024]{1,0:T(8,128)(2,1)} %maximum_dynamic-update-slice_fusion, bf16[1024,384]{1,0:T(8,128)(2,1)S(1)} %constant_dynamic-update-slice_fusion), kind=kOutput, calls=%fused_computation.233 | convolution fusion | flops 402653184 | bytes 2621440 | tf_op jit(solution)/shard_map/dot_general | solution.py:15
  91.0 0.4 convolution_convert_fusion
  91.5 32.9 %all_to_all.15 = bf16[32,32,384]{2,1,0:T(8,128)(2,1)S(1)} all-to-all(bf16[32,32,384]{2,1,0:T(8,128)(2,1)S(1)} %bitcast.85), channel_id=1, replica_groups=mesh['yl'=2,'x'=4,'yh'=2,'z'=8,'c'=2] {'yh','c','z'}, dimensions={0} | all-to-all | bytes 1572864 | tf_op jit(solution)/shard_map/all_to_all | solution.py:150
  126.2 1.1 copy-done.4
  127.3 0.8 subtract_convert_fusion
  128.1 17.6 %all_to_all.16 = bf16[8,128,384]{2,1,0:T(8,128)(2,1)S(1)} all-to-all(bf16[8,128,384]{2,1,0:T(8,128)(2,1)S(1)} %bitcast.87), channel_id=1, replica_groups=mesh['yl'=2,'x'=4,'yh'=2,'z'=8,'c'=2] {'yl','x'}, dimensions={0} | all-to-all | bytes 1572864 | tf_op jit(solution)/shard_map/all_to_all | solution.py:158
  145.8 0.8 reduce_sum.35
  (71 shorter events, 5.4 us)
Async XLA Ops:
  0.0 6.8 %copy-start = (bf16[1,1024,384]{2,1,0:T(8,128)(2,1)S(1)}, bf16[1,1024,384]{2,1,0:T(8,128)(2,1)}, u32[]{:S(2)}) copy-start(bf16[1,1024,384]{2,1,0:T(8,128)(2,1)} %param.8) | copy-start | bytes 2359300
  1.1 37.2 %collective-permute-start = (bf16[64,2048]{1,0:T(8,128)(2,1)S(1)}, bf16[64,2048]{1,0:T(8,128)(2,1)S(1)}, u32[]{:S(2)}, u32[]{:S(2)}) collective-permute-start(bf16[64,2048]{1,0:T(8,128)(2,1)S(1)} %select_bitcast_fusion), channel_id=1, source_target_pairs={{0,1},{1,0},{2,3},{3,2},{4,5},{5,4},{6,7},{7,6},{8,9},{9,8},{10,11... | collective-permute-start | bytes 786440 | tf_op jit(solution)/shard_map/ppermute | solution.py:47
  6.8 3.0 %copy-start.9 = (bf16[1,1024,256]{2,1,0:T(8,128)(2,1)S(1)}, bf16[1,1024,256]{2,1,0:T(8,128)(2,1)}, u32[]{:S(2)}) copy-start(bf16[1,1024,256]{2,1,0:T(8,128)(2,1)} %param.11) | copy-start | bytes 1572868
  6.8 3.4 %copy-start.8 = (bf16[2,1,1024,1024]{3,2,1,0:T(8,128)(2,1)S(1)}, bf16[2,1,1024,1024]{3,2,1,0:T(8,128)(2,1)}, u32[]{:S(2)}) copy-start(bf16[2,1,1024,1024]{3,2,1,0:T(8,128)(2,1)} %param.10) | copy-start | bytes 12582916
  15.8 12.8 %copy-start.7 = (s32[32]{0:T(128)S(1)}, s32[32]{0:T(128)}, u32[]{:S(2)}) copy-start(s32[32]{0:T(128)} %param.14) | copy-start | bytes 388
  17.2 47.7 %all-to-all-start = ((bf16[32,32,384]{2,1,0:T(8,128)(2,1)}), bf16[32,32,384]{2,1,0:T(8,128)(2,1)S(1)}, u32[]{:S(2)}, u32[]{:S(2)}) async-start(bf16[32,32,384]{2,1,0:T(8,128)(2,1)} %pad_maximum_fusion.1), calls=%async_computation | async-start | bytes 1572864 | tf_op jit(solution)/shard_map/all_to_all | solution.py:76
  28.7 4.1 %copy-start.6 = (s32[32,256]{1,0:T(8,128)S(1)}, s32[32,256]{1,0:T(8,128)}, u32[]{:S(2)}) copy-start(s32[32,256]{1,0:T(8,128)} %param.15) | copy-start | bytes 98308
  34.5 3.9 %copy-start.3 = (bf16[2,64,2048]{2,1,0:T(8,128)(2,1)S(1)}, bf16[2,64,2048]{2,1,0:T(8,128)(2,1)}, u32[]{:S(2)}) copy-start(bf16[2,64,2048]{2,1,0:T(8,128)(2,1)} %param.12) | copy-start | bytes 1572868
  38.4 4.4 %copy-start.1 = (bf16[64,2048]{1,0:T(8,128)(2,1)}, bf16[64,2048]{1,0:T(8,128)(2,1)S(1)}, u32[]{:S(2)}) copy-start(bf16[64,2048]{1,0:T(8,128)(2,1)S(1)} %get-tuple-element.35) | copy-start | bytes 786436
  39.3 18.4 %collective-permute-start.1 = (bf16[128,2048]{1,0:T(8,128)(2,1)}, bf16[128,2048]{1,0:T(8,128)(2,1)}, u32[]{:S(2)}, u32[]{:S(2)}) collective-permute-start(bf16[128,2048]{1,0:T(8,128)(2,1)} %pad_maximum_fusion.2), channel_id=1, source_target_pairs={{0,16},{16,0},{1,17},{17,1},{2,18},{18,2},{3,19},{19,3},{4,20},{20... | collective-permute-start | bytes 1572872 | tf_op jit(solution)/shard_map/ppermute | solution.py:51
  42.8 14.9 %copy-start.2 = (bf16[64,2048]{1,0:T(8,128)(2,1)S(1)}, bf16[64,2048]{1,0:T(8,128)(2,1)}, u32[]{:S(2)}) copy-start(bf16[64,2048]{1,0:T(8,128)(2,1)} %copy-done.1) | copy-start | bytes 786436
  59.4 6.0 %copy-start.5 = (bf16[128,384]{1,0:T(8,128)(2,1)S(1)}, bf16[128,384]{1,0:T(8,128)(2,1)}, u32[]{:S(2)}) copy-start(bf16[128,384]{1,0:T(8,128)(2,1)} %fusion.77) | copy-start | bytes 294916
  65.4 4.7 %collective-permute-start.3 = (bf16[128,384]{1,0:T(8,128)(2,1)S(1)}, bf16[128,384]{1,0:T(8,128)(2,1)S(1)}, u32[]{:S(2)}, u32[]{:S(2)}) collective-permute-start(bf16[128,384]{1,0:T(8,128)(2,1)S(1)} %get-tuple-element.22), channel_id=1, source_target_pairs={{0,14},{2,0},{4,2},{6,4},{8,6},{10,8},{12,10},{14,12},{1,15},{3,1}... | collective-permute-start | bytes 294920 | tf_op jit(solution)/shard_map/ppermute | solution.py:140
  67.1 4.6 %collective-permute-start.2 = (bf16[128,384]{1,0:T(8,128)(2,1)S(1)}, bf16[128,384]{1,0:T(8,128)(2,1)S(1)}, u32[]{:S(2)}, u32[]{:S(2)}) collective-permute-start(bf16[128,384]{1,0:T(8,128)(2,1)S(1)} %get-tuple-element.22), channel_id=1, source_target_pairs={{0,2},{2,4},{4,6},{6,8},{8,10},{10,12},{12,14},{14,0},{1,3},{3,5},... | collective-permute-start | bytes 294920 | tf_op jit(solution)/shard_map/ppermute | solution.py:139
  70.1 4.6 %collective-permute-start.5 = (bf16[128,384]{1,0:T(8,128)(2,1)S(1)}, bf16[128,384]{1,0:T(8,128)(2,1)S(1)}, u32[]{:S(2)}, u32[]{:S(2)}) collective-permute-start(bf16[128,384]{1,0:T(8,128)(2,1)S(1)} %collective-permute-done.3), channel_id=1, source_target_pairs={{0,14},{2,0},{4,2},{6,4},{8,6},{10,8},{12,10},{14,12},{1,15},{3,1}... | collective-permute-start | bytes 294920 | tf_op jit(solution)/shard_map/ppermute | solution.py:140
  71.7 5.3 %collective-permute-start.4 = (bf16[128,384]{1,0:T(8,128)(2,1)S(1)}, bf16[128,384]{1,0:T(8,128)(2,1)S(1)}, u32[]{:S(2)}, u32[]{:S(2)}) collective-permute-start(bf16[128,384]{1,0:T(8,128)(2,1)S(1)} %collective-permute-done.2), channel_id=1, source_target_pairs={{0,2},{2,4},{4,6},{6,8},{8,10},{10,12},{12,14},{14,0},{1,3},{3,5},... | collective-permute-start | bytes 294920 | tf_op jit(solution)/shard_map/ppermute | solution.py:139
  74.7 8.1 %collective-permute-start.7 = (bf16[128,384]{1,0:T(8,128)(2,1)S(1)}, bf16[128,384]{1,0:T(8,128)(2,1)S(1)}, u32[]{:S(2)}, u32[]{:S(2)}) collective-permute-start(bf16[128,384]{1,0:T(8,128)(2,1)S(1)} %collective-permute-done.5), channel_id=1, source_target_pairs={{0,14},{2,0},{4,2},{6,4},{8,6},{10,8},{12,10},{14,12},{1,15},{3,1}... | collective-permute-start | bytes 294920 | tf_op jit(solution)/shard_map/ppermute | solution.py:140
  77.0 5.8 %collective-permute-start.6 = (bf16[128,384]{1,0:T(8,128)(2,1)S(1)}, bf16[128,384]{1,0:T(8,128)(2,1)S(1)}, u32[]{:S(2)}, u32[]{:S(2)}) collective-permute-start(bf16[128,384]{1,0:T(8,128)(2,1)S(1)} %collective-permute-done.4), channel_id=1, source_target_pairs={{0,2},{2,4},{4,6},{6,8},{8,10},{10,12},{12,14},{14,0},{1,3},{3,5},... | collective-permute-start | bytes 294920 | tf_op jit(solution)/shard_map/ppermute | solution.py:139
  82.8 6.0 %collective-permute-start.8 = (bf16[128,384]{1,0:T(8,128)(2,1)S(1)}, bf16[128,384]{1,0:T(8,128)(2,1)S(1)}, u32[]{:S(2)}, u32[]{:S(2)}) collective-permute-start(bf16[128,384]{1,0:T(8,128)(2,1)S(1)} %collective-permute-done.6), channel_id=1, source_target_pairs={{0,2},{2,4},{4,6},{6,8},{8,10},{10,12},{12,14},{14,0},{1,3},{3,5},... | collective-permute-start | bytes 294920 | tf_op jit(solution)/shard_map/ppermute | solution.py:142
  125.9 1.4 copy-start.4

commit v3 on v2

v3 whole, which is shorter than its diff:
```python
import jax
import jax.numpy as jnp
from jax import lax
from jax.experimental import pallas as pl
from jax.experimental.pallas import tpu as pltpu
from jax.sharding import Mesh, PartitionSpec as P

BF = jnp.bfloat16
F32 = jnp.float32
SUB = ("yh", "z", "c")
EXCHANGE = ("yh", "c", "z")
SHIFT = ("yl", "x")
HALF = 192


def dot(a, b):
    return jnp.dot(a, b, preferred_element_type=F32)


def dot_t(a, b):
    return lax.dot_general(a, b, (((0,), (0,)), ((), ())), preferred_element_type=F32)


def roll(a):
    return jnp.concatenate([a[:, HALF:], a[:, :HALF]], axis=1)


def roll32(a):
    return pltpu.roll(a, HALF, 1)


def start_kernel(
    position_ref,
    owner_ref,
    blocks_ref,
    inverse_ref,
    rhs_ref,
    couple_ref,
    eliminated_ref,
    packed_ref,
    pack_ref,
    pick_ref,
    total_ref,
):
    j, i = pl.program_id(0), pl.program_id(1)

    @pl.when((j == 0) & (i == 0))
    def _():
        row = blocks_ref[pl.ds(owner_ref[position_ref[0]], 1), :]
        across = jnp.broadcast_to(row, (256, 256))
        down = jnp.broadcast_to(row.astype(F32), (256, 256)).T.astype(jnp.int32)
        same = (across >> 6) == (down >> 6)
        rank = jnp.sum((same & (down < across)).astype(F32), axis=0, keepdims=True)
        slot = ((row >> 7) & 7) * 32 + ((row >> 6) & 1) * 16 + rank.astype(jnp.int32)
        hit = lax.broadcasted_iota(jnp.int32, (256, 256), 0) == slot
        pack_ref[:, :256] = jnp.where(hit & (across < 1024), 1.0, 0.0).astype(BF)
        pack_ref[:, 256:] = jnp.where(hit & (across >= 1024), 1.0, 0.0).astype(BF)
        rank = jnp.sum((same & (across < down)).astype(F32), axis=1, keepdims=True)
        slot = ((down >> 7) & 7) * 32 + ((down >> 6) & 1) * 16 + rank.astype(jnp.int32)
        hit = lax.broadcasted_iota(jnp.int32, (256, 256), 1) == slot
        pick_ref[:256] = jnp.where(hit & (down < 1024), 1.0, 0.0).astype(BF)
        pick_ref[256:] = jnp.where(hit & (down >= 1024), 1.0, 0.0).astype(BF)

    @pl.when(i == 0)
    def _():
        total_ref[...] = jnp.zeros_like(total_ref)

    part = dot(inverse_ref[0, 0], rhs_ref[0]).astype(BF)
    eliminated_ref[0] = part
    total_ref[...] += dot_t(couple_ref[0], part)

    @pl.when(i == pl.num_programs(1) - 1)
    def _():
        coupled = total_ref[...].astype(BF).astype(F32)
        turned = roll32(coupled)
        low = lax.broadcasted_iota(jnp.int32, (256, 384), 1) < HALF
        for h, (a, b) in enumerate(((coupled, turned), (turned, coupled))):
            a = jnp.where(low, a, 0.0).astype(BF)
            b = jnp.where(low, 0.0, b).astype(BF)
            packed_ref[h, 0] = (dot(pack_ref[:, :256], a) + dot(pack_ref[:, 256:], b)).astype(BF)


def start(position, owner_sub, index_blocks, inverse, rhs, couple, rows=1024):
    steps = 1024 // rows
    smem = pl.BlockSpec(memory_space=pltpu.SMEM)
    return pl.pallas_call(
        start_kernel,
        grid=(2, steps),
        in_specs=[
            smem,
            smem,
            pl.BlockSpec((32, 256), lambda j, i: (0, 0)),
            pl.BlockSpec((1, 1, rows, 1024), lambda j, i: (j, 0, i, 0)),
            pl.BlockSpec((1, 1024, 384), lambda j, i: (0, 0, 0)),
            pl.BlockSpec((1, rows, 256), lambda j, i: (0, i, 0)),
        ],
        out_specs=[
            pl.BlockSpec((1, rows, 384), lambda j, i: (j, i, 0)),
            pl.BlockSpec((2, 1, 256, 384), lambda j, i: (0, j, 0, 0)),
            pl.BlockSpec((256, 512), lambda j, i: (0, 0)),
            pl.BlockSpec((512, 256), lambda j, i: (0, 0)),
        ],
        out_shape=[
            jax.ShapeDtypeStruct((2, 1024, 384), BF),
            jax.ShapeDtypeStruct((2, 2, 256, 384), BF),
            jax.ShapeDtypeStruct((256, 512), BF),
            jax.ShapeDtypeStruct((512, 256), BF),
        ],
        scratch_shapes=[pltpu.VMEM((256, 384), F32)],
        name="start",
    )(position, owner_sub, index_blocks, inverse, rhs, couple)


def finish_kernel(
    weights_ref, back_ref, pick_ref, spread0_ref, spread1_ref, eliminated_ref, out_ref, picked_ref
):
    @pl.when(pl.program_id(0) == 0)
    def _():
        low = lax.broadcasted_iota(jnp.int32, (256, 384), 1) < HALF
        for j in range(2):
            top = [dot(pick_ref[:256], back_ref[2 * h + j]) for h in range(2)]
            end = [dot(pick_ref[256:], back_ref[2 * h + j]) for h in range(2)]
            straight = jnp.where(low, top[0], end[1])
            crossed = jnp.where(low, top[1], end[0])
            picked_ref[j] = (straight + roll32(crossed)).astype(BF)

    total = weights_ref[0] * eliminated_ref[0].astype(F32)
    total += weights_ref[1] * eliminated_ref[1].astype(F32)
    total -= dot(spread0_ref[...], picked_ref[0]) + dot(spread1_ref[...], picked_ref[1])
    out_ref[...] = total.astype(BF)


def finish(weights, back, pick, spread0, spread1, eliminated, rows=512):
    return pl.pallas_call(
        finish_kernel,
        grid=(1024 // rows,),
        in_specs=[
            pl.BlockSpec(memory_space=pltpu.SMEM),
            pl.BlockSpec((4, 256, 384), lambda i: (0, 0, 0)),
            pl.BlockSpec((512, 256), lambda i: (0, 0)),
            pl.BlockSpec((rows, 256), lambda i: (i, 0)),
            pl.BlockSpec((rows, 256), lambda i: (i, 0)),
            pl.BlockSpec((2, rows, 384), lambda i: (0, i, 0)),
        ],
        out_specs=pl.BlockSpec((rows, 384), lambda i: (i, 0)),
        out_shape=jax.ShapeDtypeStruct((1024, 384), BF),
        scratch_shapes=[pltpu.VMEM((2, 256, 384), BF)],
        name="finish",
    )(weights, back, pick, spread0, spread1, eliminated)


def on_device(
    interior_rhs,
    interface_rhs,
    interior_inverse,
    coupling,
    schur_inverse,
    weights,
    owner_sub,
    index_blocks,
):
    y, z, c = lax.axis_index("yh"), lax.axis_index("z"), lax.axis_index("c")
    swap = [(0, 1), (1, 0)]

    def low(shape):
        return lax.broadcasted_iota(jnp.int32, shape, len(shape) - 1) < HALF

    position = ((y * 8 + z) * 2 + c).astype(jnp.int32)
    eliminated, packed, _, pick = start(
        position[None], owner_sub, index_blocks, interior_inverse, interior_rhs, coupling
    )
    zero = jnp.zeros((), BF)
    packed, schur_inverse = lax.optimization_barrier((packed, schur_inverse))
    packed = packed.reshape(32, 32, 384)
    arrived = lax.all_to_all(packed, EXCHANGE, 0, 0, tiled=True).reshape(1024, 384)

    keep = lax.dynamic_index_in_dim(schur_inverse, c, 0, keepdims=False)
    give = lax.dynamic_index_in_dim(schur_inverse, 1 - c, 0, keepdims=False)
    across = lax.ppermute(give, ("yh", "c"), [(0, 3), (1, 2), (2, 1), (3, 0)])
    beyond = lax.ppermute(keep, "yh", swap)
    beside = lax.ppermute(give, "c", swap)

    owners = owner_sub.reshape(2, 8, 2).transpose(0, 2, 1).reshape(32)
    names = lax.broadcasted_iota(jnp.int32, (32, 32, 1), 1)
    idx_all = jnp.sum(jnp.where(owners[:, None, None] == names, index_blocks[None], 0), axis=1)
    rows = lax.broadcasted_iota(jnp.int32, (1, 1, 256), 2)
    rows = (rows // 128) * 1024 + z * 128 + rows % 128
    held = jnp.any(idx_all[:, :, None] == rows, axis=1)
    first = lax.broadcasted_iota(jnp.int32, (256, 256), 0)
    second = lax.broadcasted_iota(jnp.int32, (256, 256), 1)
    before = ((first < second) & (first // 64 == second // 64)).astype(BF)
    place = dot(held.astype(BF), before).astype(jnp.int32)
    place = place + 16 * ((lax.broadcasted_iota(jnp.int32, (32, 256), 1) // 64) % 2)
    place = jnp.where(held, place, -1)
    select = (
        (place[:, None, :] == lax.broadcasted_iota(jnp.int32, (32, 32, 256), 1))
        .astype(BF)
        .reshape(1024, 256)
    )

    base = [lax.dynamic_slice_in_dim(interface_rhs, q * 1024 + z * 128, 128, 0) for q in range(2)]
    low_i = low((128, 384))
    plane_rhs = jnp.where(
        y == 0,
        jnp.where(low_i, base[0], roll(base[1])),
        jnp.where(low_i, roll(base[0]), base[1]),
    )

    spread = [(weights[j] * dot(interior_inverse[j, 0], coupling[0])).astype(BF) for j in range(2)]

    schur = jnp.concatenate([keep, beside, beyond, across], axis=0)
    arrived, select, spread, plane_rhs, schur = lax.optimization_barrier(
        (arrived, select, spread, plane_rhs, schur)
    )

    summed = dot_t(select, arrived)
    summed = jnp.where(low_i, summed[:128], summed[128:])
    reduced = (plane_rhs.astype(F32) - summed).astype(BF)

    up = [(i, (i + 1) % 8) for i in range(8)]
    down = [(i, (i + 7) % 8) for i in range(8)]
    gathered = jnp.zeros((1024, 384), BF)

    def put(block, step):
        return lax.dynamic_update_slice(gathered, block, (((z + step) & 7) * 128, 0))

    gathered = put(reduced, 0)
    a = b = reduced
    for s in range(1, 4):
        a = lax.ppermute(a, "z", up)
        b = lax.ppermute(b, "z", down)
        gathered = put(a, -s)
        gathered = put(b, s)
    gathered = put(lax.ppermute(a, "z", up), 4)
    from0, from1 = dot(schur[:, :1024], gathered), dot(schur[:, 1024:], gathered)

    def half(x, q):
        x = jnp.where(y == q, x[:128], x[128:])
        return jnp.where(c == 0, x, jnp.concatenate([x[64:], x[:64]], axis=0))

    straight = jnp.where(low_i, half(from0, 0), half(from1, 1))
    crossed = jnp.where(low_i, half(from0, 1), half(from1, 0))
    solved = (straight + roll(crossed)).astype(BF)
    both = jnp.concatenate(
        [jnp.where(low_i, solved, zero), jnp.where(low_i, zero, solved)], axis=0
    )
    answers = dot(select, both).astype(BF).reshape(32, 32, 384)
    back = lax.all_to_all(answers, EXCHANGE, 0, 0, tiled=True).reshape(4, 256, 384)
    total = finish(weights, back, pick, *spread, eliminated)
    pieces = lax.all_to_all(total.reshape(8, 128, 384), SHIFT, 0, 0, tiled=True)
    return jnp.sum(pieces.reshape(8, 128, 1, 384).astype(F32), axis=0)


def solution(mesh):
    fine = Mesh(mesh.devices.reshape(2, 4, 2, 8, 2), ("yl", "x", "yh", "z", "c"))
    in_specs = (
        P(SUB, None, None),
        P(),
        P(SHIFT, SUB, None, None),
        P(SUB, None, None),
        P(SHIFT, SUB, None),
        P(SHIFT),
        P(),
        P(),
    )
    out_specs = P(SHIFT, SUB, None)
    return jax.shard_map(
        on_device, mesh=fine, in_specs=in_specs, out_specs=out_specs, check_vma=False
    )
```

time: 147 us -> 123 us (0.84)
  other arithmetic: 16.8 us -> 3.53 us
  matrix products: 21.5 us -> 8.28 us
  Pallas kernels: 0 us -> 11.3 us
  local copies, waits for them, and re-layouts: 6.88 us -> 3.25 us
  waiting for transfers between devices: 27.7 us -> 24.9 us
  between operations: 2.49 us -> 0.35 us
    ppermute x3 -> x4, waiting for transfers between devices: 16.6 us -> 4.48 us  [the longest x1 4.48 us: on_device(): gathered = put(lax.ppermute(a, 'z', up), 4)]
    all_to_all x1, waiting for transfers between devices: 0.01 us -> 11.9 us  [on_device(): lax.all_to_all(packed, EXCHANGE, 0, 0, tiled=True).reshape(1024, 384)]
    pallas_call x0 -> x2, Pallas kernels: none -> 11.3 us  [the longest x1 7.31 us: start(): pl.pallas_call(start_kernel, grid=(2, steps), in_specs=[smem, smem, pl.Bl...]
    dot_general x12 -> x6, matrix products: 19 us -> 7.81 us  [dot(): return jnp.dot(a, b, preferred_element_type=F32)]
    unnamed x8 -> x0, other arithmetic: 4.83 us -> none
    ppermute x3, waiting for transfers between devices: 5.13 us -> 0.45 us  [on_device(): b = lax.ppermute(b, 'z', down)]
    concatenate x4 -> x1, other arithmetic: 3.9 us -> 0.1 us  [on_device(): schur = jnp.concatenate([keep, beside, beyond, across], axis=0)]
    select_n x8 -> x3, other arithmetic: 2.94 us -> 0.1 us  [the longest x2 0.06 us: half(): x = jnp.where(y == q, x[:128], x[128:])]
  transfers between devices with their start and end apart: 10 -> 11, of which waited for: 6 -> 6; matrix products, arithmetic and copies ran while one was open for 25% -> 10% of each run, Pallas kernels for 0% -> 0%
where the time goes in v3:
time: 123 us
  blocking collectives  49.9 us (41%)
  waiting for transfers between devices  24.9 us (20%)
  starting transfers between devices  21.6 us (18%)
  Pallas kernels  11.3 us (9%)
  matrix products  8.28 us (7%)
  other arithmetic  3.53 us (3%)
  local copies, waits for them, and re-layouts  3.25 us (3%)
    all_to_all x1, blocking collectives, on_device(): lax.all_to_all(answers, EXCHANGE, 0, 0, tiled=True).reshape(4, 256, 384)  32 us
    all_to_all x1, blocking collectives, on_device(): pieces = lax.all_to_all(total.reshape(8, 128, 384), SHIFT, 0, 0, tiled=True)  17.8 us
    all_to_all x1, waiting for transfers between devices, on_device(): lax.all_to_all(packed, EXCHANGE, 0, 0, tiled=True).reshape(1024, 384)  11.9 us
    all_to_all x1, starting transfers between devices, on_device(): lax.all_to_all(packed, EXCHANGE, 0, 0, tiled=True).reshape(1024, 384)  11.4 us
    ppermute x3, waiting for transfers between devices, on_device(): a = lax.ppermute(a, 'z', up)  8.11 us
    dot_general x6, matrix products, dot(): return jnp.dot(a, b, preferred_element_type=F32)  7.81 us
    pallas_call x1, Pallas kernels, start(): pl.pallas_call(start_kernel, grid=(2, steps), in_specs=[smem, smem, pl.Bl...  7.31 us
    ppermute x3, starting transfers between devices, on_device(): b = lax.ppermute(b, 'z', down)  4.8 us
  transfers between devices with their start and end apart: 11, of which 6 were waited for; matrix products, arithmetic and copies ran while one was open for 10% of the time, Pallas kernels for 0%

profile of v3, /device:TPU:32, one launch (start us, length us, event | category | flops | bytes accessed | tf_op | source)
XLA Modules:
  0.0 123.1 jit_solution(320086386642553094)
XLA Ops:
  0.0 7.3 %start.1 = (bf16[2,1024,384]{2,1,0:T(8,128)(2,1)}, bf16[2,2,256,384]{3,2,1,0:T(8,128)(2,1)}, bf16[256,512]{1,0:T(8,128)(2,1)}, bf16[512,256]{1,0:T(8,128)(2,1)}) custom-call(s32[1]{0:T(128)} %bitcast.position_ref, s32[32]{0:T(128)} %owner_ref.1, s32[32,256]{1,0:T(8,128)} %blocks_ref.1, bf16[2,1,1024,1024]{3,2,1,0:T(8,128)(2,1)} %inverse_ref.1, ...), custom_call_target="tpu_custom_call" | custom-call | tf_op jit(solution)/shard_map/start/pallas_call | solution.py:86
  7.3 0.0 copy-start.5
  7.4 0.0 copy-start.1
  7.4 0.1 collective-permute-start
  7.5 3.3 %collective-permute-start.2 = (bf16[64,2048]{1,0:T(8,128)(2,1)S(1)}, bf16[64,2048]{1,0:T(8,128)(2,1)S(1)}, u32[]{:S(2)}, u32[]{:S(2)}) collective-permute-start(bf16[64,2048]{1,0:T(8,128)(2,1)S(1)} %get-tuple-element.36), channel_id=1, source_target_pairs={{0,17},{1,16},{16,1},{17,0},{2,19},{3,18},{18,3},{19,2},{4,21},{5,... | collective-permute-start | bytes 786440 | tf_op jit(solution)/shard_map/ppermute | solution.py:179
  10.8 0.3 collective-permute-start.1
  11.2 11.4 %all-to-all-start = ((bf16[32,32,384]{2,1,0:T(8,128)(2,1)}), bf16[32,32,384]{2,1,0:T(8,128)(2,1)S(1)}, u32[]{:S(2)}, u32[]{:S(2)}) async-start(bf16[32,32,384]{2,1,0:T(8,128)(2,1)} %bitcast.46), calls=%async_computation | async-start | bytes 1572864 | tf_op jit(solution)/shard_map/all_to_all | solution.py:175
  22.6 0.1 reshape.111
  22.7 0.1 copy.11
  22.7 0.1 eq.61
  22.8 0.1 iota_compare_fusion.2
  22.9 0.3 select_reduce_fusion
  23.2 0.6 fusion.62
  23.8 1.4 %compare_reduce_fusion = pred[32,256]{1,0:T(8,128)(4,1)S(1)} fusion(s32[256]{0:T(256)S(1)} %fusion.49, s32[32,256]{1,0:T(8,128)S(1)} %select_reduce_fusion), kind=kLoop, calls=%fused_computation | loop fusion | flops 4186112 | bytes 41984 | tf_op jit(solution)/shard_map/reduce_or | solution.py:188
  25.2 1.1 fusion.56
  26.3 0.3 fusion.19
  26.6 4.1 %fusion.12.spread1_ref = bf16[1024,256]{1,0:T(8,128)(2,1)} fusion(bf16[2,1,1024,1024]{3,2,1,0:T(8,128)(2,1)} %inverse_ref.1, bf16[1,1024,256]{2,1,0:T(8,128)(2,1)S(1)} %copy-done.1, f32[]{:T(128)} %bitcast.8), kind=kOutput, calls=%fused_computation.11 | convolution fusion | flops 537395200 | bytes 3146240 | tf_op jit(solution)/shard_map/dot_general | solution.py:17
  30.7 2.2 %fusion.15.spread0_ref = bf16[1024,256]{1,0:T(8,128)(2,1)} fusion(bf16[2,1,1024,1024]{3,2,1,0:T(8,128)(2,1)S(1)} %copy-done, bf16[1,1024,256]{2,1,0:T(8,128)(2,1)S(1)} %copy-done.1, f32[]{:T(128)} %bitcast.5), kind=kOutput, calls=%fused_computation.12 | convolution fusion | flops 537395200 | bytes 3145732 | tf_op jit(solution)/shard_map/dot_general | solution.py:17
  32.8 0.1 iota.108
  32.9 0.2 fusion.20
  33.1 1.1 fusion.44
  34.2 0.1 pad_maximum_fusion
  34.3 11.9 %all-to-all-done = bf16[32,32,384]{2,1,0:T(8,128)(2,1)S(1)} async-done(((bf16[32,32,384]{2,1,0:T(8,128)(2,1)}), bf16[32,32,384]{2,1,0:T(8,128)(2,1)S(1)}, u32[]{:S(2)}, u32[]{:S(2)}) %all-to-all-start) | async-done | bytes 786464 | tf_op jit(solution)/shard_map/all_to_all | solution.py:175
  46.2 0.5 fusion.63
  46.7 0.1 broadcast_in_dim.44
  46.8 0.1 constant_dynamic-update-slice_fusion.7
  46.8 0.1 collective-permute-start.3
  46.9 2.0 %collective-permute-start.4 = (bf16[128,384]{1,0:T(8,128)(2,1)S(1)}, bf16[128,384]{1,0:T(8,128)(2,1)S(1)}, u32[]{:S(2)}, u32[]{:S(2)}) collective-permute-start(bf16[128,384]{1,0:T(8,128)(2,1)S(1)} %get-tuple-element.30), channel_id=1, source_target_pairs={{0,14},{2,0},{4,2},{6,4},{8,6},{10,8},{12,10},{14,12},{1,15},{3,1}... | collective-permute-start | bytes 294920 | tf_op jit(solution)/shard_map/ppermute | solution.py:231
  48.9 3.0 %collective-permute-done.3 = bf16[128,384]{1,0:T(8,128)(2,1)S(1)} collective-permute-done((bf16[128,384]{1,0:T(8,128)(2,1)S(1)}, bf16[128,384]{1,0:T(8,128)(2,1)S(1)}, u32[]{:S(2)}, u32[]{:S(2)}) %collective-permute-start.3) | collective-permute-done | bytes 98336 | tf_op jit(solution)/shard_map/ppermute | solution.py:230
  52.0 0.0 collective-permute-start.5
  52.0 0.4 collective-permute-done.4
  52.4 1.6 %collective-permute-start.6 = (bf16[128,384]{1,0:T(8,128)(2,1)S(1)}, bf16[128,384]{1,0:T(8,128)(2,1)S(1)}, u32[]{:S(2)}, u32[]{:S(2)}) collective-permute-start(bf16[128,384]{1,0:T(8,128)(2,1)S(1)} %collective-permute-done.4), channel_id=1, source_target_pairs={{0,14},{2,0},{4,2},{6,4},{8,6},{10,8},{12,10},{14,12},{1,15},{3,1}... | collective-permute-start | bytes 294920 | tf_op jit(solution)/shard_map/ppermute | solution.py:231
  54.1 2.5 %collective-permute-done.5 = bf16[128,384]{1,0:T(8,128)(2,1)S(1)} collective-permute-done((bf16[128,384]{1,0:T(8,128)(2,1)S(1)}, bf16[128,384]{1,0:T(8,128)(2,1)S(1)}, u32[]{:S(2)}, u32[]{:S(2)}) %collective-permute-start.5) | collective-permute-done | bytes 98336 | tf_op jit(solution)/shard_map/ppermute | solution.py:230
  56.6 0.8 collective-permute-start.7
  57.4 1.2 collective-permute-start.8
  58.7 2.5 %collective-permute-done.7 = bf16[128,384]{1,0:T(8,128)(2,1)S(1)} collective-permute-done((bf16[128,384]{1,0:T(8,128)(2,1)S(1)}, bf16[128,384]{1,0:T(8,128)(2,1)S(1)}, u32[]{:S(2)}, u32[]{:S(2)}) %collective-permute-start.7) | collective-permute-done | bytes 98336 | tf_op jit(solution)/shard_map/ppermute | solution.py:230
  61.2 0.8 collective-permute-start.9
  62.1 4.5 %collective-permute-done.9 = bf16[128,384]{1,0:T(8,128)(2,1)S(1)} collective-permute-done((bf16[128,384]{1,0:T(8,128)(2,1)S(1)}, bf16[128,384]{1,0:T(8,128)(2,1)S(1)}, u32[]{:S(2)}, u32[]{:S(2)}) %collective-permute-start.9) | collective-permute-done | bytes 98336 | tf_op jit(solution)/shard_map/ppermute | solution.py:234
  66.6 0.4 fusion.23
  67.0 0.4 fusion.25
  67.6 0.1 fusion.59
  67.8 0.1 broadcast_select_fusion
  67.9 0.4 convolution_convert_fusion
  68.3 32.0 %all_to_all.15 = bf16[32,32,384]{2,1,0:T(8,128)(2,1)} all-to-all(bf16[32,32,384]{2,1,0:T(8,128)(2,1)S(1)} %bitcast.44), channel_id=1, replica_groups=mesh['yl'=2,'x'=4,'yh'=2,'z'=8,'c'=2] {'yh','c','z'}, dimensions={0} | all-to-all | bytes 1572864 | tf_op jit(solution)/shard_map/all_to_all | solution.py:248
  100.4 4.0 %finish.1 = bf16[1024,384]{1,0:T(8,128)(2,1)} custom-call(f32[2]{0:T(128)} %weights_ref.1, bf16[4,256,384]{2,1,0:T(8,128)(2,1)} %bitcast.42, bf16[512,256]{1,0:T(8,128)(2,1)} %get-tuple-element.23.pick_ref, bf16[1024,256]{1,0:T(8,128)(2,1)} %fusion.15.spread0_ref, bf16[1024,256]{1,0:T(8,128)(2,1)} %fusion.12.spread1_ref, ...), custom_call_target="tpu_custom_call" | custom-call | tf_op jit(solution)/shard_map/finish/pallas_call | solution.py:134
  104.4 17.8 %all_to_all.16 = bf16[8,128,384]{2,1,0:T(8,128)(2,1)S(1)} all-to-all(bf16[8,128,384]{2,1,0:T(8,128)(2,1)} %bitcast.43), channel_id=1, replica_groups=mesh['yl'=2,'x'=4,'yh'=2,'z'=8,'c'=2] {'yl','x'}, dimensions={0} | all-to-all | bytes 1572864 | tf_op jit(solution)/shard_map/all_to_all | solution.py:250
  122.2 0.1 convert_reduce_fusion
  122.3 0.8 reduce_sum.22
  (36 shorter events, 0.4 us)
Async XLA Ops:
  0.0 7.4 %copy-start.2 = (bf16[2,64,2048]{2,1,0:T(8,128)(2,1)S(1)}, bf16[2,64,2048]{2,1,0:T(8,128)(2,1)}, u32[]{:S(2)}) copy-start(bf16[2,64,2048]{2,1,0:T(8,128)(2,1)} %param.12) | copy-start | bytes 1572868
  7.3 15.2 %copy-start.5 = (s32[32]{0:T(128)S(1)}, s32[32]{0:T(128)}, u32[]{:S(2)}) copy-start(s32[32]{0:T(128)} %owner_ref.1) | copy-start | bytes 388
  7.3 15.6 %copy-start.3 = (s32[32,256]{1,0:T(8,128)S(1)}, s32[32,256]{1,0:T(8,128)}, u32[]{:S(2)}) copy-start(s32[32,256]{1,0:T(8,128)} %blocks_ref.1) | copy-start | bytes 98308
  7.3 15.8 %copy-start.4 = (f32[2]{0:T(128)S(1)}, f32[2]{0:T(128)}, u32[]{:S(2)}) copy-start(f32[2]{0:T(128)} %weights_ref.1) | copy-start | bytes 28
  7.4 19.2 %copy-start.1 = (bf16[1,1024,256]{2,1,0:T(8,128)(2,1)S(1)}, bf16[1,1024,256]{2,1,0:T(8,128)(2,1)}, u32[]{:S(2)}) copy-start(bf16[1,1024,256]{2,1,0:T(8,128)(2,1)} %couple_ref.1) | copy-start | bytes 1572868
  7.4 26.8 %collective-permute-start = (bf16[64,2048]{1,0:T(8,128)(2,1)S(1)}, bf16[64,2048]{1,0:T(8,128)(2,1)S(1)}, u32[]{:S(2)}, u32[]{:S(2)}) collective-permute-start(bf16[64,2048]{1,0:T(8,128)(2,1)S(1)} %get-tuple-element.36), channel_id=1, source_target_pairs={{0,1},{1,0},{2,3},{3,2},{4,5},{5,4},{6,7},{7,6},{8,9},{9,8},{10,11... | collective-permute-start | bytes 786440 | tf_op jit(solution)/shard_map/ppermute | solution.py:181
  7.5 26.7 %collective-permute-start.2 = (bf16[64,2048]{1,0:T(8,128)(2,1)S(1)}, bf16[64,2048]{1,0:T(8,128)(2,1)S(1)}, u32[]{:S(2)}, u32[]{:S(2)}) collective-permute-start(bf16[64,2048]{1,0:T(8,128)(2,1)S(1)} %get-tuple-element.36), channel_id=1, source_target_pairs={{0,17},{1,16},{16,1},{17,0},{2,19},{3,18},{18,3},{19,2},{4,21},{5,... | collective-permute-start | bytes 786440 | tf_op jit(solution)/shard_map/ppermute | solution.py:179
  10.8 23.4 %collective-permute-start.1 = (bf16[64,2048]{1,0:T(8,128)(2,1)S(1)}, bf16[64,2048]{1,0:T(8,128)(2,1)S(1)}, u32[]{:S(2)}, u32[]{:S(2)}) collective-permute-start(bf16[64,2048]{1,0:T(8,128)(2,1)S(1)} %get-tuple-element.35), channel_id=1, source_target_pairs={{0,16},{16,0},{1,17},{17,1},{2,18},{18,2},{3,19},{19,3},{4,20},{20... | collective-permute-start | bytes 786440 | tf_op jit(solution)/shard_map/ppermute | solution.py:180
  11.2 35.1 %all-to-all-start = ((bf16[32,32,384]{2,1,0:T(8,128)(2,1)}), bf16[32,32,384]{2,1,0:T(8,128)(2,1)S(1)}, u32[]{:S(2)}, u32[]{:S(2)}) async-start(bf16[32,32,384]{2,1,0:T(8,128)(2,1)} %bitcast.46), calls=%async_computation | async-start | bytes 1572864 | tf_op jit(solution)/shard_map/all_to_all | solution.py:175
  26.6 4.1 %copy-start = (bf16[2,1,1024,1024]{3,2,1,0:T(8,128)(2,1)S(1)}, bf16[2,1,1024,1024]{3,2,1,0:T(8,128)(2,1)}, u32[]{:S(2)}) copy-start(bf16[2,1,1024,1024]{3,2,1,0:T(8,128)(2,1)} %inverse_ref.1) | copy-start | bytes 12582916
  46.8 5.1 %collective-permute-start.3 = (bf16[128,384]{1,0:T(8,128)(2,1)S(1)}, bf16[128,384]{1,0:T(8,128)(2,1)S(1)}, u32[]{:S(2)}, u32[]{:S(2)}) collective-permute-start(bf16[128,384]{1,0:T(8,128)(2,1)S(1)} %get-tuple-element.30), channel_id=1, source_target_pairs={{0,2},{2,4},{4,6},{6,8},{8,10},{10,12},{12,14},{14,0},{1,3},{3,5},... | collective-permute-start | bytes 294920 | tf_op jit(solution)/shard_map/ppermute | solution.py:230
  46.9 5.5 %collective-permute-start.4 = (bf16[128,384]{1,0:T(8,128)(2,1)S(1)}, bf16[128,384]{1,0:T(8,128)(2,1)S(1)}, u32[]{:S(2)}, u32[]{:S(2)}) collective-permute-start(bf16[128,384]{1,0:T(8,128)(2,1)S(1)} %get-tuple-element.30), channel_id=1, source_target_pairs={{0,14},{2,0},{4,2},{6,4},{8,6},{10,8},{12,10},{14,12},{1,15},{3,1}... | collective-permute-start | bytes 294920 | tf_op jit(solution)/shard_map/ppermute | solution.py:231
  52.0 4.6 %collective-permute-start.5 = (bf16[128,384]{1,0:T(8,128)(2,1)S(1)}, bf16[128,384]{1,0:T(8,128)(2,1)S(1)}, u32[]{:S(2)}, u32[]{:S(2)}) collective-permute-start(bf16[128,384]{1,0:T(8,128)(2,1)S(1)} %collective-permute-done.3), channel_id=1, source_target_pairs={{0,2},{2,4},{4,6},{6,8},{8,10},{10,12},{12,14},{14,0},{1,3},{3,5},... | collective-permute-start | bytes 294920 | tf_op jit(solution)/shard_map/ppermute | solution.py:230
  52.4 5.0 %collective-permute-start.6 = (bf16[128,384]{1,0:T(8,128)(2,1)S(1)}, bf16[128,384]{1,0:T(8,128)(2,1)S(1)}, u32[]{:S(2)}, u32[]{:S(2)}) collective-permute-start(bf16[128,384]{1,0:T(8,128)(2,1)S(1)} %collective-permute-done.4), channel_id=1, source_target_pairs={{0,14},{2,0},{4,2},{6,4},{8,6},{10,8},{12,10},{14,12},{1,15},{3,1}... | collective-permute-start | bytes 294920 | tf_op jit(solution)/shard_map/ppermute | solution.py:231
  56.6 4.6 %collective-permute-start.7 = (bf16[128,384]{1,0:T(8,128)(2,1)S(1)}, bf16[128,384]{1,0:T(8,128)(2,1)S(1)}, u32[]{:S(2)}, u32[]{:S(2)}) collective-permute-start(bf16[128,384]{1,0:T(8,128)(2,1)S(1)} %collective-permute-done.5), channel_id=1, source_target_pairs={{0,2},{2,4},{4,6},{6,8},{8,10},{10,12},{12,14},{14,0},{1,3},{3,5},... | collective-permute-start | bytes 294920 | tf_op jit(solution)/shard_map/ppermute | solution.py:230
  57.4 4.6 %collective-permute-start.8 = (bf16[128,384]{1,0:T(8,128)(2,1)S(1)}, bf16[128,384]{1,0:T(8,128)(2,1)S(1)}, u32[]{:S(2)}, u32[]{:S(2)}) collective-permute-start(bf16[128,384]{1,0:T(8,128)(2,1)S(1)} %collective-permute-done.6), channel_id=1, source_target_pairs={{0,14},{2,0},{4,2},{6,4},{8,6},{10,8},{12,10},{14,12},{1,15},{3,1}... | collective-permute-start | bytes 294920 | tf_op jit(solution)/shard_map/ppermute | solution.py:231
  61.2 5.3 %collective-permute-start.9 = (bf16[128,384]{1,0:T(8,128)(2,1)S(1)}, bf16[128,384]{1,0:T(8,128)(2,1)S(1)}, u32[]{:S(2)}, u32[]{:S(2)}) collective-permute-start(bf16[128,384]{1,0:T(8,128)(2,1)S(1)} %collective-permute-done.7), channel_id=1, source_target_pairs={{0,2},{2,4},{4,6},{6,8},{8,10},{10,12},{12,14},{14,0},{1,3},{3,5},... | collective-permute-start | bytes 294920 | tf_op jit(solution)/shard_map/ppermute | solution.py:234

commit v4 on v3

--- a/solution.py
+++ b/solution.py
@@ -208,9 +208,8 @@
 
     spread = [(weights[j] * dot(interior_inverse[j, 0], coupling[0])).astype(BF) for j in range(2)]
 
-    schur = jnp.concatenate([keep, beside, beyond, across], axis=0)
-    arrived, select, spread, plane_rhs, schur = lax.optimization_barrier(
-        (arrived, select, spread, plane_rhs, schur)
+    arrived, select, spread, plane_rhs = lax.optimization_barrier(
+        (arrived, select, spread, plane_rhs)
     )
 
     summed = dot_t(select, arrived)
@@ -224,14 +223,31 @@
     def put(block, step):
         return lax.dynamic_update_slice(gathered, block, (((z + step) & 7) * 128, 0))
 
-    gathered = put(reduced, 0)
-    a = b = reduced
-    for s in range(1, 4):
-        a = lax.ppermute(a, "z", up)
-        b = lax.ppermute(b, "z", down)
-        gathered = put(a, -s)
-        gathered = put(b, s)
-    gathered = put(lax.ppermute(a, "z", up), 4)
+    up2 = [(i, (i + 2) % 8) for i in range(8)]
+    down2 = [(i, (i + 6) % 8) for i in range(8)]
+    below1, above1 = lax.ppermute(reduced, "z", up), lax.ppermute(reduced, "z", down)
+    below2, above2 = lax.ppermute(reduced, "z", up2), lax.ppermute(reduced, "z", down2)
+    below1, keep, beside, beyond, across = lax.optimization_barrier(
+        (below1, keep, beside, beyond, across)
+    )
+    schur = jnp.concatenate([keep, beside, beyond, across], axis=0)
+    below1, keep, beside, beyond, across = lax.optimization_barrier(
+        (below1, keep, beside, beyond, across)
+    )
+    schur = jnp.concatenate([keep, beside, beyond, across], axis=0)
+    below3, above3 = lax.ppermute(below2, "z", up), lax.ppermute(above2, "z", down)
+    opposite = lax.ppermute(below2, "z", up2)
+    for step, block in (
+        (0, reduced),
+        (-1, below1),
+        (1, above1),
+        (-2, below2),
+        (2, above2),
+        (-3, below3),
+        (3, above3),
+        (4, opposite),
+    ):
+        gathered = put(block, step)
     from0, from1 = dot(schur[:, :1024], gathered), dot(schur[:, 1024:], gathered)
 
     def half(x, q):
@@ -264,6 +280,7 @@
         P(),
     )
     out_specs = P(SHIFT, SUB, None)
+
     return jax.shard_map(
         on_device, mesh=fine, in_specs=in_specs, out_specs=out_specs, check_vma=False
     )

time: 123 us -> 117 us (0.951)
  waiting for transfers between devices: 24.9 us -> 18.3 us
  starting transfers between devices: 21.6 us -> 24.2 us
  blocking collectives: 49.9 us -> 47.7 us
    ppermute x7, waiting for transfers between devices: 13 us -> 9.28 us  [the longest x1 4.48 us: on_device(): lax.ppermute(below2, 'z', up)]
    all_to_all x1, waiting for transfers between devices: 11.9 us -> 8.97 us  [on_device(): lax.all_to_all(packed, EXCHANGE, 0, 0, tiled=True).reshape(1024, 384)]
    all_to_all x1, blocking collectives: 32 us -> 29.2 us  [on_device(): lax.all_to_all(answers, EXCHANGE, 0, 0, tiled=True).reshape(4, 256, 384)]
    ppermute x1, starting transfers between devices: 0.33 us -> 3.06 us  [on_device(): beyond = lax.ppermute(keep, 'yh', swap)]
    all_to_all x1, starting transfers between devices: 11.4 us -> 8.73 us  [on_device(): lax.all_to_all(packed, EXCHANGE, 0, 0, tiled=True).reshape(1024, 384)]
    ppermute x7, starting transfers between devices: 6.51 us -> 8.97 us  [the longest x1 2.7 us: on_device(): lax.ppermute(reduced, 'z', down2)]
  transfers between devices with their start and end apart: 11 -> 11, of which waited for: 6 -> 4; matrix products, arithmetic and copies ran while one was open for 10% -> 11% of each run, Pallas kernels for 0% -> 0%
where the time goes in v4:
time: 117 us
  blocking collectives  47.7 us (41%)
  starting transfers between devices  24.2 us (21%)
  waiting for transfers between devices  18.3 us (16%)
  Pallas kernels  11.3 us (10%)
  matrix products  8.31 us (7%)
  other arithmetic  3.44 us (3%)
  local copies, waits for them, and re-layouts  3.31 us (3%)
    all_to_all x1, blocking collectives, on_device(): lax.all_to_all(answers, EXCHANGE, 0, 0, tiled=True).reshape(4, 256, 384)  29.2 us
    all_to_all x1, blocking collectives, on_device(): pieces = lax.all_to_all(total.reshape(8, 128, 384), SHIFT, 0, 0, tiled=True)  18.5 us
    all_to_all x1, waiting for transfers between devices, on_device(): lax.all_to_all(packed, EXCHANGE, 0, 0, tiled=True).reshape(1024, 384)  8.97 us
    all_to_all x1, starting transfers between devices, on_device(): lax.all_to_all(packed, EXCHANGE, 0, 0, tiled=True).reshape(1024, 384)  8.73 us
    dot_general x6, matrix products, dot(): return jnp.dot(a, b, preferred_element_type=F32)  7.85 us
    pallas_call x1, Pallas kernels, start(): pl.pallas_call(start_kernel, grid=(2, steps), in_specs=[smem, smem, pl.Bl...  7.31 us
    ppermute x1, waiting for transfers between devices, on_device(): lax.ppermute(below2, 'z', up)  4.48 us
    pallas_call x1, Pallas kernels, finish(): pl.pallas_call(finish_kernel, grid=(1024 // rows,), in_specs=[pl.BlockSpe...  3.97 us
  transfers between devices with their start and end apart: 11, of which 4 were waited for; matrix products, arithmetic and copies ran while one was open for 11% of the time, Pallas kernels for 0%

profile of v4, /device:TPU:32, one launch (start us, length us, event | category | flops | bytes accessed | tf_op | source)
XLA Modules:
  0.0 116.8 jit_solution(11839866112594225274)
XLA Ops:
  0.0 7.3 %start.1 = (bf16[2,1024,384]{2,1,0:T(8,128)(2,1)}, bf16[2,2,256,384]{3,2,1,0:T(8,128)(2,1)}, bf16[256,512]{1,0:T(8,128)(2,1)}, bf16[512,256]{1,0:T(8,128)(2,1)}) custom-call(s32[1]{0:T(128)} %bitcast.position_ref, s32[32]{0:T(128)} %owner_ref.1, s32[32,256]{1,0:T(8,128)} %blocks_ref.1, bf16[2,1,1024,1024]{3,2,1,0:T(8,128)(2,1)} %inverse_ref.1, ...), custom_call_target="tpu_custom_call" | custom-call | tf_op jit(solution)/shard_map/start/pallas_call | solution.py:86
  7.3 0.0 copy-start.5
  7.3 0.0 copy-start.3
  7.3 0.0 copy-start.4
  7.4 0.0 copy-start.1
  7.4 2.7 %collective-permute-start.3 = (bf16[64,2048]{1,0:T(8,128)(2,1)S(1)}, bf16[64,2048]{1,0:T(8,128)(2,1)S(1)}, u32[]{:S(2)}, u32[]{:S(2)}) collective-permute-start(bf16[64,2048]{1,0:T(8,128)(2,1)S(1)} %get-tuple-element.43), channel_id=1, source_target_pairs={{0,17},{1,16},{16,1},{17,0},{2,19},{3,18},{18,3},{19,2},{4,21},{5,... | collective-permute-start | bytes 786440 | tf_op jit(solution)/shard_map/ppermute | solution.py:179
  10.2 0.7 collective-permute-start.1
  10.8 8.7 %all-to-all-start = ((bf16[32,32,384]{2,1,0:T(8,128)(2,1)}), bf16[32,32,384]{2,1,0:T(8,128)(2,1)S(1)}, u32[]{:S(2)}, u32[]{:S(2)}) async-start(bf16[32,32,384]{2,1,0:T(8,128)(2,1)} %bitcast.46), calls=%async_computation | async-start | bytes 1572864 | tf_op jit(solution)/shard_map/all_to_all | solution.py:175
  19.6 3.1 %collective-permute-start.2 = (bf16[64,2048]{1,0:T(8,128)(2,1)S(1)}, bf16[64,2048]{1,0:T(8,128)(2,1)S(1)}, u32[]{:S(2)}, u32[]{:S(2)}) collective-permute-start(bf16[64,2048]{1,0:T(8,128)(2,1)S(1)} %get-tuple-element.26), channel_id=1, source_target_pairs={{0,16},{16,0},{1,17},{17,1},{2,18},{18,2},{3,19},{19,3},{4,20},{20... | collective-permute-start | bytes 786440 | tf_op jit(solution)/shard_map/ppermute | solution.py:180
  22.6 0.1 reshape.111
  22.7 0.1 copy.11
  22.8 0.1 eq.61
  22.9 0.1 iota_compare_fusion.2
  23.0 0.3 select_reduce_fusion
  23.3 1.4 %compare_reduce_fusion = pred[32,256]{1,0:T(8,128)(4,1)S(1)} fusion(s32[256]{0:T(256)S(1)} %fusion.49, s32[32,256]{1,0:T(8,128)S(1)} %select_reduce_fusion), kind=kLoop, calls=%fused_computation | loop fusion | flops 4186112 | bytes 41984 | tf_op jit(solution)/shard_map/reduce_or | solution.py:188
  24.7 0.1 iota.108
  24.8 0.3 fusion.19
  25.1 0.2 fusion.20
  25.3 0.6 fusion.62
  25.9 1.1 fusion.56
  27.0 1.1 fusion.44
  28.0 0.0 copy-start
  28.1 4.1 %fusion.12.spread1_ref = bf16[1024,256]{1,0:T(8,128)(2,1)} fusion(bf16[2,1,1024,1024]{3,2,1,0:T(8,128)(2,1)} %inverse_ref.1, bf16[1,1024,256]{2,1,0:T(8,128)(2,1)S(1)} %copy-done.1, f32[]{:T(128)} %bitcast.8), kind=kOutput, calls=%fused_computation.11 | convolution fusion | flops 537395200 | bytes 3146240 | tf_op jit(solution)/shard_map/dot_general | solution.py:17
  32.1 2.2 %fusion.15.spread0_ref = bf16[1024,256]{1,0:T(8,128)(2,1)} fusion(bf16[2,1,1024,1024]{3,2,1,0:T(8,128)(2,1)S(1)} %copy-done, bf16[1,1024,256]{2,1,0:T(8,128)(2,1)S(1)} %copy-done.1, f32[]{:T(128)} %bitcast.5), kind=kOutput, calls=%fused_computation.12 | convolution fusion | flops 537395200 | bytes 3145732 | tf_op jit(solution)/shard_map/dot_general | solution.py:17
  34.3 9.0 %all-to-all-done = bf16[32,32,384]{2,1,0:T(8,128)(2,1)S(1)} async-done(((bf16[32,32,384]{2,1,0:T(8,128)(2,1)}), bf16[32,32,384]{2,1,0:T(8,128)(2,1)S(1)}, u32[]{:S(2)}, u32[]{:S(2)}) %all-to-all-start) | async-done | bytes 786464 | tf_op jit(solution)/shard_map/all_to_all | solution.py:175
  43.3 0.5 fusion.63
  43.7 0.1 broadcast_in_dim.44
  43.8 0.1 constant_dynamic-update-slice_fusion.11
  43.9 0.1 collective-permute-start
  44.0 1.5 %collective-permute-start.5 = (bf16[128,384]{1,0:T(8,128)(2,1)S(1)}, bf16[128,384]{1,0:T(8,128)(2,1)S(1)}, u32[]{:S(2)}, u32[]{:S(2)}) collective-permute-start(bf16[128,384]{1,0:T(8,128)(2,1)S(1)} %get-tuple-element.38), channel_id=1, source_target_pairs={{0,4},{2,6},{4,8},{6,10},{8,12},{10,14},{12,0},{14,2},{1,5},{3,7},... | collective-permute-start | bytes 294920 | tf_op jit(solution)/shard_map/ppermute | solution.py:229
  45.5 1.9 %collective-permute-start.4 = (bf16[128,384]{1,0:T(8,128)(2,1)S(1)}, bf16[128,384]{1,0:T(8,128)(2,1)S(1)}, u32[]{:S(2)}, u32[]{:S(2)}) collective-permute-start(bf16[128,384]{1,0:T(8,128)(2,1)S(1)} %get-tuple-element.38), channel_id=1, source_target_pairs={{0,14},{2,0},{4,2},{6,4},{8,6},{10,8},{12,10},{14,12},{1,15},{3,1}... | collective-permute-start | bytes 294920 | tf_op jit(solution)/shard_map/ppermute | solution.py:228
  47.4 2.7 %collective-permute-start.6 = (bf16[128,384]{1,0:T(8,128)(2,1)S(1)}, bf16[128,384]{1,0:T(8,128)(2,1)S(1)}, u32[]{:S(2)}, u32[]{:S(2)}) collective-permute-start(bf16[128,384]{1,0:T(8,128)(2,1)S(1)} %get-tuple-element.38), channel_id=1, source_target_pairs={{0,12},{2,14},{4,0},{6,2},{8,4},{10,6},{12,8},{14,10},{1,13},{3,15... | collective-permute-start | bytes 294920 | tf_op jit(solution)/shard_map/ppermute | solution.py:229
  50.2 3.5 %collective-permute-done.5 = bf16[128,384]{1,0:T(8,128)(2,1)S(1)} collective-permute-done((bf16[128,384]{1,0:T(8,128)(2,1)S(1)}, bf16[128,384]{1,0:T(8,128)(2,1)S(1)}, u32[]{:S(2)}, u32[]{:S(2)}) %collective-permute-start.5) | collective-permute-done | bytes 98336 | tf_op jit(solution)/shard_map/ppermute | solution.py:229
  53.7 0.4 collective-permute-start.9
  54.1 2.3 %collective-permute-start.7 = (bf16[128,384]{1,0:T(8,128)(2,1)S(1)}, bf16[128,384]{1,0:T(8,128)(2,1)S(1)}, u32[]{:S(2)}, u32[]{:S(2)}) collective-permute-start(bf16[128,384]{1,0:T(8,128)(2,1)S(1)} %collective-permute-done.5), channel_id=1, source_target_pairs={{0,2},{2,4},{4,6},{6,8},{8,10},{10,12},{12,14},{14,0},{1,3},{3,5},... | collective-permute-start | bytes 294920 | tf_op jit(solution)/shard_map/ppermute | solution.py:238
  56.5 0.0 collective-permute-start.8
  56.6 4.5 %collective-permute-done.7 = bf16[128,384]{1,0:T(8,128)(2,1)S(1)} collective-permute-done((bf16[128,384]{1,0:T(8,128)(2,1)S(1)}, bf16[128,384]{1,0:T(8,128)(2,1)S(1)}, u32[]{:S(2)}, u32[]{:S(2)}) %collective-permute-start.7) | collective-permute-done | bytes 98336 | tf_op jit(solution)/shard_map/ppermute | solution.py:238
  61.2 1.3 %collective-permute-done.9 = bf16[128,384]{1,0:T(8,128)(2,1)S(1)} collective-permute-done((bf16[128,384]{1,0:T(8,128)(2,1)S(1)}, bf16[128,384]{1,0:T(8,128)(2,1)S(1)}, u32[]{:S(2)}, u32[]{:S(2)}) %collective-permute-start.9) | collective-permute-done | bytes 98336 | tf_op jit(solution)/shard_map/ppermute | solution.py:239
  62.5 0.4 fusion.21
  62.9 0.4 fusion.23
  63.6 0.1 fusion.59
  63.7 0.1 broadcast_select_fusion
  63.8 0.4 convolution_convert_fusion
  64.2 29.2 %all_to_all.15 = bf16[32,32,384]{2,1,0:T(8,128)(2,1)} all-to-all(bf16[32,32,384]{2,1,0:T(8,128)(2,1)S(1)} %bitcast.44), channel_id=1, replica_groups=mesh['yl'=2,'x'=4,'yh'=2,'z'=8,'c'=2] {'yh','c','z'}, dimensions={0} | all-to-all | bytes 1572864 | tf_op jit(solution)/shard_map/all_to_all | solution.py:264
  93.4 4.0 %finish.1 = bf16[1024,384]{1,0:T(8,128)(2,1)} custom-call(f32[2]{0:T(128)} %weights_ref.1, bf16[4,256,384]{2,1,0:T(8,128)(2,1)} %bitcast.42, bf16[512,256]{1,0:T(8,128)(2,1)} %get-tuple-element.31.pick_ref, bf16[1024,256]{1,0:T(8,128)(2,1)} %fusion.15.spread0_ref, bf16[1024,256]{1,0:T(8,128)(2,1)} %fusion.12.spread1_ref, ...), custom_call_target="tpu_custom_call" | custom-call | tf_op jit(solution)/shard_map/finish/pallas_call | solution.py:134
  97.4 18.5 %all_to_all.16 = bf16[8,128,384]{2,1,0:T(8,128)(2,1)S(1)} all-to-all(bf16[8,128,384]{2,1,0:T(8,128)(2,1)} %bitcast.43), channel_id=1, replica_groups=mesh['yl'=2,'x'=4,'yh'=2,'z'=8,'c'=2] {'yl','x'}, dimensions={0} | all-to-all | bytes 1572864 | tf_op jit(solution)/shard_map/all_to_all | solution.py:266
  115.9 0.1 convert_reduce_fusion
  116.0 0.8 reduce_sum.22
  (39 shorter events, 0.5 us)
Async XLA Ops:
  0.0 7.4 %copy-start.2 = (bf16[2,64,2048]{2,1,0:T(8,128)(2,1)S(1)}, bf16[2,64,2048]{2,1,0:T(8,128)(2,1)}, u32[]{:S(2)}) copy-start(bf16[2,64,2048]{2,1,0:T(8,128)(2,1)} %param.12) | copy-start | bytes 1572868
  7.3 15.3 %copy-start.5 = (s32[32]{0:T(128)S(1)}, s32[32]{0:T(128)}, u32[]{:S(2)}) copy-start(s32[32]{0:T(128)} %owner_ref.1) | copy-start | bytes 388
  7.3 15.7 %copy-start.3 = (s32[32,256]{1,0:T(8,128)S(1)}, s32[32,256]{1,0:T(8,128)}, u32[]{:S(2)}) copy-start(s32[32,256]{1,0:T(8,128)} %blocks_ref.1) | copy-start | bytes 98308
  7.3 18.0 %copy-start.4 = (f32[2]{0:T(128)S(1)}, f32[2]{0:T(128)}, u32[]{:S(2)}) copy-start(f32[2]{0:T(128)} %weights_ref.1) | copy-start | bytes 28
  7.4 20.6 %copy-start.1 = (bf16[1,1024,256]{2,1,0:T(8,128)(2,1)S(1)}, bf16[1,1024,256]{2,1,0:T(8,128)(2,1)}, u32[]{:S(2)}) copy-start(bf16[1,1024,256]{2,1,0:T(8,128)(2,1)} %couple_ref.1) | copy-start | bytes 1572868
  7.4 38.1 %collective-permute-start.3 = (bf16[64,2048]{1,0:T(8,128)(2,1)S(1)}, bf16[64,2048]{1,0:T(8,128)(2,1)S(1)}, u32[]{:S(2)}, u32[]{:S(2)}) collective-permute-start(bf16[64,2048]{1,0:T(8,128)(2,1)S(1)} %get-tuple-element.43), channel_id=1, source_target_pairs={{0,17},{1,16},{16,1},{17,0},{2,19},{3,18},{18,3},{19,2},{4,21},{5,... | collective-permute-start | bytes 786440 | tf_op jit(solution)/shard_map/ppermute | solution.py:179
  10.2 37.2 %collective-permute-start.1 = (bf16[64,2048]{1,0:T(8,128)(2,1)S(1)}, bf16[64,2048]{1,0:T(8,128)(2,1)S(1)}, u32[]{:S(2)}, u32[]{:S(2)}) collective-permute-start(bf16[64,2048]{1,0:T(8,128)(2,1)S(1)} %get-tuple-element.43), channel_id=1, source_target_pairs={{0,1},{1,0},{2,3},{3,2},{4,5},{5,4},{6,7},{7,6},{8,9},{9,8},{10,11... | collective-permute-start | bytes 786440 | tf_op jit(solution)/shard_map/ppermute | solution.py:181
  10.8 32.4 %all-to-all-start = ((bf16[32,32,384]{2,1,0:T(8,128)(2,1)}), bf16[32,32,384]{2,1,0:T(8,128)(2,1)S(1)}, u32[]{:S(2)}, u32[]{:S(2)}) async-start(bf16[32,32,384]{2,1,0:T(8,128)(2,1)} %bitcast.46), calls=%async_computation | async-start | bytes 1572864 | tf_op jit(solution)/shard_map/all_to_all | solution.py:175
  19.6 30.5 %collective-permute-start.2 = (bf16[64,2048]{1,0:T(8,128)(2,1)S(1)}, bf16[64,2048]{1,0:T(8,128)(2,1)S(1)}, u32[]{:S(2)}, u32[]{:S(2)}) collective-permute-start(bf16[64,2048]{1,0:T(8,128)(2,1)S(1)} %get-tuple-element.26), channel_id=1, source_target_pairs={{0,16},{16,0},{1,17},{17,1},{2,18},{18,2},{3,19},{19,3},{4,20},{20... | collective-permute-start | bytes 786440 | tf_op jit(solution)/shard_map/ppermute | solution.py:180
  28.0 4.1 %copy-start = (bf16[2,1,1024,1024]{3,2,1,0:T(8,128)(2,1)S(1)}, bf16[2,1,1024,1024]{3,2,1,0:T(8,128)(2,1)}, u32[]{:S(2)}) copy-start(bf16[2,1,1024,1024]{3,2,1,0:T(8,128)(2,1)} %inverse_ref.1) | copy-start | bytes 12582916
  43.9 6.3 %collective-permute-start = (bf16[128,384]{1,0:T(8,128)(2,1)S(1)}, bf16[128,384]{1,0:T(8,128)(2,1)S(1)}, u32[]{:S(2)}, u32[]{:S(2)}) collective-permute-start(bf16[128,384]{1,0:T(8,128)(2,1)S(1)} %get-tuple-element.38), channel_id=1, source_target_pairs={{0,2},{2,4},{4,6},{6,8},{8,10},{10,12},{12,14},{14,0},{1,3},{3,5},... | collective-permute-start | bytes 294920 | tf_op jit(solution)/shard_map/ppermute | solution.py:228
  44.0 9.8 %collective-permute-start.5 = (bf16[128,384]{1,0:T(8,128)(2,1)S(1)}, bf16[128,384]{1,0:T(8,128)(2,1)S(1)}, u32[]{:S(2)}, u32[]{:S(2)}) collective-permute-start(bf16[128,384]{1,0:T(8,128)(2,1)S(1)} %get-tuple-element.38), channel_id=1, source_target_pairs={{0,4},{2,6},{4,8},{6,10},{8,12},{10,14},{12,0},{14,2},{1,5},{3,7},... | collective-permute-start | bytes 294920 | tf_op jit(solution)/shard_map/ppermute | solution.py:229
  45.5 11.0 %collective-permute-start.4 = (bf16[128,384]{1,0:T(8,128)(2,1)S(1)}, bf16[128,384]{1,0:T(8,128)(2,1)S(1)}, u32[]{:S(2)}, u32[]{:S(2)}) collective-permute-start(bf16[128,384]{1,0:T(8,128)(2,1)S(1)} %get-tuple-element.38), channel_id=1, source_target_pairs={{0,14},{2,0},{4,2},{6,4},{8,6},{10,8},{12,10},{14,12},{1,15},{3,1}... | collective-permute-start | bytes 294920 | tf_op jit(solution)/shard_map/ppermute | solution.py:228
  47.4 9.1 %collective-permute-start.6 = (bf16[128,384]{1,0:T(8,128)(2,1)S(1)}, bf16[128,384]{1,0:T(8,128)(2,1)S(1)}, u32[]{:S(2)}, u32[]{:S(2)}) collective-permute-start(bf16[128,384]{1,0:T(8,128)(2,1)S(1)} %get-tuple-element.38), channel_id=1, source_target_pairs={{0,12},{2,14},{4,0},{6,2},{8,4},{10,6},{12,8},{14,10},{1,13},{3,15... | collective-permute-start | bytes 294920 | tf_op jit(solution)/shard_map/ppermute | solution.py:229
  53.7 8.7 %collective-permute-start.9 = (bf16[128,384]{1,0:T(8,128)(2,1)S(1)}, bf16[128,384]{1,0:T(8,128)(2,1)S(1)}, u32[]{:S(2)}, u32[]{:S(2)}) collective-permute-start(bf16[128,384]{1,0:T(8,128)(2,1)S(1)} %collective-permute-done.5), channel_id=1, source_target_pairs={{0,4},{2,6},{4,8},{6,10},{8,12},{10,14},{12,0},{14,2},{1,5},{3,7},... | collective-permute-start | bytes 294920 | tf_op jit(solution)/shard_map/ppermute | solution.py:239
  54.1 7.0 %collective-permute-start.7 = (bf16[128,384]{1,0:T(8,128)(2,1)S(1)}, bf16[128,384]{1,0:T(8,128)(2,1)S(1)}, u32[]{:S(2)}, u32[]{:S(2)}) collective-permute-start(bf16[128,384]{1,0:T(8,128)(2,1)S(1)} %collective-permute-done.5), channel_id=1, source_target_pairs={{0,2},{2,4},{4,6},{6,8},{8,10},{10,12},{12,14},{14,0},{1,3},{3,5},... | collective-permute-start | bytes 294920 | tf_op jit(solution)/shard_map/ppermute | solution.py:238
  56.5 4.6 %collective-permute-start.8 = (bf16[128,384]{1,0:T(8,128)(2,1)S(1)}, bf16[128,384]{1,0:T(8,128)(2,1)S(1)}, u32[]{:S(2)}, u32[]{:S(2)}) collective-permute-start(bf16[128,384]{1,0:T(8,128)(2,1)S(1)} %collective-permute-done.6), channel_id=1, source_target_pairs={{0,14},{2,0},{4,2},{6,4},{8,6},{10,8},{12,10},{14,12},{1,15},{3,1}... | collective-permute-start | bytes 294920 | tf_op jit(solution)/shard_map/ppermute | solution.py:238

commit v5 on v4

--- a/solution.py
+++ b/solution.py
@@ -225,18 +225,15 @@
 
     up2 = [(i, (i + 2) % 8) for i in range(8)]
     down2 = [(i, (i + 6) % 8) for i in range(8)]
+    below2 = lax.ppermute(reduced, "z", up2)
+    above2 = lax.ppermute(reduced, "z", down2)
     below1, above1 = lax.ppermute(reduced, "z", up), lax.ppermute(reduced, "z", down)
-    below2, above2 = lax.ppermute(reduced, "z", up2), lax.ppermute(reduced, "z", down2)
-    below1, keep, beside, beyond, across = lax.optimization_barrier(
-        (below1, keep, beside, beyond, across)
+    below2, keep, beside, beyond, across = lax.optimization_barrier(
+        (below2, keep, beside, beyond, across)
     )
     schur = jnp.concatenate([keep, beside, beyond, across], axis=0)
-    below1, keep, beside, beyond, across = lax.optimization_barrier(
-        (below1, keep, beside, beyond, across)
-    )
-    schur = jnp.concatenate([keep, beside, beyond, across], axis=0)
+    opposite = lax.ppermute(below2, "z", up2)
     below3, above3 = lax.ppermute(below2, "z", up), lax.ppermute(above2, "z", down)
-    opposite = lax.ppermute(below2, "z", up2)
     for step, block in (
         (0, reduced),
         (-1, below1),

time: 117 us -> 116 us (level)
  waiting for transfers between devices: 18.3 us -> 14.9 us
  starting transfers between devices: 24.2 us -> 25.6 us
    ppermute x1, starting transfers between devices: 2.34 us -> 0.01 us  [on_device(): lax.ppermute(below2, 'z', up)]
    ppermute x2, waiting for transfers between devices: 3.51 us -> 1.19 us  [the longest x1 0.98 us: on_device(): below2 = lax.ppermute(reduced, 'z', up2)]
    ppermute x1, starting transfers between devices: 0.08 us -> 2.02 us  [on_device(): lax.ppermute(reduced, 'z', up)]
    ppermute x1, starting transfers between devices: 1.92 us -> 0.01 us  [on_device(): lax.ppermute(reduced, 'z', down)]
    ppermute x1, waiting for transfers between devices: 4.48 us -> 2.7 us  [on_device(): lax.ppermute(below2, 'z', up)]
    ppermute x1, starting transfers between devices: 0.01 us -> 1.68 us  [on_device(): lax.ppermute(above2, 'z', down)]
    ppermute x2, starting transfers between devices: 4.21 us -> 5.42 us  [the longest x1 3.91 us: on_device(): above2 = lax.ppermute(reduced, 'z', down2)]
  transfers between devices with their start and end apart: 11 -> 11, of which waited for: 4 -> 7; matrix products, arithmetic and copies ran while one was open for 11% -> 11% of each run, Pallas kernels for 0% -> 0%
where the time goes in v5:
time: 116 us
  blocking collectives  48.5 us (42%)
  starting transfers between devices  25.6 us (22%)
  waiting for transfers between devices  14.9 us (13%)
  Pallas kernels  11.3 us (10%)
  matrix products  8.3 us (7%)
  other arithmetic  3.44 us (3%)
  local copies, waits for them, and re-layouts  3.3 us (3%)
    all_to_all x1, blocking collectives, on_device(): lax.all_to_all(answers, EXCHANGE, 0, 0, tiled=True).reshape(4, 256, 384)  30 us
    all_to_all x1, blocking collectives, on_device(): pieces = lax.all_to_all(total.reshape(8, 128, 384), SHIFT, 0, 0, tiled=True)  18.5 us
    all_to_all x1, waiting for transfers between devices, on_device(): lax.all_to_all(packed, EXCHANGE, 0, 0, tiled=True).reshape(1024, 384)  8.97 us
    all_to_all x1, starting transfers between devices, on_device(): lax.all_to_all(packed, EXCHANGE, 0, 0, tiled=True).reshape(1024, 384)  8.73 us
    dot_general x6, matrix products, dot(): return jnp.dot(a, b, preferred_element_type=F32)  7.84 us
    pallas_call x1, Pallas kernels, start(): pl.pallas_call(start_kernel, grid=(2, steps), in_specs=[smem, smem, pl.Bl...  7.31 us
    pallas_call x1, Pallas kernels, finish(): pl.pallas_call(finish_kernel, grid=(1024 // rows,), in_specs=[pl.BlockSpe...  3.97 us
    ppermute x1, starting transfers between devices, on_device(): above2 = lax.ppermute(reduced, 'z', down2)  3.91 us
  transfers between devices with their start and end apart: 11, of which 7 were waited for; matrix products, arithmetic and copies ran while one was open for 11% of the time, Pallas kernels for 0%

profile of v5, /device:TPU:32, one launch (start us, length us, event | category | flops | bytes accessed | tf_op | source)
XLA Modules:
  0.0 115.8 jit_solution(14447366448765163899)
XLA Ops:
  0.0 7.3 %start.1 = (bf16[2,1024,384]{2,1,0:T(8,128)(2,1)}, bf16[2,2,256,384]{3,2,1,0:T(8,128)(2,1)}, bf16[256,512]{1,0:T(8,128)(2,1)}, bf16[512,256]{1,0:T(8,128)(2,1)}) custom-call(s32[1]{0:T(128)} %bitcast.position_ref, s32[32]{0:T(128)} %owner_ref.1, s32[32,256]{1,0:T(8,128)} %blocks_ref.1, bf16[2,1,1024,1024]{3,2,1,0:T(8,128)(2,1)} %inverse_ref.1, ...), custom_call_target="tpu_custom_call" | custom-call | tf_op jit(solution)/shard_map/start/pallas_call | solution.py:86
  7.3 0.0 copy-start.5
  7.3 0.0 copy-start.3
  7.3 0.0 copy-start.4
  7.4 0.0 copy-start.1
  7.4 2.7 %collective-permute-start.3 = (bf16[64,2048]{1,0:T(8,128)(2,1)S(1)}, bf16[64,2048]{1,0:T(8,128)(2,1)S(1)}, u32[]{:S(2)}, u32[]{:S(2)}) collective-permute-start(bf16[64,2048]{1,0:T(8,128)(2,1)S(1)} %get-tuple-element.43), channel_id=1, source_target_pairs={{0,17},{1,16},{16,1},{17,0},{2,19},{3,18},{18,3},{19,2},{4,21},{5,... | collective-permute-start | bytes 786440 | tf_op jit(solution)/shard_map/ppermute | solution.py:179
  10.2 0.7 collective-permute-start.1
  10.8 8.7 %all-to-all-start = ((bf16[32,32,384]{2,1,0:T(8,128)(2,1)}), bf16[32,32,384]{2,1,0:T(8,128)(2,1)S(1)}, u32[]{:S(2)}, u32[]{:S(2)}) async-start(bf16[32,32,384]{2,1,0:T(8,128)(2,1)} %bitcast.46), calls=%async_computation | async-start | bytes 1572864 | tf_op jit(solution)/shard_map/all_to_all | solution.py:175
  19.6 3.1 %collective-permute-start.2 = (bf16[64,2048]{1,0:T(8,128)(2,1)S(1)}, bf16[64,2048]{1,0:T(8,128)(2,1)S(1)}, u32[]{:S(2)}, u32[]{:S(2)}) collective-permute-start(bf16[64,2048]{1,0:T(8,128)(2,1)S(1)} %get-tuple-element.26), channel_id=1, source_target_pairs={{0,16},{16,0},{1,17},{17,1},{2,18},{18,2},{3,19},{19,3},{4,20},{20... | collective-permute-start | bytes 786440 | tf_op jit(solution)/shard_map/ppermute | solution.py:180
  22.6 0.1 reshape.111
  22.7 0.1 copy.11
  22.8 0.1 eq.61
  22.9 0.1 iota_compare_fusion.2
  23.0 0.3 select_reduce_fusion
  23.3 1.4 %compare_reduce_fusion = pred[32,256]{1,0:T(8,128)(4,1)S(1)} fusion(s32[256]{0:T(256)S(1)} %fusion.49, s32[32,256]{1,0:T(8,128)S(1)} %select_reduce_fusion), kind=kLoop, calls=%fused_computation | loop fusion | flops 4186112 | bytes 41984 | tf_op jit(solution)/shard_map/reduce_or | solution.py:188
  24.7 0.1 iota.108
  24.8 0.3 fusion.19
  25.1 0.2 fusion.20
  25.3 0.6 fusion.62
  25.9 1.1 fusion.56
  27.0 1.1 fusion.44
  28.1 4.1 %fusion.12.spread1_ref = bf16[1024,256]{1,0:T(8,128)(2,1)} fusion(bf16[2,1,1024,1024]{3,2,1,0:T(8,128)(2,1)} %inverse_ref.1, bf16[1,1024,256]{2,1,0:T(8,128)(2,1)S(1)} %copy-done.1, f32[]{:T(128)} %bitcast.8), kind=kOutput, calls=%fused_computation.11 | convolution fusion | flops 537395200 | bytes 3146240 | tf_op jit(solution)/shard_map/dot_general | solution.py:17
  32.1 2.2 %fusion.15.spread0_ref = bf16[1024,256]{1,0:T(8,128)(2,1)} fusion(bf16[2,1,1024,1024]{3,2,1,0:T(8,128)(2,1)S(1)} %copy-done, bf16[1,1024,256]{2,1,0:T(8,128)(2,1)S(1)} %copy-done.1, f32[]{:T(128)} %bitcast.5), kind=kOutput, calls=%fused_computation.12 | convolution fusion | flops 537395200 | bytes 3145732 | tf_op jit(solution)/shard_map/dot_general | solution.py:17
  34.3 9.0 %all-to-all-done = bf16[32,32,384]{2,1,0:T(8,128)(2,1)S(1)} async-done(((bf16[32,32,384]{2,1,0:T(8,128)(2,1)}), bf16[32,32,384]{2,1,0:T(8,128)(2,1)S(1)}, u32[]{:S(2)}, u32[]{:S(2)}) %all-to-all-start) | async-done | bytes 786464 | tf_op jit(solution)/shard_map/all_to_all | solution.py:175
  43.3 0.5 fusion.63
  43.7 0.1 broadcast_in_dim.44
  43.8 0.1 constant_dynamic-update-slice_fusion.11
  43.9 1.5 %collective-permute-start = (bf16[128,384]{1,0:T(8,128)(2,1)S(1)}, bf16[128,384]{1,0:T(8,128)(2,1)S(1)}, u32[]{:S(2)}, u32[]{:S(2)}) collective-permute-start(bf16[128,384]{1,0:T(8,128)(2,1)S(1)} %get-tuple-element.38), channel_id=1, source_target_pairs={{0,4},{2,6},{4,8},{6,10},{8,12},{10,14},{12,0},{14,2},{1,5},{3,7},... | collective-permute-start | bytes 294920 | tf_op jit(solution)/shard_map/ppermute | solution.py:228
  45.4 2.0 %collective-permute-start.4 = (bf16[128,384]{1,0:T(8,128)(2,1)S(1)}, bf16[128,384]{1,0:T(8,128)(2,1)S(1)}, u32[]{:S(2)}, u32[]{:S(2)}) collective-permute-start(bf16[128,384]{1,0:T(8,128)(2,1)S(1)} %get-tuple-element.38), channel_id=1, source_target_pairs={{0,2},{2,4},{4,6},{6,8},{8,10},{10,12},{12,14},{14,0},{1,3},{3,5},... | collective-permute-start | bytes 294920 | tf_op jit(solution)/shard_map/ppermute | solution.py:230
  47.4 3.9 %collective-permute-start.6 = (bf16[128,384]{1,0:T(8,128)(2,1)S(1)}, bf16[128,384]{1,0:T(8,128)(2,1)S(1)}, u32[]{:S(2)}, u32[]{:S(2)}) collective-permute-start(bf16[128,384]{1,0:T(8,128)(2,1)S(1)} %get-tuple-element.38), channel_id=1, source_target_pairs={{0,12},{2,14},{4,0},{6,2},{8,4},{10,6},{12,8},{14,10},{1,13},{3,15... | collective-permute-start | bytes 294920 | tf_op jit(solution)/shard_map/ppermute | solution.py:229
  51.3 1.0 collective-permute-done
  52.3 1.3 %collective-permute-start.9 = (bf16[128,384]{1,0:T(8,128)(2,1)S(1)}, bf16[128,384]{1,0:T(8,128)(2,1)S(1)}, u32[]{:S(2)}, u32[]{:S(2)}) collective-permute-start(bf16[128,384]{1,0:T(8,128)(2,1)S(1)} %collective-permute-done), channel_id=1, source_target_pairs={{0,4},{2,6},{4,8},{6,10},{8,12},{10,14},{12,0},{14,2},{1,5},{3,7},... | collective-permute-start | bytes 294920 | tf_op jit(solution)/shard_map/ppermute | solution.py:235
  53.7 0.4 collective-permute-done.4
  54.2 0.2 collective-permute-done.6
  54.4 1.7 %collective-permute-start.8 = (bf16[128,384]{1,0:T(8,128)(2,1)S(1)}, bf16[128,384]{1,0:T(8,128)(2,1)S(1)}, u32[]{:S(2)}, u32[]{:S(2)}) collective-permute-start(bf16[128,384]{1,0:T(8,128)(2,1)S(1)} %collective-permute-done.6), channel_id=1, source_target_pairs={{0,14},{2,0},{4,2},{6,4},{8,6},{10,8},{12,10},{14,12},{1,15},{3,1}... | collective-permute-start | bytes 294920 | tf_op jit(solution)/shard_map/ppermute | solution.py:236
  56.1 2.7 %collective-permute-done.7 = bf16[128,384]{1,0:T(8,128)(2,1)S(1)} collective-permute-done((bf16[128,384]{1,0:T(8,128)(2,1)S(1)}, bf16[128,384]{1,0:T(8,128)(2,1)S(1)}, u32[]{:S(2)}, u32[]{:S(2)}) %collective-permute-start.7) | collective-permute-done | bytes 98336 | tf_op jit(solution)/shard_map/ppermute | solution.py:236
  58.9 0.2 collective-permute-done.8
  59.1 1.4 %collective-permute-done.9 = bf16[128,384]{1,0:T(8,128)(2,1)S(1)} collective-permute-done((bf16[128,384]{1,0:T(8,128)(2,1)S(1)}, bf16[128,384]{1,0:T(8,128)(2,1)S(1)}, u32[]{:S(2)}, u32[]{:S(2)}) %collective-permute-start.9) | collective-permute-done | bytes 98336 | tf_op jit(solution)/shard_map/ppermute | solution.py:235
  60.5 0.4 fusion.21
  61.0 0.4 fusion.23
  61.7 0.1 fusion.59
  61.8 0.1 broadcast_select_fusion
  61.9 0.4 convolution_convert_fusion
  62.3 30.0 %all_to_all.15 = bf16[32,32,384]{2,1,0:T(8,128)(2,1)} all-to-all(bf16[32,32,384]{2,1,0:T(8,128)(2,1)S(1)} %bitcast.44), channel_id=1, replica_groups=mesh['yl'=2,'x'=4,'yh'=2,'z'=8,'c'=2] {'yh','c','z'}, dimensions={0} | all-to-all | bytes 1572864 | tf_op jit(solution)/shard_map/all_to_all | solution.py:261
  92.4 4.0 %finish.1 = bf16[1024,384]{1,0:T(8,128)(2,1)} custom-call(f32[2]{0:T(128)} %weights_ref.1, bf16[4,256,384]{2,1,0:T(8,128)(2,1)} %bitcast.42, bf16[512,256]{1,0:T(8,128)(2,1)} %get-tuple-element.31.pick_ref, bf16[1024,256]{1,0:T(8,128)(2,1)} %fusion.15.spread0_ref, bf16[1024,256]{1,0:T(8,128)(2,1)} %fusion.12.spread1_ref, ...), custom_call_target="tpu_custom_call" | custom-call | tf_op jit(solution)/shard_map/finish/pallas_call | solution.py:134
  96.3 18.5 %all_to_all.16 = bf16[8,128,384]{2,1,0:T(8,128)(2,1)S(1)} all-to-all(bf16[8,128,384]{2,1,0:T(8,128)(2,1)} %bitcast.43), channel_id=1, replica_groups=mesh['yl'=2,'x'=4,'yh'=2,'z'=8,'c'=2] {'yl','x'}, dimensions={0} | all-to-all | bytes 1572864 | tf_op jit(solution)/shard_map/all_to_all | solution.py:263
  114.8 0.1 convert_reduce_fusion
  114.9 0.8 reduce_sum.22
  (39 shorter events, 0.5 us)
Async XLA Ops:
  0.0 7.4 %copy-start.2 = (bf16[2,64,2048]{2,1,0:T(8,128)(2,1)S(1)}, bf16[2,64,2048]{2,1,0:T(8,128)(2,1)}, u32[]{:S(2)}) copy-start(bf16[2,64,2048]{2,1,0:T(8,128)(2,1)} %param.12) | copy-start | bytes 1572868
  7.3 15.3 %copy-start.5 = (s32[32]{0:T(128)S(1)}, s32[32]{0:T(128)}, u32[]{:S(2)}) copy-start(s32[32]{0:T(128)} %owner_ref.1) | copy-start | bytes 388
  7.3 15.7 %copy-start.3 = (s32[32,256]{1,0:T(8,128)S(1)}, s32[32,256]{1,0:T(8,128)}, u32[]{:S(2)}) copy-start(s32[32,256]{1,0:T(8,128)} %blocks_ref.1) | copy-start | bytes 98308
  7.3 18.0 %copy-start.4 = (f32[2]{0:T(128)S(1)}, f32[2]{0:T(128)}, u32[]{:S(2)}) copy-start(f32[2]{0:T(128)} %weights_ref.1) | copy-start | bytes 28
  7.4 20.6 %copy-start.1 = (bf16[1,1024,256]{2,1,0:T(8,128)(2,1)S(1)}, bf16[1,1024,256]{2,1,0:T(8,128)(2,1)}, u32[]{:S(2)}) copy-start(bf16[1,1024,256]{2,1,0:T(8,128)(2,1)} %couple_ref.1) | copy-start | bytes 1572868
  7.4 38.0 %collective-permute-start.3 = (bf16[64,2048]{1,0:T(8,128)(2,1)S(1)}, bf16[64,2048]{1,0:T(8,128)(2,1)S(1)}, u32[]{:S(2)}, u32[]{:S(2)}) collective-permute-start(bf16[64,2048]{1,0:T(8,128)(2,1)S(1)} %get-tuple-element.43), channel_id=1, source_target_pairs={{0,17},{1,16},{16,1},{17,0},{2,19},{3,18},{18,3},{19,2},{4,21},{5,... | collective-permute-start | bytes 786440 | tf_op jit(solution)/shard_map/ppermute | solution.py:179
  10.2 37.2 %collective-permute-start.1 = (bf16[64,2048]{1,0:T(8,128)(2,1)S(1)}, bf16[64,2048]{1,0:T(8,128)(2,1)S(1)}, u32[]{:S(2)}, u32[]{:S(2)}) collective-permute-start(bf16[64,2048]{1,0:T(8,128)(2,1)S(1)} %get-tuple-element.43), channel_id=1, source_target_pairs={{0,1},{1,0},{2,3},{3,2},{4,5},{5,4},{6,7},{7,6},{8,9},{9,8},{10,11... | collective-permute-start | bytes 786440 | tf_op jit(solution)/shard_map/ppermute | solution.py:181
  10.8 32.4 %all-to-all-start = ((bf16[32,32,384]{2,1,0:T(8,128)(2,1)}), bf16[32,32,384]{2,1,0:T(8,128)(2,1)S(1)}, u32[]{:S(2)}, u32[]{:S(2)}) async-start(bf16[32,32,384]{2,1,0:T(8,128)(2,1)} %bitcast.46), calls=%async_computation | async-start | bytes 1572864 | tf_op jit(solution)/shard_map/all_to_all | solution.py:175
  19.6 31.8 %collective-permute-start.2 = (bf16[64,2048]{1,0:T(8,128)(2,1)S(1)}, bf16[64,2048]{1,0:T(8,128)(2,1)S(1)}, u32[]{:S(2)}, u32[]{:S(2)}) collective-permute-start(bf16[64,2048]{1,0:T(8,128)(2,1)S(1)} %get-tuple-element.26), channel_id=1, source_target_pairs={{0,16},{16,0},{1,17},{17,1},{2,18},{18,2},{3,19},{19,3},{4,20},{20... | collective-permute-start | bytes 786440 | tf_op jit(solution)/shard_map/ppermute | solution.py:180
  28.0 4.1 %copy-start = (bf16[2,1,1024,1024]{3,2,1,0:T(8,128)(2,1)S(1)}, bf16[2,1,1024,1024]{3,2,1,0:T(8,128)(2,1)}, u32[]{:S(2)}) copy-start(bf16[2,1,1024,1024]{3,2,1,0:T(8,128)(2,1)} %inverse_ref.1) | copy-start | bytes 12582916
  43.9 8.4 %collective-permute-start = (bf16[128,384]{1,0:T(8,128)(2,1)S(1)}, bf16[128,384]{1,0:T(8,128)(2,1)S(1)}, u32[]{:S(2)}, u32[]{:S(2)}) collective-permute-start(bf16[128,384]{1,0:T(8,128)(2,1)S(1)} %get-tuple-element.38), channel_id=1, source_target_pairs={{0,4},{2,6},{4,8},{6,10},{8,12},{10,14},{12,0},{14,2},{1,5},{3,7},... | collective-permute-start | bytes 294920 | tf_op jit(solution)/shard_map/ppermute | solution.py:228
  45.4 8.8 %collective-permute-start.5 = (bf16[128,384]{1,0:T(8,128)(2,1)S(1)}, bf16[128,384]{1,0:T(8,128)(2,1)S(1)}, u32[]{:S(2)}, u32[]{:S(2)}) collective-permute-start(bf16[128,384]{1,0:T(8,128)(2,1)S(1)} %get-tuple-element.38), channel_id=1, source_target_pairs={{0,14},{2,0},{4,2},{6,4},{8,6},{10,8},{12,10},{14,12},{1,15},{3,1}... | collective-permute-start | bytes 294920 | tf_op jit(solution)/shard_map/ppermute | solution.py:230
  45.4 8.7 %collective-permute-start.4 = (bf16[128,384]{1,0:T(8,128)(2,1)S(1)}, bf16[128,384]{1,0:T(8,128)(2,1)S(1)}, u32[]{:S(2)}, u32[]{:S(2)}) collective-permute-start(bf16[128,384]{1,0:T(8,128)(2,1)S(1)} %get-tuple-element.38), channel_id=1, source_target_pairs={{0,2},{2,4},{4,6},{6,8},{8,10},{10,12},{12,14},{14,0},{1,3},{3,5},... | collective-permute-start | bytes 294920 | tf_op jit(solution)/shard_map/ppermute | solution.py:230
  47.4 7.0 %collective-permute-start.6 = (bf16[128,384]{1,0:T(8,128)(2,1)S(1)}, bf16[128,384]{1,0:T(8,128)(2,1)S(1)}, u32[]{:S(2)}, u32[]{:S(2)}) collective-permute-start(bf16[128,384]{1,0:T(8,128)(2,1)S(1)} %get-tuple-element.38), channel_id=1, source_target_pairs={{0,12},{2,14},{4,0},{6,2},{8,4},{10,6},{12,8},{14,10},{1,13},{3,15... | collective-permute-start | bytes 294920 | tf_op jit(solution)/shard_map/ppermute | solution.py:229
  52.3 8.2 %collective-permute-start.9 = (bf16[128,384]{1,0:T(8,128)(2,1)S(1)}, bf16[128,384]{1,0:T(8,128)(2,1)S(1)}, u32[]{:S(2)}, u32[]{:S(2)}) collective-permute-start(bf16[128,384]{1,0:T(8,128)(2,1)S(1)} %collective-permute-done), channel_id=1, source_target_pairs={{0,4},{2,6},{4,8},{6,10},{8,12},{10,14},{12,0},{14,2},{1,5},{3,7},... | collective-permute-start | bytes 294920 | tf_op jit(solution)/shard_map/ppermute | solution.py:235
  53.6 5.2 %collective-permute-start.7 = (bf16[128,384]{1,0:T(8,128)(2,1)S(1)}, bf16[128,384]{1,0:T(8,128)(2,1)S(1)}, u32[]{:S(2)}, u32[]{:S(2)}) collective-permute-start(bf16[128,384]{1,0:T(8,128)(2,1)S(1)} %collective-permute-done), channel_id=1, source_target_pairs={{0,2},{2,4},{4,6},{6,8},{8,10},{10,12},{12,14},{14,0},{1,3},{3,5},... | collective-permute-start | bytes 294920 | tf_op jit(solution)/shard_map/ppermute | solution.py:236
  54.4 4.7 %collective-permute-start.8 = (bf16[128,384]{1,0:T(8,128)(2,1)S(1)}, bf16[128,384]{1,0:T(8,128)(2,1)S(1)}, u32[]{:S(2)}, u32[]{:S(2)}) collective-permute-start(bf16[128,384]{1,0:T(8,128)(2,1)S(1)} %collective-permute-done.6), channel_id=1, source_target_pairs={{0,14},{2,0},{4,2},{6,4},{8,6},{10,8},{12,10},{14,12},{1,15},{3,1}... | collective-permute-start | bytes 294920 | tf_op jit(solution)/shard_map/ppermute | solution.py:236

commit v6 on v5

--- a/solution.py
+++ b/solution.py
@@ -111,42 +111,94 @@
     )(position, owner_sub, index_blocks, inverse, rhs, couple)
 
 
+CHUNK = 256
+WHOLE = pl.BlockSpec(memory_space=pltpu.VMEM)
+SCALAR = pl.BlockSpec(memory_space=pltpu.SMEM)
+
+
+def solve_kernel(y_ref, z_ref, c_ref, *refs):
+    blocks, rows = refs[:8], refs[8:12]
+    select_ref, answers_ref, gathered_ref, schur_ref, both_ref = refs[12:]
+    y, z, c = y_ref[0], z_ref[0], c_ref[0]
+    for step, block in zip((0, -1, 1, -2, 2, -3, 3, 4), blocks):
+        at = pl.multiple_of(((z + step + 8) & 7) * 128, 128)
+        gathered_ref[pl.ds(at, 128)] = block[...]
+    for (dy, dc), part in zip(((0, 0), (0, 1), (1, 0), (1, 1)), rows):
+        at = pl.multiple_of(((y + dy) & 1) * 128 + ((c + dc) & 1) * 64, 64)
+        schur_ref[pl.ds(at, 64)] = part[...]
+    low = lax.broadcasted_iota(jnp.int32, (128, 384), 1) < HALF
+    from0 = dot(schur_ref[:, :1024], gathered_ref[...])
+    from1 = dot(schur_ref[:, 1024:], gathered_ref[...])
+    straight = jnp.where(low, from0[:128], from1[128:])
+    crossed = jnp.where(low, from0[128:], from1[:128])
+    solved = straight + roll32(crossed)
+    both_ref[:128] = jnp.where(low, solved, 0.0).astype(BF)
+    both_ref[128:] = jnp.where(low, 0.0, solved).astype(BF)
+    answers_ref[...] = dot(select_ref[...], both_ref[...]).astype(BF)
+
+
+def solve(place, blocks, rows, select):
+    return pl.pallas_call(
+        solve_kernel,
+        in_specs=[SCALAR] * 3 + [WHOLE] * 13,
+        out_specs=WHOLE,
+        out_shape=jax.ShapeDtypeStruct((1024, 384), BF),
+        scratch_shapes=[
+            pltpu.VMEM((1024, 384), BF),
+            pltpu.VMEM((256, 2048), BF),
+            pltpu.VMEM((256, 384), BF),
+        ],
+        compiler_params=pltpu.CompilerParams(vmem_limit_bytes=8 << 20),
+        name="solve",
+    )(*place, *blocks, *rows, select)
+
+
 def finish_kernel(
     weights_ref, back_ref, pick_ref, spread0_ref, spread1_ref, eliminated_ref, out_ref, picked_ref
 ):
-    @pl.when(pl.program_id(0) == 0)
-    def _():
-        low = lax.broadcasted_iota(jnp.int32, (256, 384), 1) < HALF
-        for j in range(2):
-            top = [dot(pick_ref[:256], back_ref[2 * h + j]) for h in range(2)]
-            end = [dot(pick_ref[256:], back_ref[2 * h + j]) for h in range(2)]
-            straight = jnp.where(low, top[0], end[1])
-            crossed = jnp.where(low, top[1], end[0])
-            picked_ref[j] = (straight + roll32(crossed)).astype(BF)
-
-    total = weights_ref[0] * eliminated_ref[0].astype(F32)
-    total += weights_ref[1] * eliminated_ref[1].astype(F32)
-    total -= dot(spread0_ref[...], picked_ref[0]) + dot(spread1_ref[...], picked_ref[1])
-    out_ref[...] = total.astype(BF)
-
-
-def finish(weights, back, pick, spread0, spread1, eliminated, rows=512):
+    low = lax.broadcasted_iota(jnp.int32, (256, 384), 1) < HALF
+    for j in range(2):
+        top = [dot(pick_ref[:256], back_ref[2 * h + j]) for h in range(2)]
+        end = [dot(pick_ref[256:], back_ref[2 * h + j]) for h in range(2)]
+        straight = jnp.where(low, top[0], end[1])
+        crossed = jnp.where(low, top[1], end[0])
+        picked_ref[j] = (straight + roll32(crossed)).astype(BF)
+    for i in range(1024 // CHUNK):
+        rows = pl.ds(i * CHUNK, CHUNK)
+        total = weights_ref[0] * eliminated_ref[0, rows].astype(F32)
+        total += weights_ref[1] * eliminated_ref[1, rows].astype(F32)
+        total -= dot(spread0_ref[rows], picked_ref[0]) + dot(spread1_ref[rows], picked_ref[1])
+        out_ref[rows] = total.astype(BF)
+
+
+def finish(weights, back, pick, spread0, spread1, eliminated):
     return pl.pallas_call(
         finish_kernel,
-        grid=(1024 // rows,),
-        in_specs=[
-            pl.BlockSpec(memory_space=pltpu.SMEM),
-            pl.BlockSpec((4, 256, 384), lambda i: (0, 0, 0)),
-            pl.BlockSpec((512, 256), lambda i: (0, 0)),
-            pl.BlockSpec((rows, 256), lambda i: (i, 0)),
-            pl.BlockSpec((rows, 256), lambda i: (i, 0)),
-            pl.BlockSpec((2, rows, 384), lambda i: (0, i, 0)),
-        ],
-        out_specs=pl.BlockSpec((rows, 384), lambda i: (i, 0)),
+        in_specs=[SCALAR] + [WHOLE] * 5,
+        out_specs=WHOLE,
         out_shape=jax.ShapeDtypeStruct((1024, 384), BF),
         scratch_shapes=[pltpu.VMEM((2, 256, 384), BF)],
+        compiler_params=pltpu.CompilerParams(vmem_limit_bytes=8 << 20),
         name="finish",
     )(weights, back, pick, spread0, spread1, eliminated)
+
+
+def add_kernel(pieces_ref, out_ref):
+    total = pieces_ref[0].astype(F32)
+    for i in range(1, 8):
+        total += pieces_ref[i].astype(F32)
+    out_ref[...] = total[:, None, :]
+
+
+def add(pieces):
+    return pl.pallas_call(
+        add_kernel,
+        in_specs=[WHOLE],
+        out_specs=WHOLE,
+        out_shape=jax.ShapeDtypeStruct((128, 1, 384), F32),
+        compiler_params=pltpu.CompilerParams(vmem_limit_bytes=4 << 20),
+        name="add",
+    )(pieces)
 
 
 def on_device(
@@ -169,7 +221,6 @@
     eliminated, packed, _, pick = start(
         position[None], owner_sub, index_blocks, interior_inverse, interior_rhs, coupling
     )
-    zero = jnp.zeros((), BF)
     packed, schur_inverse = lax.optimization_barrier((packed, schur_inverse))
     packed = packed.reshape(32, 32, 384)
     arrived = lax.all_to_all(packed, EXCHANGE, 0, 0, tiled=True).reshape(1024, 384)
@@ -218,50 +269,23 @@
 
     up = [(i, (i + 1) % 8) for i in range(8)]
     down = [(i, (i + 7) % 8) for i in range(8)]
-    gathered = jnp.zeros((1024, 384), BF)
-
-    def put(block, step):
-        return lax.dynamic_update_slice(gathered, block, (((z + step) & 7) * 128, 0))
-
     up2 = [(i, (i + 2) % 8) for i in range(8)]
     down2 = [(i, (i + 6) % 8) for i in range(8)]
     below2 = lax.ppermute(reduced, "z", up2)
     above2 = lax.ppermute(reduced, "z", down2)
     below1, above1 = lax.ppermute(reduced, "z", up), lax.ppermute(reduced, "z", down)
-    below2, keep, beside, beyond, across = lax.optimization_barrier(
-        (below2, keep, beside, beyond, across)
-    )
-    schur = jnp.concatenate([keep, beside, beyond, across], axis=0)
     opposite = lax.ppermute(below2, "z", up2)
     below3, above3 = lax.ppermute(below2, "z", up), lax.ppermute(above2, "z", down)
-    for step, block in (
-        (0, reduced),
-        (-1, below1),
-        (1, above1),
-        (-2, below2),
-        (2, above2),
-        (-3, below3),
-        (3, above3),
-        (4, opposite),
-    ):
-        gathered = put(block, step)
-    from0, from1 = dot(schur[:, :1024], gathered), dot(schur[:, 1024:], gathered)
-
-    def half(x, q):
-        x = jnp.where(y == q, x[:128], x[128:])
-        return jnp.where(c == 0, x, jnp.concatenate([x[64:], x[:64]], axis=0))
-
-    straight = jnp.where(low_i, half(from0, 0), half(from1, 1))
-    crossed = jnp.where(low_i, half(from0, 1), half(from1, 0))
-    solved = (straight + roll(crossed)).astype(BF)
-    both = jnp.concatenate(
-        [jnp.where(low_i, solved, zero), jnp.where(low_i, zero, solved)], axis=0
-    )
-    answers = dot(select, both).astype(BF).reshape(32, 32, 384)
+    answers = solve(
+        [i.astype(jnp.int32)[None] for i in (y, z, c)],
+        (reduced, below1, above1, below2, above2, below3, above3, opposite),
+        (keep, beside, beyond, across),
+        select,
+    ).reshape(32, 32, 384)
     back = lax.all_to_all(answers, EXCHANGE, 0, 0, tiled=True).reshape(4, 256, 384)
     total = finish(weights, back, pick, *spread, eliminated)
     pieces = lax.all_to_all(total.reshape(8, 128, 384), SHIFT, 0, 0, tiled=True)
-    return jnp.sum(pieces.reshape(8, 128, 1, 384).astype(F32), axis=0)
+    return add(pieces)
 
 
 def solution(mesh):

time: 116 us -> 116 us (level)
  waiting for transfers between devices: 14.9 us -> 19.9 us
  matrix products: 8.3 us -> 5.4 us
  starting transfers between devices: 25.6 us -> 24.2 us
    ppermute x1, starting transfers between devices: 0.01 us -> 3.23 us  [on_device(): lax.ppermute(below2, 'z', up)]
    ppermute x1, starting transfers between devices: 3.91 us -> 0.84 us  [on_device(): above2 = lax.ppermute(reduced, 'z', down2)]
    dot_general x6 -> x3, matrix products: 7.84 us -> 4.93 us  [dot(): return jnp.dot(a, b, preferred_element_type=F32)]
    ppermute x1, waiting for transfers between devices: 1.41 us -> 4.32 us  [on_device(): opposite = lax.ppermute(below2, 'z', up2)]
    ppermute x1, waiting for transfers between devices: 2.7 us -> 0.01 us  [on_device(): lax.ppermute(below2, 'z', up)]
    ppermute x1, waiting for transfers between devices: 0.98 us -> 3.15 us  [on_device(): below2 = lax.ppermute(reduced, 'z', up2)]
    ppermute x1, starting transfers between devices: 1.68 us -> 0.01 us  [on_device(): lax.ppermute(above2, 'z', down)]
    ppermute x1, waiting for transfers between devices: 0.21 us -> 1.87 us  [on_device(): above2 = lax.ppermute(reduced, 'z', down2)]
  transfers between devices with their start and end apart: 11 -> 11, of which waited for: 7 -> 4; matrix products, arithmetic and copies ran while one was open for 11% -> 9% of each run, Pallas kernels for 0% -> 0%
where the time goes in v6:
time: 116 us
  blocking collectives  48.9 us (42%)
  starting transfers between devices  24.2 us (21%)
  waiting for transfers between devices  19.9 us (17%)
  Pallas kernels  11.4 us (10%)
  matrix products  5.4 us (5%)
  other arithmetic  3.09 us (3%)
  local copies, waits for them, and re-layouts  2.79 us (2%)
    all_to_all x1, blocking collectives, on_device(): lax.all_to_all(answers, EXCHANGE, 0, 0, tiled=True).reshape(4, 256, 384)  30.6 us
    all_to_all x1, blocking collectives, on_device(): pieces = lax.all_to_all(total.reshape(8, 128, 384), SHIFT, 0, 0, tiled=True)  18.3 us
    all_to_all x1, waiting for transfers between devices, on_device(): lax.all_to_all(packed, EXCHANGE, 0, 0, tiled=True).reshape(1024, 384)  10.5 us
    all_to_all x1, starting transfers between devices, on_device(): lax.all_to_all(packed, EXCHANGE, 0, 0, tiled=True).reshape(1024, 384)  8.73 us
    pallas_call x1, Pallas kernels, start(): pl.pallas_call(start_kernel, grid=(2, steps), in_specs=[smem, smem, pl.Bl...  7.32 us
    dot_general x3, matrix products, dot(): return jnp.dot(a, b, preferred_element_type=F32)  4.93 us
    ppermute x1, waiting for transfers between devices, on_device(): opposite = lax.ppermute(below2, 'z', up2)  4.32 us
    ppermute x1, starting transfers between devices, on_device(): lax.ppermute(below2, 'z', up)  3.23 us
  transfers between devices with their start and end apart: 11, of which 4 were waited for; matrix products, arithmetic and copies ran while one was open for 9% of the time, Pallas kernels for 0%

profile of v6, /device:TPU:32, one launch (start us, length us, event | category | flops | bytes accessed | tf_op | source)
XLA Modules:
  0.0 115.9 jit_solution(6665127688040345814)
XLA Ops:
  0.0 7.3 %start.1 = (bf16[2,1024,384]{2,1,0:T(8,128)(2,1)}, bf16[2,2,256,384]{3,2,1,0:T(8,128)(2,1)}, bf16[256,512]{1,0:T(8,128)(2,1)}, bf16[512,256]{1,0:T(8,128)(2,1)}) custom-call(s32[1]{0:T(128)} %bitcast.3.position_ref, s32[32]{0:T(128)} %owner_ref.1, s32[32,256]{1,0:T(8,128)} %blocks_ref.1, bf16[2,1,1024,1024]{3,2,1,0:T(8,128)(2,1)} %inverse_ref.1, ...), custom_call_target="tpu_custom_call" | custom-call | tf_op jit(solution)/shard_map/start/pallas_call | solution.py:86
  7.3 0.0 copy-start.8
  7.3 0.0 copy-start.7
  7.3 0.0 copy-start.2
  7.4 0.8 dynamic-slice_bitcast_fusion
  8.2 2.6 %collective-permute-start.9 = (bf16[64,2048]{1,0:T(8,128)(2,1)}, bf16[64,2048]{1,0:T(8,128)(2,1)S(1)}, u32[]{:S(2)}, u32[]{:S(2)}) collective-permute-start(bf16[64,2048]{1,0:T(8,128)(2,1)} %get-tuple-element.29), channel_id=1, source_target_pairs={{0,17},{1,16},{16,1},{17,0},{2,19},{3,18},{18,3},{19,2},{4,21},{5,... | collective-permute-start | bytes 786440 | tf_op jit(solution)/shard_map/ppermute | solution.py:230
  10.8 0.7 collective-permute-start.7
  11.5 8.7 %all-to-all-start = ((bf16[32,32,384]{2,1,0:T(8,128)(2,1)}), bf16[32,32,384]{2,1,0:T(8,128)(2,1)S(1)}, u32[]{:S(2)}, u32[]{:S(2)}) async-start(bf16[32,32,384]{2,1,0:T(8,128)(2,1)} %bitcast.46), calls=%async_computation | async-start | bytes 1572864 | tf_op jit(solution)/shard_map/all_to_all | solution.py:226
  20.2 3.1 %collective-permute-start.8 = (bf16[64,2048]{1,0:T(8,128)(2,1)S(1)}, bf16[64,2048]{1,0:T(8,128)(2,1)S(1)}, u32[]{:S(2)}, u32[]{:S(2)}) collective-permute-start(bf16[64,2048]{1,0:T(8,128)(2,1)S(1)} %get-tuple-element.30.refs_8_), channel_id=1, source_target_pairs={{0,16},{16,0},{1,17},{17,1},{2,18},{18,2},{3,19},{19,3},{4,20},{20... | collective-permute-start | bytes 786440 | tf_op jit(solution)/shard_map/ppermute | solution.py:231
  23.3 0.1 reshape.108
  23.4 0.1 copy.11
  23.5 0.1 eq.49
  23.5 0.1 iota_compare_fusion.2
  23.6 0.3 select_reduce_fusion
  23.9 1.4 %compare_reduce_fusion = pred[32,256]{1,0:T(8,128)(4,1)S(1)} fusion(s32[256]{0:T(256)S(1)} %fusion.38, s32[32,256]{1,0:T(8,128)S(1)} %select_reduce_fusion), kind=kLoop, calls=%fused_computation | loop fusion | flops 4186112 | bytes 41984 | tf_op jit(solution)/shard_map/reduce_or | solution.py:239
  25.3 0.1 iota.92
  25.4 0.3 fusion.19
  25.7 0.2 fusion.20.refs_12_
  26.0 0.6 fusion.43
  26.5 1.1 fusion.42
  27.6 1.1 fusion.33
  28.7 0.0 copy-start.3
  28.7 0.0 copy-start.5
  28.7 3.4 %fusion.12.spread1_ref = bf16[1024,256]{1,0:T(8,128)(2,1)S(1)} fusion(bf16[2,1,1024,1024]{3,2,1,0:T(8,128)(2,1)} %inverse_ref.1, bf16[1,1024,256]{2,1,0:T(8,128)(2,1)S(1)} %copy-done.4, f32[]{:T(128)} %bitcast.11), kind=kOutput, calls=%fused_computation.9 | convolution fusion | flops 537395200 | bytes 3146240 | tf_op jit(solution)/shard_map/dot_general | solution.py:17
  32.1 1.3 %fusion.15.spread0_ref = bf16[1024,256]{1,0:T(8,128)(2,1)S(1)} fusion(bf16[2,1,1024,1024]{3,2,1,0:T(8,128)(2,1)S(1)} %copy-done.3, bf16[1,1024,256]{2,1,0:T(8,128)(2,1)S(1)} %copy-done.5, f32[]{:T(128)} %bitcast.8), kind=kOutput, calls=%fused_computation.10 | convolution fusion | flops 537395200 | bytes 3145732 | tf_op jit(solution)/shard_map/dot_general | solution.py:17
  33.4 10.5 %all-to-all-done = bf16[32,32,384]{2,1,0:T(8,128)(2,1)S(1)} async-done(((bf16[32,32,384]{2,1,0:T(8,128)(2,1)}), bf16[32,32,384]{2,1,0:T(8,128)(2,1)S(1)}, u32[]{:S(2)}, u32[]{:S(2)}) %all-to-all-start) | async-done | bytes 786464 | tf_op jit(solution)/shard_map/all_to_all | solution.py:226
  43.9 0.5 fusion.44
  44.4 0.8 collective-permute-start.3
  45.3 2.2 %collective-permute-start.2 = (bf16[128,384]{1,0:T(8,128)(2,1)S(1)}, bf16[128,384]{1,0:T(8,128)(2,1)S(1)}, u32[]{:S(2)}, u32[]{:S(2)}) collective-permute-start(bf16[128,384]{1,0:T(8,128)(2,1)S(1)} %fusion.26.refs_0_), channel_id=1, source_target_pairs={{0,4},{2,6},{4,8},{6,10},{8,12},{10,14},{12,0},{14,2},{1,5},{3,7},... | collective-permute-start | bytes 294920 | tf_op jit(solution)/shard_map/ppermute | solution.py:274
  47.4 0.0 collective-permute-done.9.refs_11_
  47.4 0.0 collective-permute-start.1
  47.4 0.0 collective-permute-done.7.refs_9_
  47.4 2.0 %collective-permute-start = (bf16[128,384]{1,0:T(8,128)(2,1)S(1)}, bf16[128,384]{1,0:T(8,128)(2,1)S(1)}, u32[]{:S(2)}, u32[]{:S(2)}) collective-permute-start(bf16[128,384]{1,0:T(8,128)(2,1)S(1)} %fusion.26.refs_0_), channel_id=1, source_target_pairs={{0,2},{2,4},{4,6},{6,8},{8,10},{10,12},{12,14},{14,0},{1,3},{3,5},... | collective-permute-start | bytes 294920 | tf_op jit(solution)/shard_map/ppermute | solution.py:276
  49.4 1.9 %collective-permute-done.3.refs_4_ = bf16[128,384]{1,0:T(8,128)(2,1)S(1)} collective-permute-done((bf16[128,384]{1,0:T(8,128)(2,1)S(1)}, bf16[128,384]{1,0:T(8,128)(2,1)S(1)}, u32[]{:S(2)}, u32[]{:S(2)}) %collective-permute-start.3) | collective-permute-done | bytes 98336 | tf_op jit(solution)/shard_map/ppermute | solution.py:275
  51.3 0.0 collective-permute-start.5
  51.3 3.2 %collective-permute-done.2.refs_3_ = bf16[128,384]{1,0:T(8,128)(2,1)S(1)} collective-permute-done((bf16[128,384]{1,0:T(8,128)(2,1)S(1)}, bf16[128,384]{1,0:T(8,128)(2,1)S(1)}, u32[]{:S(2)}, u32[]{:S(2)}) %collective-permute-start.2) | collective-permute-done | bytes 98336 | tf_op jit(solution)/shard_map/ppermute | solution.py:274
  54.5 0.8 collective-permute-start.6
  55.3 0.0 collective-permute-done.8.refs_10_
  55.3 3.2 %collective-permute-start.4 = (bf16[128,384]{1,0:T(8,128)(2,1)S(1)}, bf16[128,384]{1,0:T(8,128)(2,1)S(1)}, u32[]{:S(2)}, u32[]{:S(2)}) collective-permute-start(bf16[128,384]{1,0:T(8,128)(2,1)S(1)} %collective-permute-done.2.refs_3_), channel_id=1, source_target_pairs={{0,2},{2,4},{4,6},{6,8},{8,10},{10,12},{12,14},{14,0},{1,3},{3,5},... | collective-permute-start | bytes 294920 | tf_op jit(solution)/shard_map/ppermute | solution.py:278
  58.5 0.0 collective-permute-done.1.refs_2_
  58.5 0.0 collective-permute-done.refs_1_
  58.5 0.0 collective-permute-done.5.refs_6_
  58.5 4.3 %collective-permute-done.6.refs_7_ = bf16[128,384]{1,0:T(8,128)(2,1)S(1)} collective-permute-done((bf16[128,384]{1,0:T(8,128)(2,1)S(1)}, bf16[128,384]{1,0:T(8,128)(2,1)S(1)}, u32[]{:S(2)}, u32[]{:S(2)}) %collective-permute-start.6) | collective-permute-done | bytes 98336 | tf_op jit(solution)/shard_map/ppermute | solution.py:277
  62.9 1.3 %solve.1 = bf16[1024,384]{1,0:T(8,128)(2,1)S(1)} custom-call(s32[1]{0:T(128)} %bitcast.y_ref, s32[1]{0:T(128)} %bitcast.1.z_ref, s32[1]{0:T(128)} %bitcast.2.c_ref, bf16[128,384]{1,0:T(8,128)(2,1)S(1)} %fusion.26.refs_0_, bf16[128,384]{1,0:T(8,128)(2,1)S(1)} %collective-permute-done.refs_1_, bf16[128,384]{1,0:T(8,128)(2,1)S(1)} %collective-permute-done.1.refs_2_, ...), custom_call_target="tpu_custom_call" | custom-call | tf_op jit(solution)/shard_map/solve/pallas_call | solution.py:141
  64.2 30.6 %all_to_all.15 = bf16[32,32,384]{2,1,0:T(8,128)(2,1)S(1)} all-to-all(bf16[32,32,384]{2,1,0:T(8,128)(2,1)S(1)} %bitcast.44), channel_id=1, replica_groups=mesh['yl'=2,'x'=4,'yh'=2,'z'=8,'c'=2] {'yh','c','z'}, dimensions={0} | all-to-all | bytes 1572864 | tf_op jit(solution)/shard_map/all_to_all | solution.py:285
  94.8 2.0 %finish.1 = bf16[1024,384]{1,0:T(8,128)(2,1)S(1)} custom-call(f32[2]{0:T(128)S(1)} %copy-done.2, bf16[4,256,384]{2,1,0:T(8,128)(2,1)S(1)} %bitcast.42, bf16[512,256]{1,0:T(8,128)(2,1)S(1)} %copy-done.1, bf16[1024,256]{1,0:T(8,128)(2,1)S(1)} %fusion.15.spread0_ref, bf16[1024,256]{1,0:T(8,128)(2,1)S(1)} %fusion.12.spread1_ref, bf16[2,1024,384]{2,1,0:T(8,128)(2,1)S(1)} %copy-done), custom_call_target="tpu_custom_call" | custom-call | tf_op jit(solution)/shard_map/finish/pallas_call | solution.py:175
  96.8 18.3 %all_to_all.16.pieces_ref = bf16[8,128,384]{2,1,0:T(8,128)(2,1)S(1)} all-to-all(bf16[8,128,384]{2,1,0:T(8,128)(2,1)S(1)} %bitcast.43), channel_id=1, replica_groups=mesh['yl'=2,'x'=4,'yh'=2,'z'=8,'c'=2] {'yl','x'}, dimensions={0} | all-to-all | bytes 1572864 | tf_op jit(solution)/shard_map/all_to_all | solution.py:287
  115.1 0.8 add.108
  (20 shorter events, 0.1 us)
Async XLA Ops:
  0.0 7.4 %copy-start.6 = (bf16[2,64,2048]{2,1,0:T(8,128)(2,1)S(1)}, bf16[2,64,2048]{2,1,0:T(8,128)(2,1)}, u32[]{:S(2)}) copy-start(bf16[2,64,2048]{2,1,0:T(8,128)(2,1)} %param.12) | copy-start | bytes 1572868
  7.3 15.9 %copy-start.8 = (s32[32]{0:T(128)S(1)}, s32[32]{0:T(128)}, u32[]{:S(2)}) copy-start(s32[32]{0:T(128)} %owner_ref.1) | copy-start | bytes 388
  7.3 16.3 %copy-start.7 = (s32[32,256]{1,0:T(8,128)S(1)}, s32[32,256]{1,0:T(8,128)}, u32[]{:S(2)}) copy-start(s32[32,256]{1,0:T(8,128)} %blocks_ref.1) | copy-start | bytes 98308
  7.3 18.6 %copy-start.2 = (f32[2]{0:T(128)S(1)}, f32[2]{0:T(128)}, u32[]{:S(2)}) copy-start(f32[2]{0:T(128)} %weights_ref.1) | copy-start | bytes 28
  8.2 20.5 %copy-start.4 = (bf16[1,1024,256]{2,1,0:T(8,128)(2,1)S(1)}, bf16[1,1024,256]{2,1,0:T(8,128)(2,1)}, u32[]{:S(2)}) copy-start(bf16[1,1024,256]{2,1,0:T(8,128)(2,1)} %couple_ref.1) | copy-start | bytes 1572868
  8.2 39.3 %collective-permute-start.9 = (bf16[64,2048]{1,0:T(8,128)(2,1)}, bf16[64,2048]{1,0:T(8,128)(2,1)S(1)}, u32[]{:S(2)}, u32[]{:S(2)}) collective-permute-start(bf16[64,2048]{1,0:T(8,128)(2,1)} %get-tuple-element.29), channel_id=1, source_target_pairs={{0,17},{1,16},{16,1},{17,0},{2,19},{3,18},{18,3},{19,2},{4,21},{5,... | collective-permute-start | bytes 786440 | tf_op jit(solution)/shard_map/ppermute | solution.py:230
  10.8 36.6 %collective-permute-start.7 = (bf16[64,2048]{1,0:T(8,128)(2,1)}, bf16[64,2048]{1,0:T(8,128)(2,1)S(1)}, u32[]{:S(2)}, u32[]{:S(2)}) collective-permute-start(bf16[64,2048]{1,0:T(8,128)(2,1)} %get-tuple-element.29), channel_id=1, source_target_pairs={{0,1},{1,0},{2,3},{3,2},{4,5},{5,4},{6,7},{7,6},{8,9},{9,8},{10,11... | collective-permute-start | bytes 786440 | tf_op jit(solution)/shard_map/ppermute | solution.py:232
  11.5 32.4 %all-to-all-start = ((bf16[32,32,384]{2,1,0:T(8,128)(2,1)}), bf16[32,32,384]{2,1,0:T(8,128)(2,1)S(1)}, u32[]{:S(2)}, u32[]{:S(2)}) async-start(bf16[32,32,384]{2,1,0:T(8,128)(2,1)} %bitcast.46), calls=%async_computation | async-start | bytes 1572864 | tf_op jit(solution)/shard_map/all_to_all | solution.py:226
  20.2 35.1 %collective-permute-start.8 = (bf16[64,2048]{1,0:T(8,128)(2,1)S(1)}, bf16[64,2048]{1,0:T(8,128)(2,1)S(1)}, u32[]{:S(2)}, u32[]{:S(2)}) collective-permute-start(bf16[64,2048]{1,0:T(8,128)(2,1)S(1)} %get-tuple-element.30.refs_8_), channel_id=1, source_target_pairs={{0,16},{16,0},{1,17},{17,1},{2,18},{18,2},{3,19},{19,3},{4,20},{20... | collective-permute-start | bytes 786440 | tf_op jit(solution)/shard_map/ppermute | solution.py:231
  28.7 3.4 %copy-start.3 = (bf16[2,1,1024,1024]{3,2,1,0:T(8,128)(2,1)S(1)}, bf16[2,1,1024,1024]{3,2,1,0:T(8,128)(2,1)}, u32[]{:S(2)}) copy-start(bf16[2,1,1024,1024]{3,2,1,0:T(8,128)(2,1)} %inverse_ref.1) | copy-start | bytes 12582916
  28.7 3.4 %copy-start.5 = (bf16[1,1024,256]{2,1,0:T(8,128)(2,1)S(1)}, bf16[1,1024,256]{2,1,0:T(8,128)(2,1)}, u32[]{:S(2)}) copy-start(bf16[1,1024,256]{2,1,0:T(8,128)(2,1)} %couple_ref.1) | copy-start | bytes 1572868
  44.4 6.9 %collective-permute-start.3 = (bf16[128,384]{1,0:T(8,128)(2,1)S(1)}, bf16[128,384]{1,0:T(8,128)(2,1)S(1)}, u32[]{:S(2)}, u32[]{:S(2)}) collective-permute-start(bf16[128,384]{1,0:T(8,128)(2,1)S(1)} %fusion.26.refs_0_), channel_id=1, source_target_pairs={{0,12},{2,14},{4,0},{6,2},{8,4},{10,6},{12,8},{14,10},{1,13},{3,15... | collective-permute-start | bytes 294920 | tf_op jit(solution)/shard_map/ppermute | solution.py:275
  45.3 9.2 %collective-permute-start.2 = (bf16[128,384]{1,0:T(8,128)(2,1)S(1)}, bf16[128,384]{1,0:T(8,128)(2,1)S(1)}, u32[]{:S(2)}, u32[]{:S(2)}) collective-permute-start(bf16[128,384]{1,0:T(8,128)(2,1)S(1)} %fusion.26.refs_0_), channel_id=1, source_target_pairs={{0,4},{2,6},{4,8},{6,10},{8,12},{10,14},{12,0},{14,2},{1,5},{3,7},... | collective-permute-start | bytes 294920 | tf_op jit(solution)/shard_map/ppermute | solution.py:274
  47.4 11.1 %collective-permute-start.1 = (bf16[128,384]{1,0:T(8,128)(2,1)S(1)}, bf16[128,384]{1,0:T(8,128)(2,1)S(1)}, u32[]{:S(2)}, u32[]{:S(2)}) collective-permute-start(bf16[128,384]{1,0:T(8,128)(2,1)S(1)} %fusion.26.refs_0_), channel_id=1, source_target_pairs={{0,14},{2,0},{4,2},{6,4},{8,6},{10,8},{12,10},{14,12},{1,15},{3,1}... | collective-permute-start | bytes 294920 | tf_op jit(solution)/shard_map/ppermute | solution.py:276
  47.4 11.1 %collective-permute-start = (bf16[128,384]{1,0:T(8,128)(2,1)S(1)}, bf16[128,384]{1,0:T(8,128)(2,1)S(1)}, u32[]{:S(2)}, u32[]{:S(2)}) collective-permute-start(bf16[128,384]{1,0:T(8,128)(2,1)S(1)} %fusion.26.refs_0_), channel_id=1, source_target_pairs={{0,2},{2,4},{4,6},{6,8},{8,10},{10,12},{12,14},{14,0},{1,3},{3,5},... | collective-permute-start | bytes 294920 | tf_op jit(solution)/shard_map/ppermute | solution.py:276
  51.3 7.2 %collective-permute-start.5 = (bf16[128,384]{1,0:T(8,128)(2,1)S(1)}, bf16[128,384]{1,0:T(8,128)(2,1)S(1)}, u32[]{:S(2)}, u32[]{:S(2)}) collective-permute-start(bf16[128,384]{1,0:T(8,128)(2,1)S(1)} %collective-permute-done.3.refs_4_), channel_id=1, source_target_pairs={{0,14},{2,0},{4,2},{6,4},{8,6},{10,8},{12,10},{14,12},{1,15},{3,1}... | collective-permute-start | bytes 294920 | tf_op jit(solution)/shard_map/ppermute | solution.py:278
  54.5 8.4 %collective-permute-start.6 = (bf16[128,384]{1,0:T(8,128)(2,1)S(1)}, bf16[128,384]{1,0:T(8,128)(2,1)S(1)}, u32[]{:S(2)}, u32[]{:S(2)}) collective-permute-start(bf16[128,384]{1,0:T(8,128)(2,1)S(1)} %collective-permute-done.2.refs_3_), channel_id=1, source_target_pairs={{0,4},{2,6},{4,8},{6,10},{8,12},{10,14},{12,0},{14,2},{1,5},{3,7},... | collective-permute-start | bytes 294920 | tf_op jit(solution)/shard_map/ppermute | solution.py:277
  55.3 7.6 %collective-permute-start.4 = (bf16[128,384]{1,0:T(8,128)(2,1)S(1)}, bf16[128,384]{1,0:T(8,128)(2,1)S(1)}, u32[]{:S(2)}, u32[]{:S(2)}) collective-permute-start(bf16[128,384]{1,0:T(8,128)(2,1)S(1)} %collective-permute-done.2.refs_3_), channel_id=1, source_target_pairs={{0,2},{2,4},{4,6},{6,8},{8,10},{10,12},{12,14},{14,0},{1,3},{3,5},... | collective-permute-start | bytes 294920 | tf_op jit(solution)/shard_map/ppermute | solution.py:278
  62.9 31.9 %copy-start = (bf16[2,1024,384]{2,1,0:T(8,128)(2,1)S(1)}, bf16[2,1024,384]{2,1,0:T(8,128)(2,1)}, u32[]{:S(2)}) copy-start(bf16[2,1024,384]{2,1,0:T(8,128)(2,1)} %get-tuple-element.24.eliminated_ref) | copy-start | bytes 4718596
  62.9 31.9 %copy-start.1 = (bf16[512,256]{1,0:T(8,128)(2,1)S(1)}, bf16[512,256]{1,0:T(8,128)(2,1)}, u32[]{:S(2)}) copy-start(bf16[512,256]{1,0:T(8,128)(2,1)} %get-tuple-element.21.pick_ref) | copy-start | bytes 786436

commit v7 on v6

--- a/solution.py
+++ b/solution.py
@@ -38,8 +38,8 @@
     couple_ref,
     eliminated_ref,
     packed_ref,
+    pick_ref,
     pack_ref,
-    pick_ref,
     total_ref,
 ):
     j, i = pl.program_id(0), pl.program_id(1)
@@ -97,16 +97,14 @@
         out_specs=[
             pl.BlockSpec((1, rows, 384), lambda j, i: (j, i, 0)),
             pl.BlockSpec((2, 1, 256, 384), lambda j, i: (0, j, 0, 0)),
-            pl.BlockSpec((256, 512), lambda j, i: (0, 0)),
             pl.BlockSpec((512, 256), lambda j, i: (0, 0)),
         ],
         out_shape=[
             jax.ShapeDtypeStruct((2, 1024, 384), BF),
             jax.ShapeDtypeStruct((2, 2, 256, 384), BF),
-            jax.ShapeDtypeStruct((256, 512), BF),
             jax.ShapeDtypeStruct((512, 256), BF),
         ],
-        scratch_shapes=[pltpu.VMEM((256, 384), F32)],
+        scratch_shapes=[pltpu.VMEM((256, 512), BF), pltpu.VMEM((256, 384), F32)],
         name="start",
     )(position, owner_sub, index_blocks, inverse, rhs, couple)
 
@@ -168,7 +166,10 @@
         total = weights_ref[0] * eliminated_ref[0, rows].astype(F32)
         total += weights_ref[1] * eliminated_ref[1, rows].astype(F32)
         total -= dot(spread0_ref[rows], picked_ref[0]) + dot(spread1_ref[rows], picked_ref[1])
-        out_ref[rows] = total.astype(BF)
+        total = total.astype(BF)
+        for b in range(CHUNK // 128):
+            yl, x = divmod(i * CHUNK // 128 + b, 4)
+            out_ref[pl.ds((2 * x + yl) * 128, 128)] = total[128 * b : 128 * b + 128]
 
 
 def finish(weights, back, pick, spread0, spread1, eliminated):
@@ -218,7 +219,7 @@
         return lax.broadcasted_iota(jnp.int32, shape, len(shape) - 1) < HALF
 
     position = ((y * 8 + z) * 2 + c).astype(jnp.int32)
-    eliminated, packed, _, pick = start(
+    eliminated, packed, pick = start(
         position[None], owner_sub, index_blocks, interior_inverse, interior_rhs, coupling
     )
     packed, schur_inverse = lax.optimization_barrier((packed, schur_inverse))
@@ -284,7 +285,7 @@
     ).reshape(32, 32, 384)
     back = lax.all_to_all(answers, EXCHANGE, 0, 0, tiled=True).reshape(4, 256, 384)
     total = finish(weights, back, pick, *spread, eliminated)
-    pieces = lax.all_to_all(total.reshape(8, 128, 384), SHIFT, 0, 0, tiled=True)
+    pieces = lax.all_to_all(total.reshape(8, 128, 384), ("x", "yl"), 0, 0, tiled=True)
     return add(pieces)
 
 

time: 116 us -> 116 us (level)
  no operation moved by 1% of the time
where the time goes in v7:
time: 116 us; the launch traced here: 115 us
  blocking collectives  48.5 us (42%)
  starting transfers between devices  24.2 us (21%)
  waiting for transfers between devices  19.9 us (17%)
  Pallas kernels  11.3 us (10%)
  matrix products  5.39 us (5%)
  other arithmetic  3.09 us (3%)
  local copies, waits for them, and re-layouts  2.79 us (2%)
    all_to_all x1, blocking collectives, on_device(): lax.all_to_all(answers, EXCHANGE, 0, 0, tiled=True).reshape(4, 256, 384)  30.6 us
    all_to_all x1, blocking collectives, on_device(): lax.all_to_all(total.reshape(8, 128, 384), ('x', 'yl'), 0, 0, tiled=True)  18 us
    all_to_all x1, waiting for transfers between devices, on_device(): lax.all_to_all(packed, EXCHANGE, 0, 0, tiled=True).reshape(1024, 384)  10.5 us
    all_to_all x1, starting transfers between devices, on_device(): lax.all_to_all(packed, EXCHANGE, 0, 0, tiled=True).reshape(1024, 384)  8.73 us
    pallas_call x1, Pallas kernels, start(): pl.pallas_call(start_kernel, grid=(2, steps), in_specs=[smem, smem, pl.Bl...  7.21 us
    dot_general x3, matrix products, dot(): return jnp.dot(a, b, preferred_element_type=F32)  4.93 us
    ppermute x1, waiting for transfers between devices, on_device(): opposite = lax.ppermute(below2, 'z', up2)  4.31 us
    ppermute x1, starting transfers between devices, on_device(): lax.ppermute(below2, 'z', up)  3.23 us
  transfers between devices with their start and end apart: 11, of which 4 were waited for; matrix products, arithmetic and copies ran while one was open for 9% of the time, Pallas kernels for 0%

profile of v7, /device:TPU:32, one launch (start us, length us, event | category | flops | bytes accessed | tf_op | source)
XLA Modules:
  0.0 115.4 jit_solution(9674297341306307398)
XLA Ops:
  0.0 7.2 %start.1 = (bf16[2,1024,384]{2,1,0:T(8,128)(2,1)}, bf16[2,2,256,384]{3,2,1,0:T(8,128)(2,1)}, bf16[512,256]{1,0:T(8,128)(2,1)}) custom-call(s32[1]{0:T(128)} %bitcast.3.position_ref, s32[32]{0:T(128)} %owner_ref.1, s32[32,256]{1,0:T(8,128)} %blocks_ref.1, bf16[2,1,1024,1024]{3,2,1,0:T(8,128)(2,1)} %inverse_ref.1, bf16[1,1024,384]{2,1,0:T(8,128)(2,1)} %rhs_ref.1, ...), custom_call_target="tpu_custom_call" | custom-call | tf_op jit(solution)/shard_map/start/pallas_call | solution.py:86
  7.2 0.0 copy-start.8
  7.2 0.0 copy-start.7
  7.2 0.0 copy-start.2
  7.3 0.8 dynamic-slice_bitcast_fusion
  8.0 2.7 %collective-permute-start.9 = (bf16[64,2048]{1,0:T(8,128)(2,1)}, bf16[64,2048]{1,0:T(8,128)(2,1)S(1)}, u32[]{:S(2)}, u32[]{:S(2)}) collective-permute-start(bf16[64,2048]{1,0:T(8,128)(2,1)} %get-tuple-element.29), channel_id=1, source_target_pairs={{0,17},{1,16},{16,1},{17,0},{2,19},{3,18},{18,3},{19,2},{4,21},{5,... | collective-permute-start | bytes 786440 | tf_op jit(solution)/shard_map/ppermute | solution.py:231
  10.7 0.7 collective-permute-start.7
  11.4 8.7 %all-to-all-start = ((bf16[32,32,384]{2,1,0:T(8,128)(2,1)}), bf16[32,32,384]{2,1,0:T(8,128)(2,1)S(1)}, u32[]{:S(2)}, u32[]{:S(2)}) async-start(bf16[32,32,384]{2,1,0:T(8,128)(2,1)} %bitcast.46), calls=%async_computation | async-start | bytes 1572864 | tf_op jit(solution)/shard_map/all_to_all | solution.py:227
  20.1 3.1 %collective-permute-start.8 = (bf16[64,2048]{1,0:T(8,128)(2,1)S(1)}, bf16[64,2048]{1,0:T(8,128)(2,1)S(1)}, u32[]{:S(2)}, u32[]{:S(2)}) collective-permute-start(bf16[64,2048]{1,0:T(8,128)(2,1)S(1)} %get-tuple-element.30.refs_8_), channel_id=1, source_target_pairs={{0,16},{16,0},{1,17},{17,1},{2,18},{18,2},{3,19},{19,3},{4,20},{20... | collective-permute-start | bytes 786440 | tf_op jit(solution)/shard_map/ppermute | solution.py:232
  23.2 0.1 reshape.108
  23.3 0.1 copy.11
  23.4 0.1 eq.49
  23.4 0.1 iota_compare_fusion.2
  23.5 0.3 select_reduce_fusion
  23.8 1.4 %compare_reduce_fusion = pred[32,256]{1,0:T(8,128)(4,1)S(1)} fusion(s32[256]{0:T(256)S(1)} %fusion.38, s32[32,256]{1,0:T(8,128)S(1)} %select_reduce_fusion), kind=kLoop, calls=%fused_computation | loop fusion | flops 4186112 | bytes 41984 | tf_op jit(solution)/shard_map/reduce_or | solution.py:240
  25.2 0.1 iota.92
  25.3 0.3 fusion.19
  25.6 0.2 fusion.20.refs_12_
  25.9 0.6 fusion.43
  26.4 1.1 fusion.42
  27.5 1.1 fusion.33
  28.6 0.0 copy-start.3
  28.6 0.0 copy-start.5
  28.6 3.4 %fusion.12.spread1_ref = bf16[1024,256]{1,0:T(8,128)(2,1)S(1)} fusion(bf16[2,1,1024,1024]{3,2,1,0:T(8,128)(2,1)} %inverse_ref.1, bf16[1,1024,256]{2,1,0:T(8,128)(2,1)S(1)} %copy-done.4, f32[]{:T(128)} %bitcast.11), kind=kOutput, calls=%fused_computation.9 | convolution fusion | flops 537395200 | bytes 3146240 | tf_op jit(solution)/shard_map/dot_general | solution.py:17
  32.0 1.3 %fusion.15.spread0_ref = bf16[1024,256]{1,0:T(8,128)(2,1)S(1)} fusion(bf16[2,1,1024,1024]{3,2,1,0:T(8,128)(2,1)S(1)} %copy-done.3, bf16[1,1024,256]{2,1,0:T(8,128)(2,1)S(1)} %copy-done.5, f32[]{:T(128)} %bitcast.8), kind=kOutput, calls=%fused_computation.10 | convolution fusion | flops 537395200 | bytes 3145732 | tf_op jit(solution)/shard_map/dot_general | solution.py:17
  33.3 10.5 %all-to-all-done = bf16[32,32,384]{2,1,0:T(8,128)(2,1)S(1)} async-done(((bf16[32,32,384]{2,1,0:T(8,128)(2,1)}), bf16[32,32,384]{2,1,0:T(8,128)(2,1)S(1)}, u32[]{:S(2)}, u32[]{:S(2)}) %all-to-all-start) | async-done | bytes 786464 | tf_op jit(solution)/shard_map/all_to_all | solution.py:227
  43.8 0.5 fusion.44
  44.3 0.8 collective-permute-start.3
  45.2 2.2 %collective-permute-start.2 = (bf16[128,384]{1,0:T(8,128)(2,1)S(1)}, bf16[128,384]{1,0:T(8,128)(2,1)S(1)}, u32[]{:S(2)}, u32[]{:S(2)}) collective-permute-start(bf16[128,384]{1,0:T(8,128)(2,1)S(1)} %fusion.26.refs_0_), channel_id=1, source_target_pairs={{0,4},{2,6},{4,8},{6,10},{8,12},{10,14},{12,0},{14,2},{1,5},{3,7},... | collective-permute-start | bytes 294920 | tf_op jit(solution)/shard_map/ppermute | solution.py:275
  47.3 0.0 collective-permute-done.9.refs_11_
  47.3 0.0 collective-permute-start.1
  47.3 0.0 collective-permute-done.7.refs_9_
  47.3 2.0 %collective-permute-start = (bf16[128,384]{1,0:T(8,128)(2,1)S(1)}, bf16[128,384]{1,0:T(8,128)(2,1)S(1)}, u32[]{:S(2)}, u32[]{:S(2)}) collective-permute-start(bf16[128,384]{1,0:T(8,128)(2,1)S(1)} %fusion.26.refs_0_), channel_id=1, source_target_pairs={{0,2},{2,4},{4,6},{6,8},{8,10},{10,12},{12,14},{14,0},{1,3},{3,5},... | collective-permute-start | bytes 294920 | tf_op jit(solution)/shard_map/ppermute | solution.py:277
  49.3 1.9 %collective-permute-done.3.refs_4_ = bf16[128,384]{1,0:T(8,128)(2,1)S(1)} collective-permute-done((bf16[128,384]{1,0:T(8,128)(2,1)S(1)}, bf16[128,384]{1,0:T(8,128)(2,1)S(1)}, u32[]{:S(2)}, u32[]{:S(2)}) %collective-permute-start.3) | collective-permute-done | bytes 98336 | tf_op jit(solution)/shard_map/ppermute | solution.py:276
  51.2 0.0 collective-permute-start.5
  51.2 3.2 %collective-permute-done.2.refs_3_ = bf16[128,384]{1,0:T(8,128)(2,1)S(1)} collective-permute-done((bf16[128,384]{1,0:T(8,128)(2,1)S(1)}, bf16[128,384]{1,0:T(8,128)(2,1)S(1)}, u32[]{:S(2)}, u32[]{:S(2)}) %collective-permute-start.2) | collective-permute-done | bytes 98336 | tf_op jit(solution)/shard_map/ppermute | solution.py:275
  54.4 0.8 collective-permute-start.6
  55.2 0.0 collective-permute-done.8.refs_10_
  55.2 3.2 %collective-permute-start.4 = (bf16[128,384]{1,0:T(8,128)(2,1)S(1)}, bf16[128,384]{1,0:T(8,128)(2,1)S(1)}, u32[]{:S(2)}, u32[]{:S(2)}) collective-permute-start(bf16[128,384]{1,0:T(8,128)(2,1)S(1)} %collective-permute-done.2.refs_3_), channel_id=1, source_target_pairs={{0,2},{2,4},{4,6},{6,8},{8,10},{10,12},{12,14},{14,0},{1,3},{3,5},... | collective-permute-start | bytes 294920 | tf_op jit(solution)/shard_map/ppermute | solution.py:279
  58.4 0.0 collective-permute-done.refs_1_
  58.4 0.0 collective-permute-done.5.refs_6_
  58.4 4.3 %collective-permute-done.6.refs_7_ = bf16[128,384]{1,0:T(8,128)(2,1)S(1)} collective-permute-done((bf16[128,384]{1,0:T(8,128)(2,1)S(1)}, bf16[128,384]{1,0:T(8,128)(2,1)S(1)}, u32[]{:S(2)}, u32[]{:S(2)}) %collective-permute-start.6) | collective-permute-done | bytes 98336 | tf_op jit(solution)/shard_map/ppermute | solution.py:278
  62.8 0.0 collective-permute-done.4.refs_5_
  62.8 1.3 %solve.1 = bf16[1024,384]{1,0:T(8,128)(2,1)S(1)} custom-call(s32[1]{0:T(128)} %bitcast.y_ref, s32[1]{0:T(128)} %bitcast.1.z_ref, s32[1]{0:T(128)} %bitcast.2.c_ref, bf16[128,384]{1,0:T(8,128)(2,1)S(1)} %fusion.26.refs_0_, bf16[128,384]{1,0:T(8,128)(2,1)S(1)} %collective-permute-done.refs_1_, bf16[128,384]{1,0:T(8,128)(2,1)S(1)} %collective-permute-done.1.refs_2_, ...), custom_call_target="tpu_custom_call" | custom-call | tf_op jit(solution)/shard_map/solve/pallas_call | solution.py:139
  64.1 30.6 %all_to_all.15 = bf16[32,32,384]{2,1,0:T(8,128)(2,1)S(1)} all-to-all(bf16[32,32,384]{2,1,0:T(8,128)(2,1)S(1)} %bitcast.44), channel_id=1, replica_groups=mesh['yl'=2,'x'=4,'yh'=2,'z'=8,'c'=2] {'yh','c','z'}, dimensions={0} | all-to-all | bytes 1572864 | tf_op jit(solution)/shard_map/all_to_all | solution.py:286
  94.7 2.0 %finish.1 = bf16[1024,384]{1,0:T(8,128)(2,1)S(1)} custom-call(f32[2]{0:T(128)S(1)} %copy-done.2, bf16[4,256,384]{2,1,0:T(8,128)(2,1)S(1)} %bitcast.42, bf16[512,256]{1,0:T(8,128)(2,1)S(1)} %copy-done.1, bf16[1024,256]{1,0:T(8,128)(2,1)S(1)} %fusion.15.spread0_ref, bf16[1024,256]{1,0:T(8,128)(2,1)S(1)} %fusion.12.spread1_ref, bf16[2,1024,384]{2,1,0:T(8,128)(2,1)S(1)} %copy-done), custom_call_target="tpu_custom_call" | custom-call | tf_op jit(solution)/shard_map/finish/pallas_call | solution.py:176
  96.7 18.0 %all_to_all.16.pieces_ref = bf16[8,128,384]{2,1,0:T(8,128)(2,1)S(1)} all-to-all(bf16[8,128,384]{2,1,0:T(8,128)(2,1)S(1)} %bitcast.43), channel_id=1, replica_groups=mesh['yl'=2,'x'=4,'yh'=2,'z'=8,'c'=2] {'x','yl'}, dimensions={0} | all-to-all | bytes 1572864 | tf_op jit(solution)/shard_map/all_to_all | solution.py:288
  114.6 0.8 add.108
  (20 shorter events, 0.1 us)
Async XLA Ops:
  0.0 7.3 %copy-start.6 = (bf16[2,64,2048]{2,1,0:T(8,128)(2,1)S(1)}, bf16[2,64,2048]{2,1,0:T(8,128)(2,1)}, u32[]{:S(2)}) copy-start(bf16[2,64,2048]{2,1,0:T(8,128)(2,1)} %param.12) | copy-start | bytes 1572868
  7.2 16.0 %copy-start.8 = (s32[32]{0:T(128)S(1)}, s32[32]{0:T(128)}, u32[]{:S(2)}) copy-start(s32[32]{0:T(128)} %owner_ref.1) | copy-start | bytes 388
  7.2 16.3 %copy-start.7 = (s32[32,256]{1,0:T(8,128)S(1)}, s32[32,256]{1,0:T(8,128)}, u32[]{:S(2)}) copy-start(s32[32,256]{1,0:T(8,128)} %blocks_ref.1) | copy-start | bytes 98308
  7.2 18.6 %copy-start.2 = (f32[2]{0:T(128)S(1)}, f32[2]{0:T(128)}, u32[]{:S(2)}) copy-start(f32[2]{0:T(128)} %weights_ref.1) | copy-start | bytes 28
  8.0 20.5 %copy-start.4 = (bf16[1,1024,256]{2,1,0:T(8,128)(2,1)S(1)}, bf16[1,1024,256]{2,1,0:T(8,128)(2,1)}, u32[]{:S(2)}) copy-start(bf16[1,1024,256]{2,1,0:T(8,128)(2,1)} %couple_ref.1) | copy-start | bytes 1572868
  8.0 39.3 %collective-permute-start.9 = (bf16[64,2048]{1,0:T(8,128)(2,1)}, bf16[64,2048]{1,0:T(8,128)(2,1)S(1)}, u32[]{:S(2)}, u32[]{:S(2)}) collective-permute-start(bf16[64,2048]{1,0:T(8,128)(2,1)} %get-tuple-element.29), channel_id=1, source_target_pairs={{0,17},{1,16},{16,1},{17,0},{2,19},{3,18},{18,3},{19,2},{4,21},{5,... | collective-permute-start | bytes 786440 | tf_op jit(solution)/shard_map/ppermute | solution.py:231
  10.7 36.6 %collective-permute-start.7 = (bf16[64,2048]{1,0:T(8,128)(2,1)}, bf16[64,2048]{1,0:T(8,128)(2,1)S(1)}, u32[]{:S(2)}, u32[]{:S(2)}) collective-permute-start(bf16[64,2048]{1,0:T(8,128)(2,1)} %get-tuple-element.29), channel_id=1, source_target_pairs={{0,1},{1,0},{2,3},{3,2},{4,5},{5,4},{6,7},{7,6},{8,9},{9,8},{10,11... | collective-permute-start | bytes 786440 | tf_op jit(solution)/shard_map/ppermute | solution.py:233
  11.4 32.4 %all-to-all-start = ((bf16[32,32,384]{2,1,0:T(8,128)(2,1)}), bf16[32,32,384]{2,1,0:T(8,128)(2,1)S(1)}, u32[]{:S(2)}, u32[]{:S(2)}) async-start(bf16[32,32,384]{2,1,0:T(8,128)(2,1)} %bitcast.46), calls=%async_computation | async-start | bytes 1572864 | tf_op jit(solution)/shard_map/all_to_all | solution.py:227
  20.1 35.1 %collective-permute-start.8 = (bf16[64,2048]{1,0:T(8,128)(2,1)S(1)}, bf16[64,2048]{1,0:T(8,128)(2,1)S(1)}, u32[]{:S(2)}, u32[]{:S(2)}) collective-permute-start(bf16[64,2048]{1,0:T(8,128)(2,1)S(1)} %get-tuple-element.30.refs_8_), channel_id=1, source_target_pairs={{0,16},{16,0},{1,17},{17,1},{2,18},{18,2},{3,19},{19,3},{4,20},{20... | collective-permute-start | bytes 786440 | tf_op jit(solution)/shard_map/ppermute | solution.py:232
  28.6 3.4 %copy-start.3 = (bf16[2,1,1024,1024]{3,2,1,0:T(8,128)(2,1)S(1)}, bf16[2,1,1024,1024]{3,2,1,0:T(8,128)(2,1)}, u32[]{:S(2)}) copy-start(bf16[2,1,1024,1024]{3,2,1,0:T(8,128)(2,1)} %inverse_ref.1) | copy-start | bytes 12582916
  28.6 3.4 %copy-start.5 = (bf16[1,1024,256]{2,1,0:T(8,128)(2,1)S(1)}, bf16[1,1024,256]{2,1,0:T(8,128)(2,1)}, u32[]{:S(2)}) copy-start(bf16[1,1024,256]{2,1,0:T(8,128)(2,1)} %couple_ref.1) | copy-start | bytes 1572868
  44.3 6.9 %collective-permute-start.3 = (bf16[128,384]{1,0:T(8,128)(2,1)S(1)}, bf16[128,384]{1,0:T(8,128)(2,1)S(1)}, u32[]{:S(2)}, u32[]{:S(2)}) collective-permute-start(bf16[128,384]{1,0:T(8,128)(2,1)S(1)} %fusion.26.refs_0_), channel_id=1, source_target_pairs={{0,12},{2,14},{4,0},{6,2},{8,4},{10,6},{12,8},{14,10},{1,13},{3,15... | collective-permute-start | bytes 294920 | tf_op jit(solution)/shard_map/ppermute | solution.py:276
  45.2 9.2 %collective-permute-start.2 = (bf16[128,384]{1,0:T(8,128)(2,1)S(1)}, bf16[128,384]{1,0:T(8,128)(2,1)S(1)}, u32[]{:S(2)}, u32[]{:S(2)}) collective-permute-start(bf16[128,384]{1,0:T(8,128)(2,1)S(1)} %fusion.26.refs_0_), channel_id=1, source_target_pairs={{0,4},{2,6},{4,8},{6,10},{8,12},{10,14},{12,0},{14,2},{1,5},{3,7},... | collective-permute-start | bytes 294920 | tf_op jit(solution)/shard_map/ppermute | solution.py:275
  47.3 11.1 %collective-permute-start.1 = (bf16[128,384]{1,0:T(8,128)(2,1)S(1)}, bf16[128,384]{1,0:T(8,128)(2,1)S(1)}, u32[]{:S(2)}, u32[]{:S(2)}) collective-permute-start(bf16[128,384]{1,0:T(8,128)(2,1)S(1)} %fusion.26.refs_0_), channel_id=1, source_target_pairs={{0,14},{2,0},{4,2},{6,4},{8,6},{10,8},{12,10},{14,12},{1,15},{3,1}... | collective-permute-start | bytes 294920 | tf_op jit(solution)/shard_map/ppermute | solution.py:277
  47.3 11.1 %collective-permute-start = (bf16[128,384]{1,0:T(8,128)(2,1)S(1)}, bf16[128,384]{1,0:T(8,128)(2,1)S(1)}, u32[]{:S(2)}, u32[]{:S(2)}) collective-permute-start(bf16[128,384]{1,0:T(8,128)(2,1)S(1)} %fusion.26.refs_0_), channel_id=1, source_target_pairs={{0,2},{2,4},{4,6},{6,8},{8,10},{10,12},{12,14},{14,0},{1,3},{3,5},... | collective-permute-start | bytes 294920 | tf_op jit(solution)/shard_map/ppermute | solution.py:277
  51.2 7.2 %collective-permute-start.5 = (bf16[128,384]{1,0:T(8,128)(2,1)S(1)}, bf16[128,384]{1,0:T(8,128)(2,1)S(1)}, u32[]{:S(2)}, u32[]{:S(2)}) collective-permute-start(bf16[128,384]{1,0:T(8,128)(2,1)S(1)} %collective-permute-done.3.refs_4_), channel_id=1, source_target_pairs={{0,14},{2,0},{4,2},{6,4},{8,6},{10,8},{12,10},{14,12},{1,15},{3,1}... | collective-permute-start | bytes 294920 | tf_op jit(solution)/shard_map/ppermute | solution.py:279
  54.4 8.4 %collective-permute-start.6 = (bf16[128,384]{1,0:T(8,128)(2,1)S(1)}, bf16[128,384]{1,0:T(8,128)(2,1)S(1)}, u32[]{:S(2)}, u32[]{:S(2)}) collective-permute-start(bf16[128,384]{1,0:T(8,128)(2,1)S(1)} %collective-permute-done.2.refs_3_), channel_id=1, source_target_pairs={{0,4},{2,6},{4,8},{6,10},{8,12},{10,14},{12,0},{14,2},{1,5},{3,7},... | collective-permute-start | bytes 294920 | tf_op jit(solution)/shard_map/ppermute | solution.py:278
  55.2 7.6 %collective-permute-start.4 = (bf16[128,384]{1,0:T(8,128)(2,1)S(1)}, bf16[128,384]{1,0:T(8,128)(2,1)S(1)}, u32[]{:S(2)}, u32[]{:S(2)}) collective-permute-start(bf16[128,384]{1,0:T(8,128)(2,1)S(1)} %collective-permute-done.2.refs_3_), channel_id=1, source_target_pairs={{0,2},{2,4},{4,6},{6,8},{8,10},{10,12},{12,14},{14,0},{1,3},{3,5},... | collective-permute-start | bytes 294920 | tf_op jit(solution)/shard_map/ppermute | solution.py:279
  62.8 31.9 %copy-start = (bf16[2,1024,384]{2,1,0:T(8,128)(2,1)S(1)}, bf16[2,1024,384]{2,1,0:T(8,128)(2,1)}, u32[]{:S(2)}) copy-start(bf16[2,1024,384]{2,1,0:T(8,128)(2,1)} %get-tuple-element.24.eliminated_ref) | copy-start | bytes 4718596
  62.8 31.9 %copy-start.1 = (bf16[512,256]{1,0:T(8,128)(2,1)S(1)}, bf16[512,256]{1,0:T(8,128)(2,1)}, u32[]{:S(2)}) copy-start(bf16[512,256]{1,0:T(8,128)(2,1)} %get-tuple-element.21.pick_ref) | copy-start | bytes 786436

commit v8 on v7

--- a/solution.py
+++ b/solution.py
@@ -35,14 +35,21 @@
     blocks_ref,
     inverse_ref,
     rhs_ref,
-    couple_ref,
+    couple_hbm,
     eliminated_ref,
     packed_ref,
     pick_ref,
     pack_ref,
     total_ref,
+    couple_ref,
+    sem,
 ):
     j, i = pl.program_id(0), pl.program_id(1)
+    fetch = pltpu.make_async_copy(couple_hbm, couple_ref, sem)
+
+    @pl.when((j == 0) & (i == 0))
+    def _():
+        fetch.start()
 
     @pl.when((j == 0) & (i == 0))
     def _():
@@ -67,7 +74,12 @@
 
     part = dot(inverse_ref[0, 0], rhs_ref[0]).astype(BF)
     eliminated_ref[0] = part
-    total_ref[...] += dot_t(couple_ref[0], part)
+
+    @pl.when((j == 0) & (i == 0))
+    def _():
+        fetch.wait()
+
+    total_ref[...] += dot_t(couple_ref[0, pl.ds(i * part.shape[0], part.shape[0])], part)
 
     @pl.when(i == pl.num_programs(1) - 1)
     def _():
@@ -92,7 +104,7 @@
             pl.BlockSpec((32, 256), lambda j, i: (0, 0)),
             pl.BlockSpec((1, 1, rows, 1024), lambda j, i: (j, 0, i, 0)),
             pl.BlockSpec((1, 1024, 384), lambda j, i: (0, 0, 0)),
-            pl.BlockSpec((1, rows, 256), lambda j, i: (0, i, 0)),
+            pl.BlockSpec(memory_space=pl.ANY),
         ],
         out_specs=[
             pl.BlockSpec((1, rows, 384), lambda j, i: (j, i, 0)),
@@ -104,7 +116,12 @@
             jax.ShapeDtypeStruct((2, 2, 256, 384), BF),
             jax.ShapeDtypeStruct((512, 256), BF),
         ],
-        scratch_shapes=[pltpu.VMEM((256, 512), BF), pltpu.VMEM((256, 384), F32)],
+        scratch_shapes=[
+            pltpu.VMEM((256, 512), BF),
+            pltpu.VMEM((256, 384), F32),
+            pltpu.VMEM((1, 1024, 256), BF),
+            pltpu.SemaphoreType.DMA,
+        ],
         name="start",
     )(position, owner_sub, index_blocks, inverse, rhs, couple)
 

time: 116 us -> 116 us (level)
  no operation moved by 1% of the time
where the time goes in v8:
time: 116 us
  blocking collectives  48.5 us (42%)
  starting transfers between devices  24.2 us (21%)
  waiting for transfers between devices  19.9 us (17%)
  Pallas kernels  11.6 us (10%)
  matrix products  5.39 us (5%)
  other arithmetic  3.09 us (3%)
  local copies, waits for them, and re-layouts  2.79 us (2%)
    all_to_all x1, blocking collectives, on_device(): lax.all_to_all(answers, EXCHANGE, 0, 0, tiled=True).reshape(4, 256, 384)  30.6 us
    all_to_all x1, blocking collectives, on_device(): lax.all_to_all(total.reshape(8, 128, 384), ('x', 'yl'), 0, 0, tiled=True)  18 us
    all_to_all x1, waiting for transfers between devices, on_device(): lax.all_to_all(packed, EXCHANGE, 0, 0, tiled=True).reshape(1024, 384)  10.5 us
    all_to_all x1, starting transfers between devices, on_device(): lax.all_to_all(packed, EXCHANGE, 0, 0, tiled=True).reshape(1024, 384)  8.73 us
    pallas_call x1, Pallas kernels, start(): pl.pallas_call(start_kernel, grid=(2, steps), in_specs=[smem, smem, pl.Bl...  7.46 us
    dot_general x3, matrix products, dot(): return jnp.dot(a, b, preferred_element_type=F32)  4.93 us
    ppermute x1, waiting for transfers between devices, on_device(): opposite = lax.ppermute(below2, 'z', up2)  4.31 us
    ppermute x1, starting transfers between devices, on_device(): lax.ppermute(below2, 'z', up)  3.23 us
  transfers between devices with their start and end apart: 11, of which 4 were waited for; matrix products, arithmetic and copies ran while one was open for 9% of the time, Pallas kernels for 0%

profile of v8, /device:TPU:32, one launch (start us, length us, event | category | flops | bytes accessed | tf_op | source)
XLA Modules:
  0.0 115.7 jit_solution(8226530828361406071)
XLA Ops:
  0.0 7.5 %start.1 = (bf16[2,1024,384]{2,1,0:T(8,128)(2,1)}, bf16[2,2,256,384]{3,2,1,0:T(8,128)(2,1)}, bf16[512,256]{1,0:T(8,128)(2,1)}) custom-call(s32[1]{0:T(128)} %bitcast.3.position_ref, s32[32]{0:T(128)} %owner_ref.1, s32[32,256]{1,0:T(8,128)} %blocks_ref.1, bf16[2,1,1024,1024]{3,2,1,0:T(8,128)(2,1)} %inverse_ref.1, bf16[1,1024,384]{2,1,0:T(8,128)(2,1)} %rhs_ref.1, ...), custom_call_target="tpu_custom_call" | custom-call | tf_op jit(solution)/shard_map/start/pallas_call | solution.py:98
  7.5 0.0 copy-start.8
  7.5 0.0 copy-start.7
  7.5 0.0 copy-start.2
  7.5 0.8 dynamic-slice_bitcast_fusion
  8.3 2.6 %collective-permute-start.9 = (bf16[64,2048]{1,0:T(8,128)(2,1)}, bf16[64,2048]{1,0:T(8,128)(2,1)S(1)}, u32[]{:S(2)}, u32[]{:S(2)}) collective-permute-start(bf16[64,2048]{1,0:T(8,128)(2,1)} %get-tuple-element.29), channel_id=1, source_target_pairs={{0,17},{1,16},{16,1},{17,0},{2,19},{3,18},{18,3},{19,2},{4,21},{5,... | collective-permute-start | bytes 786440 | tf_op jit(solution)/shard_map/ppermute | solution.py:248
  10.9 0.7 collective-permute-start.7
  11.6 8.7 %all-to-all-start = ((bf16[32,32,384]{2,1,0:T(8,128)(2,1)}), bf16[32,32,384]{2,1,0:T(8,128)(2,1)S(1)}, u32[]{:S(2)}, u32[]{:S(2)}) async-start(bf16[32,32,384]{2,1,0:T(8,128)(2,1)} %bitcast.46), calls=%async_computation | async-start | bytes 1572864 | tf_op jit(solution)/shard_map/all_to_all | solution.py:244
  20.3 3.1 %collective-permute-start.8 = (bf16[64,2048]{1,0:T(8,128)(2,1)S(1)}, bf16[64,2048]{1,0:T(8,128)(2,1)S(1)}, u32[]{:S(2)}, u32[]{:S(2)}) collective-permute-start(bf16[64,2048]{1,0:T(8,128)(2,1)S(1)} %get-tuple-element.30.refs_8_), channel_id=1, source_target_pairs={{0,16},{16,0},{1,17},{17,1},{2,18},{18,2},{3,19},{19,3},{4,20},{20... | collective-permute-start | bytes 786440 | tf_op jit(solution)/shard_map/ppermute | solution.py:249
  23.4 0.1 reshape.108
  23.5 0.1 copy.11
  23.6 0.1 eq.49
  23.7 0.1 iota_compare_fusion.2
  23.8 0.3 select_reduce_fusion
  24.0 1.4 %compare_reduce_fusion = pred[32,256]{1,0:T(8,128)(4,1)S(1)} fusion(s32[256]{0:T(256)S(1)} %fusion.38, s32[32,256]{1,0:T(8,128)S(1)} %select_reduce_fusion), kind=kLoop, calls=%fused_computation | loop fusion | flops 4186112 | bytes 41984 | tf_op jit(solution)/shard_map/reduce_or | solution.py:257
  25.5 0.1 iota.92
  25.6 0.3 fusion.19
  25.9 0.2 fusion.20.refs_12_
  26.1 0.6 fusion.43
  26.7 1.1 fusion.42
  27.7 1.1 fusion.33
  28.8 0.0 copy-start.3
  28.8 0.0 copy-start.5
  28.8 3.4 %fusion.12.spread1_ref = bf16[1024,256]{1,0:T(8,128)(2,1)S(1)} fusion(bf16[2,1,1024,1024]{3,2,1,0:T(8,128)(2,1)} %inverse_ref.1, bf16[1,1024,256]{2,1,0:T(8,128)(2,1)S(1)} %copy-done.4, f32[]{:T(128)} %bitcast.11), kind=kOutput, calls=%fused_computation.9 | convolution fusion | flops 537395200 | bytes 3146240 | tf_op jit(solution)/shard_map/dot_general | solution.py:17
  32.2 1.3 %fusion.15.spread0_ref = bf16[1024,256]{1,0:T(8,128)(2,1)S(1)} fusion(bf16[2,1,1024,1024]{3,2,1,0:T(8,128)(2,1)S(1)} %copy-done.3, bf16[1,1024,256]{2,1,0:T(8,128)(2,1)S(1)} %copy-done.5, f32[]{:T(128)} %bitcast.8), kind=kOutput, calls=%fused_computation.10 | convolution fusion | flops 537395200 | bytes 3145732 | tf_op jit(solution)/shard_map/dot_general | solution.py:17
  33.5 10.5 %all-to-all-done = bf16[32,32,384]{2,1,0:T(8,128)(2,1)S(1)} async-done(((bf16[32,32,384]{2,1,0:T(8,128)(2,1)}), bf16[32,32,384]{2,1,0:T(8,128)(2,1)S(1)}, u32[]{:S(2)}, u32[]{:S(2)}) %all-to-all-start) | async-done | bytes 786464 | tf_op jit(solution)/shard_map/all_to_all | solution.py:244
  44.0 0.5 fusion.44
  44.5 0.8 collective-permute-start.3
  45.4 2.2 %collective-permute-start.2 = (bf16[128,384]{1,0:T(8,128)(2,1)S(1)}, bf16[128,384]{1,0:T(8,128)(2,1)S(1)}, u32[]{:S(2)}, u32[]{:S(2)}) collective-permute-start(bf16[128,384]{1,0:T(8,128)(2,1)S(1)} %fusion.26.refs_0_), channel_id=1, source_target_pairs={{0,4},{2,6},{4,8},{6,10},{8,12},{10,14},{12,0},{14,2},{1,5},{3,7},... | collective-permute-start | bytes 294920 | tf_op jit(solution)/shard_map/ppermute | solution.py:292
  47.5 0.0 collective-permute-done.9.refs_11_
  47.6 0.0 collective-permute-start.1
  47.6 0.0 collective-permute-done.7.refs_9_
  47.6 2.0 %collective-permute-start = (bf16[128,384]{1,0:T(8,128)(2,1)S(1)}, bf16[128,384]{1,0:T(8,128)(2,1)S(1)}, u32[]{:S(2)}, u32[]{:S(2)}) collective-permute-start(bf16[128,384]{1,0:T(8,128)(2,1)S(1)} %fusion.26.refs_0_), channel_id=1, source_target_pairs={{0,2},{2,4},{4,6},{6,8},{8,10},{10,12},{12,14},{14,0},{1,3},{3,5},... | collective-permute-start | bytes 294920 | tf_op jit(solution)/shard_map/ppermute | solution.py:294
  49.6 1.9 %collective-permute-done.3.refs_4_ = bf16[128,384]{1,0:T(8,128)(2,1)S(1)} collective-permute-done((bf16[128,384]{1,0:T(8,128)(2,1)S(1)}, bf16[128,384]{1,0:T(8,128)(2,1)S(1)}, u32[]{:S(2)}, u32[]{:S(2)}) %collective-permute-start.3) | collective-permute-done | bytes 98336 | tf_op jit(solution)/shard_map/ppermute | solution.py:293
  51.5 0.0 collective-permute-start.5
  51.5 3.2 %collective-permute-done.2.refs_3_ = bf16[128,384]{1,0:T(8,128)(2,1)S(1)} collective-permute-done((bf16[128,384]{1,0:T(8,128)(2,1)S(1)}, bf16[128,384]{1,0:T(8,128)(2,1)S(1)}, u32[]{:S(2)}, u32[]{:S(2)}) %collective-permute-start.2) | collective-permute-done | bytes 98336 | tf_op jit(solution)/shard_map/ppermute | solution.py:292
  54.6 0.8 collective-permute-start.6
  55.4 0.0 collective-permute-done.8.refs_10_
  55.4 3.2 %collective-permute-start.4 = (bf16[128,384]{1,0:T(8,128)(2,1)S(1)}, bf16[128,384]{1,0:T(8,128)(2,1)S(1)}, u32[]{:S(2)}, u32[]{:S(2)}) collective-permute-start(bf16[128,384]{1,0:T(8,128)(2,1)S(1)} %collective-permute-done.2.refs_3_), channel_id=1, source_target_pairs={{0,2},{2,4},{4,6},{6,8},{8,10},{10,12},{12,14},{14,0},{1,3},{3,5},... | collective-permute-start | bytes 294920 | tf_op jit(solution)/shard_map/ppermute | solution.py:296
  58.7 0.0 collective-permute-done.1.refs_2_
  58.7 0.0 collective-permute-done.refs_1_
  58.7 4.3 %collective-permute-done.6.refs_7_ = bf16[128,384]{1,0:T(8,128)(2,1)S(1)} collective-permute-done((bf16[128,384]{1,0:T(8,128)(2,1)S(1)}, bf16[128,384]{1,0:T(8,128)(2,1)S(1)}, u32[]{:S(2)}, u32[]{:S(2)}) %collective-permute-start.6) | collective-permute-done | bytes 98336 | tf_op jit(solution)/shard_map/ppermute | solution.py:295
  63.0 0.0 collective-permute-done.4.refs_5_
  63.0 1.3 %solve.1 = bf16[1024,384]{1,0:T(8,128)(2,1)S(1)} custom-call(s32[1]{0:T(128)} %bitcast.y_ref, s32[1]{0:T(128)} %bitcast.1.z_ref, s32[1]{0:T(128)} %bitcast.2.c_ref, bf16[128,384]{1,0:T(8,128)(2,1)S(1)} %fusion.26.refs_0_, bf16[128,384]{1,0:T(8,128)(2,1)S(1)} %collective-permute-done.refs_1_, bf16[128,384]{1,0:T(8,128)(2,1)S(1)} %collective-permute-done.1.refs_2_, ...), custom_call_target="tpu_custom_call" | custom-call | tf_op jit(solution)/shard_map/solve/pallas_call | solution.py:156
  64.3 30.6 %all_to_all.15 = bf16[32,32,384]{2,1,0:T(8,128)(2,1)S(1)} all-to-all(bf16[32,32,384]{2,1,0:T(8,128)(2,1)S(1)} %bitcast.44), channel_id=1, replica_groups=mesh['yl'=2,'x'=4,'yh'=2,'z'=8,'c'=2] {'yh','c','z'}, dimensions={0} | all-to-all | bytes 1572864 | tf_op jit(solution)/shard_map/all_to_all | solution.py:303
  94.9 2.0 %finish.1 = bf16[1024,384]{1,0:T(8,128)(2,1)S(1)} custom-call(f32[2]{0:T(128)S(1)} %copy-done.2, bf16[4,256,384]{2,1,0:T(8,128)(2,1)S(1)} %bitcast.42, bf16[512,256]{1,0:T(8,128)(2,1)S(1)} %copy-done.1, bf16[1024,256]{1,0:T(8,128)(2,1)S(1)} %fusion.15.spread0_ref, bf16[1024,256]{1,0:T(8,128)(2,1)S(1)} %fusion.12.spread1_ref, bf16[2,1024,384]{2,1,0:T(8,128)(2,1)S(1)} %copy-done), custom_call_target="tpu_custom_call" | custom-call | tf_op jit(solution)/shard_map/finish/pallas_call | solution.py:193
  96.9 18.0 %all_to_all.16.pieces_ref = bf16[8,128,384]{2,1,0:T(8,128)(2,1)S(1)} all-to-all(bf16[8,128,384]{2,1,0:T(8,128)(2,1)S(1)} %bitcast.43), channel_id=1, replica_groups=mesh['yl'=2,'x'=4,'yh'=2,'z'=8,'c'=2] {'x','yl'}, dimensions={0} | all-to-all | bytes 1572864 | tf_op jit(solution)/shard_map/all_to_all | solution.py:305
  114.9 0.8 add.108
  (20 shorter events, 0.1 us)
Async XLA Ops:
  0.0 7.5 %copy-start.6 = (bf16[2,64,2048]{2,1,0:T(8,128)(2,1)S(1)}, bf16[2,64,2048]{2,1,0:T(8,128)(2,1)}, u32[]{:S(2)}) copy-start(bf16[2,64,2048]{2,1,0:T(8,128)(2,1)} %param.12) | copy-start | bytes 1572868
  7.5 15.9 %copy-start.8 = (s32[32]{0:T(128)S(1)}, s32[32]{0:T(128)}, u32[]{:S(2)}) copy-start(s32[32]{0:T(128)} %owner_ref.1) | copy-start | bytes 388
  7.5 16.3 %copy-start.7 = (s32[32,256]{1,0:T(8,128)S(1)}, s32[32,256]{1,0:T(8,128)}, u32[]{:S(2)}) copy-start(s32[32,256]{1,0:T(8,128)} %blocks_ref.1) | copy-start | bytes 98308
  7.5 18.6 %copy-start.2 = (f32[2]{0:T(128)S(1)}, f32[2]{0:T(128)}, u32[]{:S(2)}) copy-start(f32[2]{0:T(128)} %weights_ref.1) | copy-start | bytes 28
  8.3 20.5 %copy-start.4 = (bf16[1,1024,256]{2,1,0:T(8,128)(2,1)S(1)}, bf16[1,1024,256]{2,1,0:T(8,128)(2,1)}, u32[]{:S(2)}) copy-start(bf16[1,1024,256]{2,1,0:T(8,128)(2,1)} %couple_hbm.1) | copy-start | bytes 1572868
  8.3 39.2 %collective-permute-start.9 = (bf16[64,2048]{1,0:T(8,128)(2,1)}, bf16[64,2048]{1,0:T(8,128)(2,1)S(1)}, u32[]{:S(2)}, u32[]{:S(2)}) collective-permute-start(bf16[64,2048]{1,0:T(8,128)(2,1)} %get-tuple-element.29), channel_id=1, source_target_pairs={{0,17},{1,16},{16,1},{17,0},{2,19},{3,18},{18,3},{19,2},{4,21},{5,... | collective-permute-start | bytes 786440 | tf_op jit(solution)/shard_map/ppermute | solution.py:248
  10.9 36.6 %collective-permute-start.7 = (bf16[64,2048]{1,0:T(8,128)(2,1)}, bf16[64,2048]{1,0:T(8,128)(2,1)S(1)}, u32[]{:S(2)}, u32[]{:S(2)}) collective-permute-start(bf16[64,2048]{1,0:T(8,128)(2,1)} %get-tuple-element.29), channel_id=1, source_target_pairs={{0,1},{1,0},{2,3},{3,2},{4,5},{5,4},{6,7},{7,6},{8,9},{9,8},{10,11... | collective-permute-start | bytes 786440 | tf_op jit(solution)/shard_map/ppermute | solution.py:250
  11.6 32.4 %all-to-all-start = ((bf16[32,32,384]{2,1,0:T(8,128)(2,1)}), bf16[32,32,384]{2,1,0:T(8,128)(2,1)S(1)}, u32[]{:S(2)}, u32[]{:S(2)}) async-start(bf16[32,32,384]{2,1,0:T(8,128)(2,1)} %bitcast.46), calls=%async_computation | async-start | bytes 1572864 | tf_op jit(solution)/shard_map/all_to_all | solution.py:244
  20.3 35.1 %collective-permute-start.8 = (bf16[64,2048]{1,0:T(8,128)(2,1)S(1)}, bf16[64,2048]{1,0:T(8,128)(2,1)S(1)}, u32[]{:S(2)}, u32[]{:S(2)}) collective-permute-start(bf16[64,2048]{1,0:T(8,128)(2,1)S(1)} %get-tuple-element.30.refs_8_), channel_id=1, source_target_pairs={{0,16},{16,0},{1,17},{17,1},{2,18},{18,2},{3,19},{19,3},{4,20},{20... | collective-permute-start | bytes 786440 | tf_op jit(solution)/shard_map/ppermute | solution.py:249
  28.8 3.4 %copy-start.3 = (bf16[2,1,1024,1024]{3,2,1,0:T(8,128)(2,1)S(1)}, bf16[2,1,1024,1024]{3,2,1,0:T(8,128)(2,1)}, u32[]{:S(2)}) copy-start(bf16[2,1,1024,1024]{3,2,1,0:T(8,128)(2,1)} %inverse_ref.1) | copy-start | bytes 12582916
  28.8 3.4 %copy-start.5 = (bf16[1,1024,256]{2,1,0:T(8,128)(2,1)S(1)}, bf16[1,1024,256]{2,1,0:T(8,128)(2,1)}, u32[]{:S(2)}) copy-start(bf16[1,1024,256]{2,1,0:T(8,128)(2,1)} %couple_hbm.1) | copy-start | bytes 1572868
  44.5 6.9 %collective-permute-start.3 = (bf16[128,384]{1,0:T(8,128)(2,1)S(1)}, bf16[128,384]{1,0:T(8,128)(2,1)S(1)}, u32[]{:S(2)}, u32[]{:S(2)}) collective-permute-start(bf16[128,384]{1,0:T(8,128)(2,1)S(1)} %fusion.26.refs_0_), channel_id=1, source_target_pairs={{0,12},{2,14},{4,0},{6,2},{8,4},{10,6},{12,8},{14,10},{1,13},{3,15... | collective-permute-start | bytes 294920 | tf_op jit(solution)/shard_map/ppermute | solution.py:293
  45.4 9.2 %collective-permute-start.2 = (bf16[128,384]{1,0:T(8,128)(2,1)S(1)}, bf16[128,384]{1,0:T(8,128)(2,1)S(1)}, u32[]{:S(2)}, u32[]{:S(2)}) collective-permute-start(bf16[128,384]{1,0:T(8,128)(2,1)S(1)} %fusion.26.refs_0_), channel_id=1, source_target_pairs={{0,4},{2,6},{4,8},{6,10},{8,12},{10,14},{12,0},{14,2},{1,5},{3,7},... | collective-permute-start | bytes 294920 | tf_op jit(solution)/shard_map/ppermute | solution.py:292
  47.6 11.1 %collective-permute-start.1 = (bf16[128,384]{1,0:T(8,128)(2,1)S(1)}, bf16[128,384]{1,0:T(8,128)(2,1)S(1)}, u32[]{:S(2)}, u32[]{:S(2)}) collective-permute-start(bf16[128,384]{1,0:T(8,128)(2,1)S(1)} %fusion.26.refs_0_), channel_id=1, source_target_pairs={{0,14},{2,0},{4,2},{6,4},{8,6},{10,8},{12,10},{14,12},{1,15},{3,1}... | collective-permute-start | bytes 294920 | tf_op jit(solution)/shard_map/ppermute | solution.py:294
  47.6 11.1 %collective-permute-start = (bf16[128,384]{1,0:T(8,128)(2,1)S(1)}, bf16[128,384]{1,0:T(8,128)(2,1)S(1)}, u32[]{:S(2)}, u32[]{:S(2)}) collective-permute-start(bf16[128,384]{1,0:T(8,128)(2,1)S(1)} %fusion.26.refs_0_), channel_id=1, source_target_pairs={{0,2},{2,4},{4,6},{6,8},{8,10},{10,12},{12,14},{14,0},{1,3},{3,5},... | collective-permute-start | bytes 294920 | tf_op jit(solution)/shard_map/ppermute | solution.py:294
  51.5 7.2 %collective-permute-start.5 = (bf16[128,384]{1,0:T(8,128)(2,1)S(1)}, bf16[128,384]{1,0:T(8,128)(2,1)S(1)}, u32[]{:S(2)}, u32[]{:S(2)}) collective-permute-start(bf16[128,384]{1,0:T(8,128)(2,1)S(1)} %collective-permute-done.3.refs_4_), channel_id=1, source_target_pairs={{0,14},{2,0},{4,2},{6,4},{8,6},{10,8},{12,10},{14,12},{1,15},{3,1}... | collective-permute-start | bytes 294920 | tf_op jit(solution)/shard_map/ppermute | solution.py:296
  54.6 8.4 %collective-permute-start.6 = (bf16[128,384]{1,0:T(8,128)(2,1)S(1)}, bf16[128,384]{1,0:T(8,128)(2,1)S(1)}, u32[]{:S(2)}, u32[]{:S(2)}) collective-permute-start(bf16[128,384]{1,0:T(8,128)(2,1)S(1)} %collective-permute-done.2.refs_3_), channel_id=1, source_target_pairs={{0,4},{2,6},{4,8},{6,10},{8,12},{10,14},{12,0},{14,2},{1,5},{3,7},... | collective-permute-start | bytes 294920 | tf_op jit(solution)/shard_map/ppermute | solution.py:295
  55.4 7.6 %collective-permute-start.4 = (bf16[128,384]{1,0:T(8,128)(2,1)S(1)}, bf16[128,384]{1,0:T(8,128)(2,1)S(1)}, u32[]{:S(2)}, u32[]{:S(2)}) collective-permute-start(bf16[128,384]{1,0:T(8,128)(2,1)S(1)} %collective-permute-done.2.refs_3_), channel_id=1, source_target_pairs={{0,2},{2,4},{4,6},{6,8},{8,10},{10,12},{12,14},{14,0},{1,3},{3,5},... | collective-permute-start | bytes 294920 | tf_op jit(solution)/shard_map/ppermute | solution.py:296
  63.0 31.9 %copy-start = (bf16[2,1024,384]{2,1,0:T(8,128)(2,1)S(1)}, bf16[2,1024,384]{2,1,0:T(8,128)(2,1)}, u32[]{:S(2)}) copy-start(bf16[2,1024,384]{2,1,0:T(8,128)(2,1)} %get-tuple-element.24.eliminated_ref) | copy-start | bytes 4718596
  63.0 31.9 %copy-start.1 = (bf16[512,256]{1,0:T(8,128)(2,1)S(1)}, bf16[512,256]{1,0:T(8,128)(2,1)}, u32[]{:S(2)}) copy-start(bf16[512,256]{1,0:T(8,128)(2,1)} %get-tuple-element.21.pick_ref) | copy-start | bytes 786436
